TPU v7x, 256 devices: a whole 4x4x8 slice. The times are simulated.
256 devices in a mesh: coil: 8 (over z_hi, y), space: 32 (over x, z_lo, core).
Axes of the slice: x: 4, y: 4, z: 8 (z_hi: 2, z_lo: 4; z = z_hi * 4 + z_lo), core: 2. Of those that a mesh axis runs over, the one named last changes fastest.
Arguments:
- measured: bfloat16 [16, 2, 8, 512, 512], P('coil', None, None, 'space'), may hold values from -6 to 6
- sensitivity: bfloat16 [16, 2, 8, 512, 512], P('coil', None, None, 'space'), may hold values from -1.5 to 1.5
- sample_lines: int32 [8, 128], replicated, may hold values from 0 to 511, as said below
- kspace_first: bfloat16 [64, 2, 3, 3], replicated, may hold values from -1.5 to 1.5
- kspace_second: bfloat16 [2, 64, 3, 3], replicated, may hold values from -0.25 to 0.25
- image_first: bfloat16 [64, 2, 3, 3, 3], replicated, may hold values from -0.875 to 0.875
- image_second: bfloat16 [2, 64, 3, 3, 3], replicated, may hold values from -0.15625 to 0.15625
Outputs:
- kspace_out: bfloat16 [16, 2, 8, 512, 512], P('coil', None, None, 'space')
- image_out: bfloat16 [2, 8, 512, 512], P(None, None, 'space')
Inputs may be any that keep to these rules, and one draw needn't show every extreme that they name: `sample_lines`: each slice lists 128 distinct k-space rows, always including row 0 and row 511.
All inputs are finite; a program needn't handle non-finite values.
Results may differ from a plain program's by a relative error of at most 0.01.
Values may be sent and summed in bfloat16 or wider, within the bound.
No kernel may reach another device: no remote copies, remote signals or barrier semaphores. Data moves between devices by JAX's collectives and lax.ppermute only.
A program may use at most 64 MiB of HBM per device.

v0:
```python
import math

import jax
import jax.numpy as jnp
import numpy as np
from jax import lax
from jax.experimental import pallas as pl
from jax.experimental.pallas import tpu as pltpu
from jax.sharding import PartitionSpec as P

N = 512
COILS = 2
SLICES = 8
ROWS = 16
CH = 64
SPACE = 32
COIL = 8
PAIRS = COILS * SLICES
LANES = PAIRS * ROWS
HROWS = ROWS + 2
BF = jnp.bfloat16
F32 = jnp.float32
VMEM = pl.BlockSpec(memory_space=pltpu.VMEM)
SMEM = pl.BlockSpec(memory_space=pltpu.SMEM)
NT = (((1,), (1,)), ((), ()))


def dft_tables():
    position = np.arange(N)
    angles = (position[:, None] * position[None, :] % N).astype(np.float32) * np.float32(
        2.0 * math.pi / N
    )
    factor = np.float32(1.0 / math.sqrt(N))
    return (np.cos(angles) * factor).astype(BF), (np.sin(angles) * factor).astype(BF)


def kspace_bands():
    first = np.zeros((HROWS, 18, 128), np.float32)
    for r in range(HROWS):
        for h in range(2):
            for p in range(3):
                for q in range(3):
                    row = r + p
                    if 2 <= row < 18:
                        column = q * 32 + h * 16 + row - 2
                    else:
                        e = row if row < 2 else row - 16
                        column = 96 + q * 8 + h * 4 + e
                    first[r, h * 9 + p * 3 + q, column] = 1
    second = np.zeros((HROWS // 2, 96, 36), np.float32)
    for pair in range(HROWS // 2):
        for parity in range(2):
            for q in range(3):
                for o in range(2):
                    for r in range(ROWS):
                        p = 2 * pair + parity - r
                        if 0 <= p < 3:
                            second[pair, q * 32 + o * 16 + r, parity * 18 + q * 6 + o * 3 + p] = 1
    return first.astype(BF), second.astype(BF)


def image_bands():
    first = np.zeros((4, 54, 144), np.float32)
    for x in range(4):
        for h in range(2):
            for a in range(3):
                for p in range(3):
                    for q in range(3):
                        first[x, h * 27 + a * 9 + p * 3 + q, a * 48 + q * 16 + (x + p) * 2 + h] = 1
    second = np.zeros((2, 72, 108), np.float32)
    for pair in range(2):
        for parity in range(2):
            for o in range(2):
                for a in range(3):
                    for q in range(3):
                        for e in range(2):
                            p = 2 * pair + parity - e
                            if 0 <= p < 3:
                                second[
                                    pair,
                                    a * 24 + q * 8 + o * 2 + e,
                                    parity * 54 + o * 27 + a * 9 + p * 3 + q,
                                ] = 1
    return first.astype(BF), second.astype(BF)


def dot(a, b):
    return jnp.dot(a, b, preferred_element_type=F32)


def dot_nt(a, b):
    return lax.dot_general(a, b, NT, preferred_element_type=F32)


def before(v):
    lane = lax.broadcasted_iota(jnp.int32, v.shape, 1)
    return jnp.where(lane == 0, 0.0, pltpu.roll(v, 1, 1))


def after(v):
    lane = lax.broadcasted_iota(jnp.int32, v.shape, 1)
    return jnp.where(lane == N - 1, 0.0, pltpu.roll(v, N - 1, 1))


def blocks_swapped(tiles):
    tiles = list(tiles)
    group = lax.broadcasted_iota(jnp.int32, tiles[0].shape, 1) // 16
    for bit in (4, 2, 1):
        upper = (group & bit) != 0
        for i in range(8):
            if i & bit:
                continue
            a, b = tiles[i], tiles[i + bit]
            tiles[i] = jnp.where(upper, pltpu.roll(b, 16 * bit, 1), a)
            tiles[i + bit] = jnp.where(upper, b, pltpu.roll(a, 128 - 16 * bit, 1))
    return tiles


def wide(ref, *where):
    *lead, rows = where
    return jnp.concatenate([ref[(*lead, b, rows, slice(None))] for b in range(4)], axis=1)


def put(ref, value, *where):
    *lead, rows = where
    for b in range(4):
        ref[(*lead, b, rows, slice(None))] = value[:, b * 128 : (b + 1) * 128]


def regroup(received, left):
    for octet in range(SPACE // 8):
        for coil in range(COILS):
            tiles = [
                received[octet * 8 + i, :, :, coil * 128 : (coil + 1) * 128]
                .astype(F32)
                .reshape(32, 128)
                for i in range(8)
            ]
            for s, tile in enumerate(blocks_swapped(tiles)):
                row = coil * 128 + s * 16
                tile = tile.astype(BF)
                for h in range(2):
                    left[h, row : row + 16, octet * 128 : (octet + 1) * 128] = tile[
                        h * 16 : (h + 1) * 16
                    ]


def kspace_kernel(
    edge, measured, halo, keep, first, second, band1, band2, cos, sin, out, w1, w2, x3, hidden, refined
):
    for r in range(HROWS):
        block = dot(first[...], band1[r])
        if r == 0:
            block = block * edge[0]
        if r == HROWS - 1:
            block = block * edge[1]
        w1[r * CH : (r + 1) * CH, :] = block.astype(BF)
    for pair in range(HROWS // 2):
        w2[:, pair * 128 : (pair + 1) * 128] = dot(band2[pair], second[...]).astype(BF)

    def one(i, carry):
        c, s = i // SLICES, i % SLICES
        mask = keep[s] > 0
        own = jnp.concatenate(
            [jnp.where(mask, measured[c, h, s].astype(F32), 0.0) for h in range(2)], axis=0
        )
        rim = halo[i].astype(F32)
        x3[0:32] = before(own).astype(BF)
        x3[32:64] = own.astype(BF)
        x3[64:96] = after(own).astype(BF)
        x3[96:128] = jnp.concatenate(
            [before(rim), rim, after(rim), jnp.zeros_like(rim)], axis=0
        ).astype(BF)
        hidden[...] = jnp.maximum(dot(w1[...], x3[...]).astype(BF), 0)
        spread = dot(w2[...], hidden[...])
        total = own + before(spread[0:32]) + spread[32:64] + after(spread[64:96])
        total = total.astype(BF)
        row = pl.multiple_of(i * 16, 16)
        for h in range(2):
            refined[h, pl.ds(row, 16), :] = total[h * 16 : (h + 1) * 16]
        return carry

    lax.fori_loop(0, PAIRS, one, 0)
    for part in range(2):
        rows = pl.ds(part * 256, 256)
        co, si = cos[rows, :], sin[rows, :]
        real = dot_nt(co, refined[0]) - dot_nt(si, refined[1])
        imag = dot_nt(si, refined[0]) + dot_nt(co, refined[1])
        out[part * 16 : (part + 1) * 16, 0] = real.astype(BF).reshape(16, 16, LANES)
        out[part * 16 : (part + 1) * 16, 1] = imag.astype(BF).reshape(16, 16, LANES)


def combine_kernel(received, sens, cos, sin, out, left, image, partial):
    regroup(received, left)
    for c in range(COILS):
        rows = slice(c * 128, (c + 1) * 128)
        image[0] = dot(left[0, rows], cos[...]) - dot(left[1, rows], sin[...])
        image[1] = dot(left[0, rows], sin[...]) + dot(left[1, rows], cos[...])
        for s in range(SLICES):
            rows = slice(s * 16, (s + 1) * 16)
            real, imag = image[0, rows], image[1, rows]
            sr, si = sens[c, 0, s].astype(F32), sens[c, 1, s].astype(F32)
            pr = sr * real + si * imag
            pi = sr * imag - si * real
            if c:
                pr = pr + wide(partial, 0, rows)
                pi = pi + wide(partial, 1, rows)
            put(partial, pr, 0, rows)
            put(partial, pi, 1, rows)
    for g in range(COIL):
        for e in range(2):
            both = jnp.concatenate(
                [wide(partial, h, pl.ds(2 * g + e, 8, stride=16)) for h in range(2)], axis=0
            )
            out[g, e * 16 : (e + 1) * 16] = both.astype(BF)


def image_kernel(
    edge, previous, own, following, first, second, band1, band2, out, w1, w2, rows6, x3, acc, fin
):
    for x in range(4):
        block = dot(first[...], band1[x])
        if x == 0:
            block = block * edge[0]
        if x == 3:
            block = block * edge[1]
        w1[x * CH : (x + 1) * CH, :] = block.astype(BF)
    for pair in range(2):
        w2[:, pair * 128 : (pair + 1) * 128] = dot(band2[pair], second[...]).astype(BF)
    for n, source in enumerate((previous, own, following)):
        put(rows6, source[...].astype(F32), slice(n * 32, (n + 1) * 32))
    put(rows6, jnp.zeros((32, N), F32), slice(96, 128))
    x3[0:48] = jnp.zeros((48, N), BF)
    x3[432:480] = jnp.zeros((48, N), BF)
    for s in range(SLICES):
        v = wide(rows6, pl.ds(s, 16, stride=8))
        base = (s + 1) * 48
        x3[base : base + 16] = before(v).astype(BF)
        x3[base + 16 : base + 32] = v.astype(BF)
        x3[base + 32 : base + 48] = after(v).astype(BF)
    acc[...] = jnp.zeros_like(acc)
    for t in range(SLICES):
        hidden = jnp.maximum(dot(w1[...], x3[t * 48 : t * 48 + 144]).astype(BF), 0)
        spread = dot(w2[...], hidden)
        for a in range(3):
            s = t + 1 - a
            if 0 <= s < SLICES:
                acc[s * 24 : (s + 1) * 24] = acc[s * 24 : (s + 1) * 24] + spread[a * 24 : (a + 1) * 24]
    for s in range(SLICES):
        v = acc[s * 24 : (s + 1) * 24]
        put(fin, before(v[0:8]) + v[8:16] + after(v[16:24]), slice(s * 8, (s + 1) * 8))
    for e in range(2):
        update = jnp.concatenate([wide(fin, pl.ds(o * 2 + e, 8, stride=8)) for o in range(2)], axis=0)
        rows = slice(32 + e * 16, 48 + e * 16)
        value = (wide(rows6, rows) + update).astype(BF)
        for g in range(COIL):
            out[g, e * 16 : (e + 1) * 16] = value


def expand_kernel(gathered, sens, cos, sin, out, image_out, image, data):
    for g in range(COIL):
        for e in range(2):
            both = gathered[g, e * 16 : (e + 1) * 16].astype(F32)
            for h in range(2):
                put(image, both[h * 8 : (h + 1) * 8], h, pl.ds(2 * g + e, 8, stride=16))
    for s in range(SLICES):
        rows = slice(s * 16, (s + 1) * 16)
        real, imag = wide(image, 0, rows), wide(image, 1, rows)
        image_out[0, s] = real.astype(BF)
        image_out[1, s] = imag.astype(BF)
        for c in range(COILS):
            sr, si = sens[c, 0, s].astype(F32), sens[c, 1, s].astype(F32)
            rows = slice(c * 128 + s * 16, c * 128 + (s + 1) * 16)
            data[0, rows] = (sr * real - si * imag).astype(BF)
            data[1, rows] = (sr * imag + si * real).astype(BF)
    for part in range(2):
        rows = pl.ds(part * 256, 256)
        co, si = cos[rows, :], sin[rows, :]
        real = dot_nt(co, data[0]) + dot_nt(si, data[1])
        imag = dot_nt(co, data[1]) - dot_nt(si, data[0])
        out[part * 16 : (part + 1) * 16, 0] = real.astype(BF).reshape(16, 16, LANES)
        out[part * 16 : (part + 1) * 16, 1] = imag.astype(BF).reshape(16, 16, LANES)


def finish_kernel(received, measured, keep, cos, sin, out, left):
    regroup(received, left)
    for c in range(COILS):
        rows = slice(c * 128, (c + 1) * 128)
        real = dot(left[0, rows], cos[...]) + dot(left[1, rows], sin[...])
        imag = dot(left[1, rows], cos[...]) - dot(left[0, rows], sin[...])
        for s in range(SLICES):
            mask = keep[s] > 0
            rows = slice(s * 16, (s + 1) * 16)
            for h, value in enumerate((real, imag)):
                out[c, h, s] = jnp.where(
                    mask, measured[c, h, s].astype(F32), value[rows]
                ).astype(BF)


def call(kernel, shapes, scratch, scalars, *operands):
    single = not isinstance(shapes, list)
    return pl.pallas_call(
        kernel,
        out_shape=shapes,
        in_specs=[SMEM] * scalars + [VMEM] * (len(operands) - scalars),
        out_specs=VMEM if single else [VMEM] * len(shapes),
        scratch_shapes=scratch,
        compiler_params=pltpu.CompilerParams(vmem_limit_bytes=40 * 1024 * 1024),
    )(*operands)


def spread(array, axis):
    return lax.all_to_all(array, axis, split_axis=0, concat_axis=0, tiled=True)


def arr(*shape, dtype=BF):
    return jax.ShapeDtypeStruct(shape, dtype)


def local(
    measured, sensitivity, sample_lines, kspace_first, kspace_second, image_first, image_second
):
    space, coil = lax.axis_index("space"), lax.axis_index("coil")
    cos, sin = (jnp.asarray(t) for t in dft_tables())
    kband1, kband2 = (jnp.asarray(t) for t in kspace_bands())
    iband1, iband2 = (jnp.asarray(t) for t in image_bands())

    rows = space * ROWS + jnp.arange(ROWS, dtype=jnp.int32)
    sampled = jnp.any(sample_lines[:, :, None] == rows[None, None, :], axis=1)
    keep = sampled.astype(F32)[:, :, None]

    def rim(start):
        part = jnp.where(
            sampled[None, None, :, start : start + 2, None],
            measured[:, :, :, start : start + 2, :],
            jnp.zeros((), BF),
        )
        return part.transpose(0, 2, 1, 3, 4)

    up = [(i, i + 1) for i in range(SPACE - 1)]
    down = [(i + 1, i) for i in range(SPACE - 1)]
    low = lax.ppermute(rim(ROWS - 2), "space", up)
    high = lax.ppermute(rim(0), "space", down)
    halo = jnp.concatenate([low, high], axis=3).reshape(PAIRS, 8, N)

    def ends(first, last):
        return jnp.stack([1 - first.astype(F32), 1 - last.astype(F32)])

    kedge = ends(space == 0, space == SPACE - 1)
    kfirst = kspace_first.reshape(CH, 18)
    ksecond = kspace_second.transpose(3, 0, 2, 1).reshape(18, CH)
    zero = jnp.zeros_like(ksecond)
    ksecond = jnp.block([[ksecond, zero], [zero, ksecond]])
    ifirst = image_first.reshape(CH, 54)
    isecond = image_second.transpose(0, 2, 3, 4, 1).reshape(54, CH)
    zero = jnp.zeros_like(isecond)
    isecond = jnp.block([[isecond, zero], [zero, isecond]])

    half_done = call(
        kspace_kernel,
        arr(SPACE, 2, ROWS, LANES),
        [
            pltpu.VMEM((HROWS * CH, 128), BF),
            pltpu.VMEM((96, HROWS * CH), BF),
            pltpu.VMEM((128, N), BF),
            pltpu.VMEM((HROWS * CH, N), BF),
            pltpu.VMEM((2, LANES, N), BF),
        ],
        1,
        kedge, measured, halo, keep, kfirst, ksecond, kband1, kband2, cos, sin,
    )
    half_done = spread(half_done, "space")
    partial = call(
        combine_kernel,
        arr(COIL, 32, N),
        [
            pltpu.VMEM((2, LANES, N), BF),
            pltpu.VMEM((2, 128, N), F32),
            pltpu.VMEM((2, 4, 128, 128), F32),
        ],
        0,
        half_done, sensitivity, cos, sin,
    )
    image_in = spread(partial, "coil").astype(F32).sum(axis=0).astype(BF)

    def place(i):
        return (i % COIL) * SPACE + i // COIL

    count = COIL * SPACE
    forward = [(place(i), place(i + 1)) for i in range(count - 1)]
    previous = lax.ppermute(image_in, ("coil", "space"), forward)
    following = lax.ppermute(image_in, ("coil", "space"), [(b, a) for a, b in forward])
    iedge = ends(
        (space == 0) & (coil == 0), (space == SPACE - 1) & (coil == COIL - 1)
    )
    copies = call(
        image_kernel,
        arr(COIL, 32, N),
        [
            pltpu.VMEM((4 * CH, 144), BF),
            pltpu.VMEM((72, 4 * CH), BF),
            pltpu.VMEM((4, 128, 128), F32),
            pltpu.VMEM((480, N), BF),
            pltpu.VMEM((SLICES * 24, N), F32),
            pltpu.VMEM((4, SLICES * 8, 128), F32),
        ],
        1,
        iedge, previous, image_in, following, ifirst, isecond, iband1, iband2,
    )
    gathered = spread(copies, "coil")
    midway, image_out = call(
        expand_kernel,
        [arr(SPACE, 2, ROWS, LANES), arr(2, SLICES, ROWS, N)],
        [pltpu.VMEM((2, 4, 128, 128), F32), pltpu.VMEM((2, LANES, N), BF)],
        0,
        gathered, sensitivity, cos, sin,
    )
    midway = spread(midway, "space")
    kspace_out = call(
        finish_kernel,
        arr(COILS, 2, SLICES, ROWS, N),
        [pltpu.VMEM((2, LANES, N), BF)],
        0,
        midway, measured, keep, cos, sin,
    )
    return kspace_out, image_out


def solution(mesh):
    placed = P("coil", None, None, "space", None)
    return jax.shard_map(
        local,
        mesh=mesh,
        in_specs=(placed, placed, P(), P(), P(), P(), P()),
        out_specs=(placed, P(None, None, "space", None)),
        check_vma=False,
    )
```

profile of v0, /device:TPU:1, one launch (start us, length us, event | category | flops | bytes accessed | tf_op | source)
XLA Modules:
  0.0 144.5 jit_solution(13819090303067701311)
XLA Ops:
  0.6 0.0 copy-start.13
  0.7 0.7 copy-done.13
  1.3 0.3 compare_reduce_fusion
  1.6 0.1 fusion.8
  1.7 0.0 copy-start.11
  1.7 0.0 copy-start.12
  1.7 0.0 copy-start.1
  1.7 1.3 fusion
  3.0 0.0 copy-start
  3.0 5.1 %collective-permute-start = (bf16[2,8,2,2,512]{4,3,1,2,0:T(2,128)(2,1)S(1)}, bf16[2,8,2,2,512]{4,3,1,2,0:T(2,128)(2,1)S(1)}, u32[]{:S(2)}, u32[]{:S(2)}) collective-permute-start(bf16[2,8,2,2,512]{4,3,1,2,0:T(2,128)(2,1)S(1)} %get-tuple-element.6), channel_id=1, source_target_pairs={{0,1},{1,2},{2,3},{3,4},{4,5},{5,6},{6,7},{7,8},{8,9},{9,10},{10,1... | collective-permute-start | bytes 196616 | tf_op jit(solution)/shard_map/ppermute | solution.py:342
  8.0 1.9 %collective-permute-start.1 = (bf16[2,8,2,2,512]{4,3,1,2,0:T(2,128)(2,1)S(1)}, bf16[2,8,2,2,512]{4,3,1,2,0:T(2,128)(2,1)S(1)}, u32[]{:S(2)}, u32[]{:S(2)}) collective-permute-start(bf16[2,8,2,2,512]{4,3,1,2,0:T(2,128)(2,1)S(1)} %get-tuple-element.7), channel_id=1, source_target_pairs={{1,0},{2,1},{3,2},{4,3},{5,4},{6,5},{7,6},{8,7},{9,8},{10,9},{11,1... | collective-permute-start | bytes 196616 | tf_op jit(solution)/shard_map/ppermute | solution.py:343
  10.0 0.0 copy-done.11
  10.0 0.0 copy-done.12
  10.1 0.1 fusion.7.second
  10.2 0.1 copy.35.first
  10.3 0.1 copy.34.keep
  10.4 0.1 pad_maximum_fusion.2.edge
  10.5 0.0 collective-permute-done
  10.5 3.2 %collective-permute-done.1 = bf16[2,8,2,2,512]{4,3,1,2,0:T(2,128)(2,1)S(1)} collective-permute-done((bf16[2,8,2,2,512]{4,3,1,2,0:T(2,128)(2,1)S(1)}, bf16[2,8,2,2,512]{4,3,1,2,0:T(2,128)(2,1)S(1)}, u32[]{:S(2)}, u32[]{:S(2)}) %collective-permute-start.1) | collective-permute-done | bytes 65568 | tf_op jit(solution)/shard_map/ppermute | solution.py:343
  13.6 0.1 pad_maximum_fusion
  13.8 0.0 copy-start.7
  13.9 0.0 copy-done.1
  13.9 0.0 copy-done
  13.9 0.8 copy-done.7
  14.7 0.0 copy-start.2
  14.7 1.0 copy-done.2
  15.8 0.0 copy-start.5
  15.8 0.9 copy-done.5
  16.7 15.2 %shard_map.140 = bf16[32,2,16,256]{3,2,1,0:T(8,128)(2,1)S(1)} custom-call(f32[2]{0:T(128)S(1)} %pad_maximum_fusion.2.edge, bf16[2,2,8,16,512]{4,3,2,1,0:T(8,128)(2,1)S(1)} %copy-done.2, bf16[16,8,512]{2,1,0:T(8,128)(2,1)S(1)} %reshape.35.halo, f32[8,16,1]{2,1,0:T(8,128)S(1)} %copy.34.keep, bf16[64,18]{1,0:T(8,128)(2,1)S(1)} %copy.35.first, ...), custom_call_target="tpu_custom_call" | custom-call | tf_op jit(solution)/shard_map/pallas_call | solution.py:302
  31.9 0.0 copy-start.4
  32.0 26.0 %all_to_all.20.received = bf16[32,2,16,256]{3,2,1,0:T(8,128)(2,1)S(1)} all-to-all(bf16[32,2,16,256]{3,2,1,0:T(8,128)(2,1)S(1)} %shard_map.140), channel_id=1, replica_groups=mesh['coil'=8,'space'=32] {'space'}, dimensions={0} | all-to-all | bytes 1048576 | tf_op jit(solution)/shard_map/all_to_all | solution.py:313
  57.9 0.0 copy-done.4
  57.9 2.2 %shard_map.141 = bf16[8,32,512]{2,1,0:T(8,128)(2,1)} custom-call(bf16[32,2,16,256]{3,2,1,0:T(8,128)(2,1)S(1)} %all_to_all.20.received, bf16[2,2,8,16,512]{4,3,2,1,0:T(8,128)(2,1)S(1)} %copy-done.4, bf16[512,512]{1,0:T(8,128)(2,1)S(1)} %copy-done.1, bf16[512,512]{1,0:T(8,128)(2,1)S(1)} %copy-done), custom_call_target="tpu_custom_call" | custom-call | tf_op jit(solution)/shard_map/pallas_call | solution.py:302
  60.2 10.8 %all-to-all-start.1 = ((bf16[8,32,512]{2,1,0:T(8,128)(2,1)}), bf16[8,32,512]{2,1,0:T(8,128)(2,1)S(1)}, u32[]{:S(2)}, u32[]{:S(2)}) async-start(bf16[8,32,512]{2,1,0:T(8,128)(2,1)} %shard_map.141), calls=%async_computation.1 | async-start | bytes 524288 | tf_op jit(solution)/shard_map/all_to_all | solution.py:313
  71.0 0.0 copy-start.9
  71.0 0.7 copy-done.9
  71.7 0.1 fusion.4.second
  71.8 9.4 %all-to-all-done.1 = bf16[8,32,512]{2,1,0:T(8,128)(2,1)S(1)} async-done(((bf16[8,32,512]{2,1,0:T(8,128)(2,1)}), bf16[8,32,512]{2,1,0:T(8,128)(2,1)S(1)}, u32[]{:S(2)}, u32[]{:S(2)}) %all-to-all-start.1) | async-done | bytes 262176 | tf_op jit(solution)/shard_map/all_to_all | solution.py:313
  81.2 0.0 copy-start.10
  81.2 0.0 copy-start.6
  81.2 6.7 %collective-permute-start.3 = (bf16[32,512]{1,0:T(8,128)(2,1)S(1)}, bf16[32,512]{1,0:T(8,128)(2,1)S(1)}, u32[]{:S(2)}, u32[]{:S(2)}) collective-permute-start(bf16[32,512]{1,0:T(8,128)(2,1)S(1)} %reduce_sum.12.own), channel_id=1, source_target_pairs={{32,0},{64,32},{96,64},{128,96},{160,128},{192,160},{224,192},{1,2... | collective-permute-start | bytes 98312 | tf_op jit(solution)/shard_map/ppermute | solution.py:392
  87.9 1.9 %collective-permute-start.2 = (bf16[32,512]{1,0:T(8,128)(2,1)S(1)}, bf16[32,512]{1,0:T(8,128)(2,1)S(1)}, u32[]{:S(2)}, u32[]{:S(2)}) collective-permute-start(bf16[32,512]{1,0:T(8,128)(2,1)S(1)} %reduce_sum.12.own), channel_id=1, source_target_pairs={{0,32},{32,64},{64,96},{96,128},{128,160},{160,192},{192,224},{224... | collective-permute-start | bytes 98312 | tf_op jit(solution)/shard_map/ppermute | solution.py:391
  89.8 0.1 pad_maximum_fusion.1.edge
  89.9 0.0 copy-done.10
  89.9 0.0 copy-start.8
  90.0 0.1 copy.38.first
  90.1 0.0 collective-permute-done.3.following
  90.1 9.1 %collective-permute-done.2.previous = bf16[32,512]{1,0:T(8,128)(2,1)S(1)} collective-permute-done((bf16[32,512]{1,0:T(8,128)(2,1)S(1)}, bf16[32,512]{1,0:T(8,128)(2,1)S(1)}, u32[]{:S(2)}, u32[]{:S(2)}) %collective-permute-start.2) | collective-permute-done | bytes 32800 | tf_op jit(solution)/shard_map/ppermute | solution.py:391
  99.2 0.0 copy-done.6
  99.2 0.0 copy-done.8
  99.2 2.7 %shard_map.142 = bf16[8,32,512]{2,1,0:T(8,128)(2,1)S(1)} custom-call(f32[2]{0:T(128)S(1)} %pad_maximum_fusion.1.edge, bf16[32,512]{1,0:T(8,128)(2,1)S(1)} %collective-permute-done.2.previous, bf16[32,512]{1,0:T(8,128)(2,1)S(1)} %reduce_sum.12.own, bf16[32,512]{1,0:T(8,128)(2,1)S(1)} %collective-permute-done.3.following, bf16[64,54]{1,0:T(8,128)(2,1)S(1)} %copy.38.first, ...), custom_call_target="tpu_custom_call" | custom-call | tf_op jit(solution)/shard_map/pallas_call | solution.py:302
  101.9 12.4 %all_to_all.21.gathered = bf16[8,32,512]{2,1,0:T(8,128)(2,1)S(1)} all-to-all(bf16[8,32,512]{2,1,0:T(8,128)(2,1)S(1)} %shard_map.142), channel_id=1, replica_groups=mesh['coil'=8,'space'=32] {'coil'}, dimensions={0} | all-to-all | bytes 524288 | tf_op jit(solution)/shard_map/all_to_all | solution.py:313
  114.3 1.4 shard_map.143
  115.7 0.0 copy-start.3
  115.7 26.7 %all_to_all.22.received = bf16[32,2,16,256]{3,2,1,0:T(8,128)(2,1)S(1)} all-to-all(bf16[32,2,16,256]{3,2,1,0:T(8,128)(2,1)S(1)} %get-tuple-element.4), channel_id=1, replica_groups=mesh['coil'=8,'space'=32] {'space'}, dimensions={0} | all-to-all | bytes 1048576 | tf_op jit(solution)/shard_map/all_to_all | solution.py:313
  142.4 0.0 copy-done.3
  142.4 2.1 %shard_map.144 = bf16[2,2,8,16,512]{4,3,2,1,0:T(8,128)(2,1)} custom-call(bf16[32,2,16,256]{3,2,1,0:T(8,128)(2,1)S(1)} %all_to_all.22.received, bf16[2,2,8,16,512]{4,3,2,1,0:T(8,128)(2,1)S(1)} %copy-done.3, f32[8,16,1]{2,1,0:T(8,128)S(1)} %copy.34.keep, bf16[512,512]{1,0:T(8,128)(2,1)S(1)} %copy-done.1, bf16[512,512]{1,0:T(8,128)(2,1)S(1)} %copy-done), custom_call_target="tpu_custom_call" | custom-call | tf_op jit(solution)/shard_map/pallas_call | solution.py:302
  (13 shorter events, 0.2 us)
Async XLA Ops:
  0.6 0.7 copy-start.13
  1.7 8.3 %copy-start.11 = (bf16[64,2,3,3]{0,1,3,2:T(2,128)(2,1)S(1)}, bf16[64,2,3,3]{0,1,3,2:T(2,128)(2,1)}, u32[]{:S(2)}) copy-start(bf16[64,2,3,3]{0,1,3,2:T(2,128)(2,1)} %param.16) | copy-start | bytes 6916
  1.7 8.4 %copy-start.12 = (bf16[2,64,3,3]{1,0,3,2:T(2,128)(2,1)S(1)}, bf16[2,64,3,3]{1,0,3,2:T(2,128)(2,1)}, u32[]{:S(2)}) copy-start(bf16[2,64,3,3]{1,0,3,2:T(2,128)(2,1)} %param.17) | copy-start | bytes 6916
  1.7 12.2 %copy-start.1 = (bf16[512,512]{1,0:T(8,128)(2,1)S(1)}, bf16[512,512]{1,0:T(8,128)(2,1)}, u32[]{:S(2)}) copy-start(bf16[512,512]{1,0:T(8,128)(2,1)} %constant.39.clone.cos) | copy-start | bytes 1572868
  3.0 10.9 %copy-start = (bf16[512,512]{1,0:T(8,128)(2,1)S(1)}, bf16[512,512]{1,0:T(8,128)(2,1)}, u32[]{:S(2)}) copy-start(bf16[512,512]{1,0:T(8,128)(2,1)} %constant.40.clone.sin) | copy-start | bytes 1572868
  3.0 7.5 %collective-permute-start = (bf16[2,8,2,2,512]{4,3,1,2,0:T(2,128)(2,1)S(1)}, bf16[2,8,2,2,512]{4,3,1,2,0:T(2,128)(2,1)S(1)}, u32[]{:S(2)}, u32[]{:S(2)}) collective-permute-start(bf16[2,8,2,2,512]{4,3,1,2,0:T(2,128)(2,1)S(1)} %get-tuple-element.6), channel_id=1, source_target_pairs={{0,1},{1,2},{2,3},{3,4},{4,5},{5,6},{6,7},{7,8},{8,9},{9,10},{10,1... | collective-permute-start | bytes 196616 | tf_op jit(solution)/shard_map/ppermute | solution.py:342
  8.0 5.6 %collective-permute-start.1 = (bf16[2,8,2,2,512]{4,3,1,2,0:T(2,128)(2,1)S(1)}, bf16[2,8,2,2,512]{4,3,1,2,0:T(2,128)(2,1)S(1)}, u32[]{:S(2)}, u32[]{:S(2)}) collective-permute-start(bf16[2,8,2,2,512]{4,3,1,2,0:T(2,128)(2,1)S(1)} %get-tuple-element.7), channel_id=1, source_target_pairs={{1,0},{2,1},{3,2},{4,3},{5,4},{6,5},{7,6},{8,7},{9,8},{10,9},{11,1... | collective-permute-start | bytes 196616 | tf_op jit(solution)/shard_map/ppermute | solution.py:343
  13.8 0.9 copy-start.7
  14.7 1.0 copy-start.2
  15.8 0.9 copy-start.5
  31.9 26.0 %copy-start.4 = (bf16[2,2,8,16,512]{4,3,2,1,0:T(8,128)(2,1)S(1)}, bf16[2,2,8,16,512]{4,3,2,1,0:T(8,128)(2,1)}, u32[]{:S(2)}) copy-start(bf16[2,2,8,16,512]{4,3,2,1,0:T(8,128)(2,1)} %sens.3) | copy-start | bytes 1572868
  60.2 21.0 %all-to-all-start.1 = ((bf16[8,32,512]{2,1,0:T(8,128)(2,1)}), bf16[8,32,512]{2,1,0:T(8,128)(2,1)S(1)}, u32[]{:S(2)}, u32[]{:S(2)}) async-start(bf16[8,32,512]{2,1,0:T(8,128)(2,1)} %shard_map.141), calls=%async_computation.1 | async-start | bytes 524288 | tf_op jit(solution)/shard_map/all_to_all | solution.py:313
  71.0 0.7 copy-start.9
  81.2 8.8 %copy-start.10 = (bf16[64,2,3,3,3]{0,1,4,3,2:T(2,128)(2,1)S(1)}, bf16[64,2,3,3,3]{0,1,4,3,2:T(2,128)(2,1)}, u32[]{:S(2)}) copy-start(bf16[64,2,3,3,3]{0,1,4,3,2:T(2,128)(2,1)} %param.18) | copy-start | bytes 20740
  81.2 18.0 %copy-start.6 = (bf16[4,54,144]{2,1,0:T(8,128)(2,1)S(1)}, bf16[4,54,144]{2,1,0:T(8,128)(2,1)}, u32[]{:S(2)}) copy-start(bf16[4,54,144]{2,1,0:T(8,128)(2,1)} %constant.43.clone.band1) | copy-start | bytes 186628
  81.2 8.9 %collective-permute-start.3 = (bf16[32,512]{1,0:T(8,128)(2,1)S(1)}, bf16[32,512]{1,0:T(8,128)(2,1)S(1)}, u32[]{:S(2)}, u32[]{:S(2)}) collective-permute-start(bf16[32,512]{1,0:T(8,128)(2,1)S(1)} %reduce_sum.12.own), channel_id=1, source_target_pairs={{32,0},{64,32},{96,64},{128,96},{160,128},{192,160},{224,192},{1,2... | collective-permute-start | bytes 98312 | tf_op jit(solution)/shard_map/ppermute | solution.py:392
  87.9 11.3 %collective-permute-start.2 = (bf16[32,512]{1,0:T(8,128)(2,1)S(1)}, bf16[32,512]{1,0:T(8,128)(2,1)S(1)}, u32[]{:S(2)}, u32[]{:S(2)}) collective-permute-start(bf16[32,512]{1,0:T(8,128)(2,1)S(1)} %reduce_sum.12.own), channel_id=1, source_target_pairs={{0,32},{32,64},{64,96},{96,128},{128,160},{160,192},{192,224},{224... | collective-permute-start | bytes 98312 | tf_op jit(solution)/shard_map/ppermute | solution.py:391
  89.9 9.2 %copy-start.8 = (bf16[2,72,108]{2,1,0:T(8,128)(2,1)S(1)}, bf16[2,72,108]{2,1,0:T(8,128)(2,1)}, u32[]{:S(2)}) copy-start(bf16[2,72,108]{2,1,0:T(8,128)(2,1)} %constant.44.clone.band2) | copy-start | bytes 93316
  115.7 26.7 %copy-start.3 = (bf16[2,2,8,16,512]{4,3,2,1,0:T(8,128)(2,1)S(1)}, bf16[2,2,8,16,512]{4,3,2,1,0:T(8,128)(2,1)}, u32[]{:S(2)}) copy-start(bf16[2,2,8,16,512]{4,3,2,1,0:T(8,128)(2,1)} %measured.3) | copy-start | bytes 1572868
where the time goes:
time: 145 us; the launch traced here: 144 us
  blocking collectives  65 us (45%)
  starting transfers between devices  26.4 us (18%)
  Pallas kernels  23.7 us (16%)
  waiting for transfers between devices  21.6 us (15%)
  local copies, waits for them, and re-layouts  4.81 us (3%)
  other arithmetic  2.06 us (1%)
    all_to_all x3, blocking collectives, spread(): return lax.all_to_all(array, axis, split_axis=0, concat_axis=0, tiled=True)  65 us
    pallas_call x5, Pallas kernels, call(): pl.pallas_call(kernel, out_shape=shapes, in_specs=[SMEM] * scalars + [VME...  23.7 us
    all_to_all x1, starting transfers between devices, spread(): return lax.all_to_all(array, axis, split_axis=0, concat_axis=0, tiled=True)  10.8 us
    all_to_all x1, waiting for transfers between devices, spread(): return lax.all_to_all(array, axis, split_axis=0, concat_axis=0, tiled=True)  9.37 us
    ppermute x1, waiting for transfers between devices, local(): previous = lax.ppermute(image_in, ('coil', 'space'), forward)  9.09 us
    ppermute x1, starting transfers between devices, local(): lax.ppermute(image_in, ('coil', 'space'), [(b, a) for a, b in forward])  6.69 us
    ppermute x1, starting transfers between devices, local(): low = lax.ppermute(rim(ROWS - 2), 'space', up)  5.06 us
    unnamed x30, local copies, waits for them, and re-layouts  4.22 us
  transfers between devices with their start and end apart: 5, of which 3 were waited for; matrix products, arithmetic and copies ran while one was open for 1% of the time, Pallas kernels for 0%

commit v1 on v0

--- a/solution.py
+++ b/solution.py
@@ -6,6 +6,7 @@
 from jax import lax
 from jax.experimental import pallas as pl
 from jax.experimental.pallas import tpu as pltpu
+from jax.sharding import Mesh
 from jax.sharding import PartitionSpec as P
 
 N = 512
@@ -14,7 +15,8 @@
 ROWS = 16
 CH = 64
 SPACE = 32
-COIL = 8
+RING = 4
+HALVES = 2
 PAIRS = COILS * SLICES
 LANES = PAIRS * ROWS
 HROWS = ROWS + 2
@@ -60,25 +62,25 @@
 
 
 def image_bands():
-    first = np.zeros((4, 54, 144), np.float32)
-    for x in range(4):
+    first = np.zeros((6, 54, 144), np.float32)
+    for x in range(6):
         for h in range(2):
             for a in range(3):
                 for p in range(3):
                     for q in range(3):
                         first[x, h * 27 + a * 9 + p * 3 + q, a * 48 + q * 16 + (x + p) * 2 + h] = 1
-    second = np.zeros((2, 72, 108), np.float32)
-    for pair in range(2):
+    second = np.zeros((3, 72, 108), np.float32)
+    for pair in range(3):
         for parity in range(2):
             for o in range(2):
                 for a in range(3):
                     for q in range(3):
-                        for e in range(2):
+                        for e in range(4):
                             p = 2 * pair + parity - e
                             if 0 <= p < 3:
                                 second[
                                     pair,
-                                    a * 24 + q * 8 + o * 2 + e,
+                                    a * 24 + q * 8 + o * 4 + e,
                                     parity * 54 + o * 27 + a * 9 + p * 3 + q,
                                 ] = 1
     return first.astype(BF), second.astype(BF)
@@ -207,33 +209,33 @@
                 pi = pi + wide(partial, 1, rows)
             put(partial, pr, 0, rows)
             put(partial, pi, 1, rows)
-    for g in range(COIL):
-        for e in range(2):
-            both = jnp.concatenate(
-                [wide(partial, h, pl.ds(2 * g + e, 8, stride=16)) for h in range(2)], axis=0
-            )
-            out[g, e * 16 : (e + 1) * 16] = both.astype(BF)
+    for x in range(ROWS):
+        both = jnp.concatenate(
+            [wide(partial, h, pl.ds(x, 8, stride=16)) for h in range(2)], axis=0
+        )
+        out[x // 4, x % 4 * 16 : (x % 4 + 1) * 16] = both.astype(BF)
 
 
 def image_kernel(
-    edge, previous, own, following, first, second, band1, band2, out, w1, w2, rows6, x3, acc, fin
+    edge, own, other, before1, before2, after1, after2, first, second, band1, band2, out,
+    w1, w2, rows8, x3, acc, fin
 ):
-    for x in range(4):
+    for x in range(6):
         block = dot(first[...], band1[x])
         if x == 0:
             block = block * edge[0]
-        if x == 3:
+        if x == 5:
             block = block * edge[1]
         w1[x * CH : (x + 1) * CH, :] = block.astype(BF)
-    for pair in range(2):
+    for pair in range(3):
         w2[:, pair * 128 : (pair + 1) * 128] = dot(band2[pair], second[...]).astype(BF)
-    for n, source in enumerate((previous, own, following)):
-        put(rows6, source[...].astype(F32), slice(n * 32, (n + 1) * 32))
-    put(rows6, jnp.zeros((32, N), F32), slice(96, 128))
+    for start, stop, a, b in ((0, 32, before1, before2), (32, 96, own, other), (96, 128, after1, after2)):
+        total = (a[...].astype(F32) + b[...].astype(F32)).astype(BF)
+        put(rows8, total.astype(F32), slice(start, stop))
     x3[0:48] = jnp.zeros((48, N), BF)
     x3[432:480] = jnp.zeros((48, N), BF)
     for s in range(SLICES):
-        v = wide(rows6, pl.ds(s, 16, stride=8))
+        v = wide(rows8, pl.ds(s, 16, stride=8))
         base = (s + 1) * 48
         x3[base : base + 16] = before(v).astype(BF)
         x3[base + 16 : base + 32] = v.astype(BF)
@@ -249,20 +251,18 @@
     for s in range(SLICES):
         v = acc[s * 24 : (s + 1) * 24]
         put(fin, before(v[0:8]) + v[8:16] + after(v[16:24]), slice(s * 8, (s + 1) * 8))
-    for e in range(2):
-        update = jnp.concatenate([wide(fin, pl.ds(o * 2 + e, 8, stride=8)) for o in range(2)], axis=0)
-        rows = slice(32 + e * 16, 48 + e * 16)
-        value = (wide(rows6, rows) + update).astype(BF)
-        for g in range(COIL):
-            out[g, e * 16 : (e + 1) * 16] = value
+    for e in range(4):
+        update = jnp.concatenate([wide(fin, pl.ds(o * 4 + e, 8, stride=8)) for o in range(2)], axis=0)
+        value = (wide(rows8, slice(32 + e * 16, 48 + e * 16)) + update).astype(BF)
+        for y in range(RING):
+            out[y, e * 16 : (e + 1) * 16] = value
 
 
 def expand_kernel(gathered, sens, cos, sin, out, image_out, image, data):
-    for g in range(COIL):
-        for e in range(2):
-            both = gathered[g, e * 16 : (e + 1) * 16].astype(F32)
-            for h in range(2):
-                put(image, both[h * 8 : (h + 1) * 8], h, pl.ds(2 * g + e, 8, stride=16))
+    for x in range(ROWS):
+        both = gathered[x // 4, x % 4 * 16 : (x % 4 + 1) * 16].astype(F32)
+        for h in range(2):
+            put(image, both[h * 8 : (h + 1) * 8], h, pl.ds(x, 8, stride=16))
     for s in range(SLICES):
         rows = slice(s * 16, (s + 1) * 16)
         real, imag = wide(image, 0, rows), wide(image, 1, rows)
@@ -320,7 +320,7 @@
 def local(
     measured, sensitivity, sample_lines, kspace_first, kspace_second, image_first, image_second
 ):
-    space, coil = lax.axis_index("space"), lax.axis_index("coil")
+    space, ring = lax.axis_index("space"), lax.axis_index("ring")
     cos, sin = (jnp.asarray(t) for t in dft_tables())
     kband1, kband2 = (jnp.asarray(t) for t in kspace_bands())
     iband1, iband2 = (jnp.asarray(t) for t in image_bands())
@@ -372,7 +372,7 @@
     half_done = spread(half_done, "space")
     partial = call(
         combine_kernel,
-        arr(COIL, 32, N),
+        arr(RING, 64, N),
         [
             pltpu.VMEM((2, LANES, N), BF),
             pltpu.VMEM((2, 128, N), F32),
@@ -381,33 +381,45 @@
         0,
         half_done, sensitivity, cos, sin,
     )
-    image_in = spread(partial, "coil").astype(F32).sum(axis=0).astype(BF)
-
-    def place(i):
-        return (i % COIL) * SPACE + i // COIL
-
-    count = COIL * SPACE
-    forward = [(place(i), place(i + 1)) for i in range(count - 1)]
-    previous = lax.ppermute(image_in, ("coil", "space"), forward)
-    following = lax.ppermute(image_in, ("coil", "space"), [(b, a) for a, b in forward])
-    iedge = ends(
-        (space == 0) & (coil == 0), (space == SPACE - 1) & (coil == COIL - 1)
-    )
+    part = spread(partial, "ring").astype(F32).sum(axis=0).astype(BF)
+
+    def place(half, i):
+        return (half * RING + i % RING) * SPACE + i // RING
+
+    count = RING * SPACE
+    axes = ("half", "ring", "space")
+
+    def moved(array, step, flip):
+        pairs = [
+            (place(half, i), place(half ^ flip, i + step))
+            for half in range(HALVES)
+            for i in range(count)
+            if 0 <= i + step < count
+        ]
+        return lax.ppermute(array, axes, pairs)
+
+    low, high = part[:32], part[32:]
+    before2 = moved(high, 1, 1)
+    after2 = moved(low, -1, 1)
+    other = moved(part, 0, 1)
+    before1 = moved(high, 1, 0)
+    after1 = moved(low, -1, 0)
+    iedge = ends((space == 0) & (ring == 0), (space == SPACE - 1) & (ring == RING - 1))
     copies = call(
         image_kernel,
-        arr(COIL, 32, N),
+        arr(RING, 64, N),
         [
-            pltpu.VMEM((4 * CH, 144), BF),
-            pltpu.VMEM((72, 4 * CH), BF),
+            pltpu.VMEM((6 * CH, 144), BF),
+            pltpu.VMEM((72, 6 * CH), BF),
             pltpu.VMEM((4, 128, 128), F32),
             pltpu.VMEM((480, N), BF),
             pltpu.VMEM((SLICES * 24, N), F32),
             pltpu.VMEM((4, SLICES * 8, 128), F32),
         ],
         1,
-        iedge, previous, image_in, following, ifirst, isecond, iband1, iband2,
-    )
-    gathered = spread(copies, "coil")
+        iedge, part, other, before1, before2, after1, after2, ifirst, isecond, iband1, iband2,
+    )
+    gathered = spread(copies, "ring")
     midway, image_out = call(
         expand_kernel,
         [arr(SPACE, 2, ROWS, LANES), arr(2, SLICES, ROWS, N)],
@@ -427,7 +439,8 @@
 
 
 def solution(mesh):
-    placed = P("coil", None, None, "space", None)
+    mesh = Mesh(mesh.devices.reshape(HALVES, RING, SPACE), ("half", "ring", "space"))
+    placed = P(("half", "ring"), None, None, "space", None)
     return jax.shard_map(
         local,
         mesh=mesh,

time: 145 us -> 136 us (0.938)
  waiting for transfers between devices: 21.6 us -> 10.2 us
  starting transfers between devices: 26.4 us -> 34.5 us
  blocking collectives: 65 us -> 58.9 us
    ppermute x2 -> x5, starting transfers between devices: 8.61 us -> 23.3 us  [moved(): return lax.ppermute(array, axes, pairs)]
    ppermute x2 -> x5, waiting for transfers between devices: 9.09 us -> 1.72 us  [moved(): return lax.ppermute(array, axes, pairs)]
    all_to_all x1, starting transfers between devices: 10.8 us -> 4.18 us  [spread(): return lax.all_to_all(array, axis, split_axis=0, concat_axis=0, tiled=True)]
    all_to_all x3, blocking collectives: 65 us -> 58.9 us  [spread(): return lax.all_to_all(array, axis, split_axis=0, concat_axis=0, tiled=True)]
    all_to_all x1, waiting for transfers between devices: 9.37 us -> 5.31 us  [spread(): return lax.all_to_all(array, axis, split_axis=0, concat_axis=0, tiled=True)]
  transfers between devices with their start and end apart: 5 -> 8, of which waited for: 3 -> 4; matrix products, arithmetic and copies ran while one was open for 1% -> 1% of each run, Pallas kernels for 0% -> 0%
where the time goes in v1:
time: 136 us; the launch traced here: 135 us
  blocking collectives  58.9 us (43%)
  starting transfers between devices  34.5 us (25%)
  Pallas kernels  24.1 us (18%)
  waiting for transfers between devices  10.2 us (7%)
  local copies, waits for them, and re-layouts  4.84 us (4%)
  other arithmetic  2.06 us (2%)
    all_to_all x3, blocking collectives, spread(): return lax.all_to_all(array, axis, split_axis=0, concat_axis=0, tiled=True)  58.9 us
    pallas_call x5, Pallas kernels, call(): pl.pallas_call(kernel, out_shape=shapes, in_specs=[SMEM] * scalars + [VME...  24.1 us
    ppermute x5, starting transfers between devices, moved(): return lax.ppermute(array, axes, pairs)  23.3 us
    all_to_all x1, waiting for transfers between devices, spread(): return lax.all_to_all(array, axis, split_axis=0, concat_axis=0, tiled=True)  5.31 us
    ppermute x1, starting transfers between devices, local(): low = lax.ppermute(rim(ROWS - 2), 'space', up)  5.06 us
    unnamed x30, local copies, waits for them, and re-layouts  4.24 us
    all_to_all x1, starting transfers between devices, spread(): return lax.all_to_all(array, axis, split_axis=0, concat_axis=0, tiled=True)  4.18 us
    ppermute x1, waiting for transfers between devices, local(): high = lax.ppermute(rim(0), 'space', down)  3.16 us
  transfers between devices with their start and end apart: 8, of which 4 were waited for; matrix products, arithmetic and copies ran while one was open for 1% of the time, Pallas kernels for 0%

profile of v1, /device:TPU:1, one launch (start us, length us, event | category | flops | bytes accessed | tf_op | source)
XLA Modules:
  0.0 135.4 jit_solution(7267107980898713192)
XLA Ops:
  0.6 0.0 copy-start.13
  0.7 0.7 copy-done.13
  1.3 0.3 compare_reduce_fusion
  1.6 0.1 fusion.9
  1.7 0.0 copy-start.11
  1.7 0.0 copy-start.12
  1.7 0.0 copy-start.1
  1.7 1.3 fusion
  3.0 0.0 copy-start
  3.0 5.1 %collective-permute-start = (bf16[2,8,2,2,512]{4,3,1,2,0:T(2,128)(2,1)S(1)}, bf16[2,8,2,2,512]{4,3,1,2,0:T(2,128)(2,1)S(1)}, u32[]{:S(2)}, u32[]{:S(2)}) collective-permute-start(bf16[2,8,2,2,512]{4,3,1,2,0:T(2,128)(2,1)S(1)} %get-tuple-element.6), channel_id=1, source_target_pairs={{0,1},{1,2},{2,3},{3,4},{4,5},{5,6},{6,7},{7,8},{8,9},{9,10},{10,1... | collective-permute-start | bytes 196616 | tf_op jit(solution)/shard_map/ppermute | solution.py:342
  8.0 1.9 %collective-permute-start.1 = (bf16[2,8,2,2,512]{4,3,1,2,0:T(2,128)(2,1)S(1)}, bf16[2,8,2,2,512]{4,3,1,2,0:T(2,128)(2,1)S(1)}, u32[]{:S(2)}, u32[]{:S(2)}) collective-permute-start(bf16[2,8,2,2,512]{4,3,1,2,0:T(2,128)(2,1)S(1)} %get-tuple-element.7), channel_id=1, source_target_pairs={{1,0},{2,1},{3,2},{4,3},{5,4},{6,5},{7,6},{8,7},{9,8},{10,9},{11,1... | collective-permute-start | bytes 196616 | tf_op jit(solution)/shard_map/ppermute | solution.py:343
  10.0 0.0 copy-done.11
  10.0 0.0 copy-done.12
  10.1 0.1 fusion.7.second
  10.2 0.1 copy.35.first
  10.3 0.1 copy.34.keep
  10.4 0.1 pad_maximum_fusion.2.edge
  10.5 0.0 collective-permute-done
  10.5 3.2 %collective-permute-done.1 = bf16[2,8,2,2,512]{4,3,1,2,0:T(2,128)(2,1)S(1)} collective-permute-done((bf16[2,8,2,2,512]{4,3,1,2,0:T(2,128)(2,1)S(1)}, bf16[2,8,2,2,512]{4,3,1,2,0:T(2,128)(2,1)S(1)}, u32[]{:S(2)}, u32[]{:S(2)}) %collective-permute-start.1) | collective-permute-done | bytes 65568 | tf_op jit(solution)/shard_map/ppermute | solution.py:343
  13.6 0.1 pad_maximum_fusion
  13.8 0.0 copy-start.7
  13.9 0.0 copy-done.1
  13.9 0.0 copy-done
  13.9 0.8 copy-done.7
  14.7 0.0 copy-start.2
  14.7 1.0 copy-done.2
  15.8 0.0 copy-start.5
  15.8 0.9 copy-done.5
  16.7 15.2 %shard_map.140 = bf16[32,2,16,256]{3,2,1,0:T(8,128)(2,1)S(1)} custom-call(f32[2]{0:T(128)S(1)} %pad_maximum_fusion.2.edge, bf16[2,2,8,16,512]{4,3,2,1,0:T(8,128)(2,1)S(1)} %copy-done.2, bf16[16,8,512]{2,1,0:T(8,128)(2,1)S(1)} %reshape.35.halo, f32[8,16,1]{2,1,0:T(8,128)S(1)} %copy.34.keep, bf16[64,18]{1,0:T(8,128)(2,1)S(1)} %copy.35.first, ...), custom_call_target="tpu_custom_call" | custom-call | tf_op jit(solution)/shard_map/pallas_call | solution.py:302
  31.9 0.0 copy-start.4
  32.0 26.0 %all_to_all.20.received = bf16[32,2,16,256]{3,2,1,0:T(8,128)(2,1)S(1)} all-to-all(bf16[32,2,16,256]{3,2,1,0:T(8,128)(2,1)S(1)} %shard_map.140), channel_id=1, replica_groups=mesh['half'=2,'ring'=4,'space'=32] {'space'}, dimensions={0} | all-to-all | bytes 1048576 | tf_op jit(solution)/shard_map/all_to_all | solution.py:313
  57.9 0.0 copy-done.4
  57.9 2.2 %shard_map.141 = bf16[4,64,512]{2,1,0:T(8,128)(2,1)} custom-call(bf16[32,2,16,256]{3,2,1,0:T(8,128)(2,1)S(1)} %all_to_all.20.received, bf16[2,2,8,16,512]{4,3,2,1,0:T(8,128)(2,1)S(1)} %copy-done.4, bf16[512,512]{1,0:T(8,128)(2,1)S(1)} %copy-done.1, bf16[512,512]{1,0:T(8,128)(2,1)S(1)} %copy-done), custom_call_target="tpu_custom_call" | custom-call | tf_op jit(solution)/shard_map/pallas_call | solution.py:302
  60.2 4.2 %all-to-all-start.1 = ((bf16[4,64,512]{2,1,0:T(8,128)(2,1)}), bf16[4,64,512]{2,1,0:T(8,128)(2,1)S(1)}, u32[]{:S(2)}, u32[]{:S(2)}) async-start(bf16[4,64,512]{2,1,0:T(8,128)(2,1)} %shard_map.141), calls=%async_computation.1 | async-start | bytes 524288 | tf_op jit(solution)/shard_map/all_to_all | solution.py:313
  64.3 0.0 copy-start.9
  64.3 0.7 copy-done.9
  65.1 0.1 fusion.4.second
  65.2 5.3 %all-to-all-done.1 = bf16[4,64,512]{2,1,0:T(8,128)(2,1)S(1)} async-done(((bf16[4,64,512]{2,1,0:T(8,128)(2,1)}), bf16[4,64,512]{2,1,0:T(8,128)(2,1)S(1)}, u32[]{:S(2)}, u32[]{:S(2)}) %all-to-all-start.1) | async-done | bytes 262176 | tf_op jit(solution)/shard_map/all_to_all | solution.py:313
  70.5 0.0 copy-start.10
  70.5 0.0 copy-start.6
  70.6 0.0 copy-start.8
  70.6 10.9 %collective-permute-start.6 = (bf16[32,512]{1,0:T(8,128)(2,1)S(1)}, bf16[32,512]{1,0:T(8,128)(2,1)S(1)}, u32[]{:S(2)}, u32[]{:S(2)}) collective-permute-start(bf16[32,512]{1,0:T(8,128)(2,1)S(1)} %get-tuple-element.8), channel_id=1, source_target_pairs={{32,128},{64,160},{96,192},{1,224},{33,129},{65,161},{97,193},{2,2... | collective-permute-start | bytes 98312 | tf_op jit(solution)/shard_map/ppermute | solution.py:399
  81.5 1.9 %collective-permute-start.5 = (bf16[32,512]{1,0:T(8,128)(2,1)S(1)}, bf16[32,512]{1,0:T(8,128)(2,1)S(1)}, u32[]{:S(2)}, u32[]{:S(2)}) collective-permute-start(bf16[32,512]{1,0:T(8,128)(2,1)S(1)} %get-tuple-element.8), channel_id=1, source_target_pairs={{32,0},{64,32},{96,64},{1,96},{33,1},{65,33},{97,65},{2,97},{34,2}... | collective-permute-start | bytes 98312 | tf_op jit(solution)/shard_map/ppermute | solution.py:399
  83.4 1.9 %collective-permute-start.4 = (bf16[32,512]{1,0:T(8,128)(2,1)S(1)}, bf16[32,512]{1,0:T(8,128)(2,1)S(1)}, u32[]{:S(2)}, u32[]{:S(2)}) collective-permute-start(bf16[32,512]{1,0:T(8,128)(2,1)S(1)} %get-tuple-element.9), channel_id=1, source_target_pairs={{0,160},{32,192},{64,224},{96,129},{1,161},{33,193},{65,225},{97,1... | collective-permute-start | bytes 98312 | tf_op jit(solution)/shard_map/ppermute | solution.py:399
  85.4 3.4 %collective-permute-start.3 = (bf16[32,512]{1,0:T(8,128)(2,1)S(1)}, bf16[32,512]{1,0:T(8,128)(2,1)S(1)}, u32[]{:S(2)}, u32[]{:S(2)}) collective-permute-start(bf16[32,512]{1,0:T(8,128)(2,1)S(1)} %get-tuple-element.9), channel_id=1, source_target_pairs={{0,32},{32,64},{64,96},{96,1},{1,33},{33,65},{65,97},{97,2},{2,34}... | collective-permute-start | bytes 98312 | tf_op jit(solution)/shard_map/ppermute | solution.py:399
  88.7 5.2 %collective-permute-start.2 = (bf16[64,512]{1,0:T(8,128)(2,1)S(1)}, bf16[64,512]{1,0:T(8,128)(2,1)S(1)}, u32[]{:S(2)}, u32[]{:S(2)}) collective-permute-start(bf16[64,512]{1,0:T(8,128)(2,1)S(1)} %reduce_sum.12.own), channel_id=1, source_target_pairs={{0,128},{32,160},{64,192},{96,224},{1,129},{33,161},{65,193},{97,2... | collective-permute-start | bytes 196616 | tf_op jit(solution)/shard_map/ppermute | solution.py:399
  93.9 0.1 pad_maximum_fusion.1.edge
  94.0 0.0 copy-done.10
  94.0 0.1 copy.38.first
  94.1 0.0 collective-permute-done.6.after2
  94.1 0.0 collective-permute-done.5.after1
  94.1 0.6 collective-permute-done.4.before2
  94.8 0.0 collective-permute-done.3.before1
  94.8 1.1 collective-permute-done.2.other
  95.8 0.0 copy-done.6
  95.8 0.0 copy-done.8
  95.8 3.0 %shard_map.142 = bf16[4,64,512]{2,1,0:T(8,128)(2,1)S(1)} custom-call(f32[2]{0:T(128)S(1)} %pad_maximum_fusion.1.edge, bf16[64,512]{1,0:T(8,128)(2,1)S(1)} %reduce_sum.12.own, bf16[64,512]{1,0:T(8,128)(2,1)S(1)} %collective-permute-done.2.other, bf16[32,512]{1,0:T(8,128)(2,1)S(1)} %collective-permute-done.3.before1, ...), custom_call_target="tpu_custom_call" | custom-call | tf_op jit(solution)/shard_map/pallas_call | solution.py:302
  98.9 8.7 %all_to_all.21.gathered = bf16[4,64,512]{2,1,0:T(8,128)(2,1)S(1)} all-to-all(bf16[4,64,512]{2,1,0:T(8,128)(2,1)S(1)} %shard_map.142), channel_id=1, replica_groups=mesh['half'=2,'ring'=4,'space'=32] {'ring'}, dimensions={0} | all-to-all | bytes 524288 | tf_op jit(solution)/shard_map/all_to_all | solution.py:313
  107.6 1.4 %shard_map.143 = (bf16[32,2,16,256]{3,2,1,0:T(8,128)(2,1)S(1)}, bf16[2,8,16,512]{3,2,1,0:T(8,128)(2,1)}) custom-call(bf16[4,64,512]{2,1,0:T(8,128)(2,1)S(1)} %all_to_all.21.gathered, bf16[2,2,8,16,512]{4,3,2,1,0:T(8,128)(2,1)S(1)} %copy-done.4, bf16[512,512]{1,0:T(8,128)(2,1)S(1)} %copy-done.1, bf16[512,512]{1,0:T(8,128)(2,1)S(1)} %copy-done), custom_call_target="tpu_custom_call" | custom-call | tf_op jit(solution)/shard_map/pallas_call | solution.py:302
  109.0 0.0 copy-start.3
  109.0 24.3 %all_to_all.22.received = bf16[32,2,16,256]{3,2,1,0:T(8,128)(2,1)S(1)} all-to-all(bf16[32,2,16,256]{3,2,1,0:T(8,128)(2,1)S(1)} %get-tuple-element.4), channel_id=1, replica_groups=mesh['half'=2,'ring'=4,'space'=32] {'space'}, dimensions={0} | all-to-all | bytes 1048576 | tf_op jit(solution)/shard_map/all_to_all | solution.py:313
  133.3 0.0 copy-done.3
  133.3 2.1 %shard_map.144 = bf16[2,2,8,16,512]{4,3,2,1,0:T(8,128)(2,1)} custom-call(bf16[32,2,16,256]{3,2,1,0:T(8,128)(2,1)S(1)} %all_to_all.22.received, bf16[2,2,8,16,512]{4,3,2,1,0:T(8,128)(2,1)S(1)} %copy-done.3, f32[8,16,1]{2,1,0:T(8,128)S(1)} %copy.34.keep, bf16[512,512]{1,0:T(8,128)(2,1)S(1)} %copy-done.1, bf16[512,512]{1,0:T(8,128)(2,1)S(1)} %copy-done), custom_call_target="tpu_custom_call" | custom-call | tf_op jit(solution)/shard_map/pallas_call | solution.py:302
  (14 shorter events, 0.2 us)
Async XLA Ops:
  0.6 0.7 copy-start.13
  1.7 8.3 %copy-start.11 = (bf16[64,2,3,3]{0,1,3,2:T(2,128)(2,1)S(1)}, bf16[64,2,3,3]{0,1,3,2:T(2,128)(2,1)}, u32[]{:S(2)}) copy-start(bf16[64,2,3,3]{0,1,3,2:T(2,128)(2,1)} %param.16) | copy-start | bytes 6916
  1.7 8.4 %copy-start.12 = (bf16[2,64,3,3]{1,0,3,2:T(2,128)(2,1)S(1)}, bf16[2,64,3,3]{1,0,3,2:T(2,128)(2,1)}, u32[]{:S(2)}) copy-start(bf16[2,64,3,3]{1,0,3,2:T(2,128)(2,1)} %param.17) | copy-start | bytes 6916
  1.7 12.2 %copy-start.1 = (bf16[512,512]{1,0:T(8,128)(2,1)S(1)}, bf16[512,512]{1,0:T(8,128)(2,1)}, u32[]{:S(2)}) copy-start(bf16[512,512]{1,0:T(8,128)(2,1)} %constant.39.clone.cos) | copy-start | bytes 1572868
  3.0 10.9 %copy-start = (bf16[512,512]{1,0:T(8,128)(2,1)S(1)}, bf16[512,512]{1,0:T(8,128)(2,1)}, u32[]{:S(2)}) copy-start(bf16[512,512]{1,0:T(8,128)(2,1)} %constant.40.clone.sin) | copy-start | bytes 1572868
  3.0 7.5 %collective-permute-start = (bf16[2,8,2,2,512]{4,3,1,2,0:T(2,128)(2,1)S(1)}, bf16[2,8,2,2,512]{4,3,1,2,0:T(2,128)(2,1)S(1)}, u32[]{:S(2)}, u32[]{:S(2)}) collective-permute-start(bf16[2,8,2,2,512]{4,3,1,2,0:T(2,128)(2,1)S(1)} %get-tuple-element.6), channel_id=1, source_target_pairs={{0,1},{1,2},{2,3},{3,4},{4,5},{5,6},{6,7},{7,8},{8,9},{9,10},{10,1... | collective-permute-start | bytes 196616 | tf_op jit(solution)/shard_map/ppermute | solution.py:342
  8.0 5.6 %collective-permute-start.1 = (bf16[2,8,2,2,512]{4,3,1,2,0:T(2,128)(2,1)S(1)}, bf16[2,8,2,2,512]{4,3,1,2,0:T(2,128)(2,1)S(1)}, u32[]{:S(2)}, u32[]{:S(2)}) collective-permute-start(bf16[2,8,2,2,512]{4,3,1,2,0:T(2,128)(2,1)S(1)} %get-tuple-element.7), channel_id=1, source_target_pairs={{1,0},{2,1},{3,2},{4,3},{5,4},{6,5},{7,6},{8,7},{9,8},{10,9},{11,1... | collective-permute-start | bytes 196616 | tf_op jit(solution)/shard_map/ppermute | solution.py:343
  13.8 0.9 copy-start.7
  14.7 1.0 copy-start.2
  15.8 0.9 copy-start.5
  31.9 26.0 %copy-start.4 = (bf16[2,2,8,16,512]{4,3,2,1,0:T(8,128)(2,1)S(1)}, bf16[2,2,8,16,512]{4,3,2,1,0:T(8,128)(2,1)}, u32[]{:S(2)}) copy-start(bf16[2,2,8,16,512]{4,3,2,1,0:T(8,128)(2,1)} %sens.3) | copy-start | bytes 1572868
  60.2 10.3 %all-to-all-start.1 = ((bf16[4,64,512]{2,1,0:T(8,128)(2,1)}), bf16[4,64,512]{2,1,0:T(8,128)(2,1)S(1)}, u32[]{:S(2)}, u32[]{:S(2)}) async-start(bf16[4,64,512]{2,1,0:T(8,128)(2,1)} %shard_map.141), calls=%async_computation.1 | async-start | bytes 524288 | tf_op jit(solution)/shard_map/all_to_all | solution.py:313
  64.3 0.7 copy-start.9
  70.5 23.5 %copy-start.10 = (bf16[64,2,3,3,3]{0,1,4,3,2:T(2,128)(2,1)S(1)}, bf16[64,2,3,3,3]{0,1,4,3,2:T(2,128)(2,1)}, u32[]{:S(2)}) copy-start(bf16[64,2,3,3,3]{0,1,4,3,2:T(2,128)(2,1)} %param.18) | copy-start | bytes 20740
  70.5 25.3 %copy-start.6 = (bf16[6,54,144]{2,1,0:T(8,128)(2,1)S(1)}, bf16[6,54,144]{2,1,0:T(8,128)(2,1)}, u32[]{:S(2)}) copy-start(bf16[6,54,144]{2,1,0:T(8,128)(2,1)} %constant.43.clone.band1) | copy-start | bytes 279940
  70.6 25.3 %copy-start.8 = (bf16[3,72,108]{2,1,0:T(8,128)(2,1)S(1)}, bf16[3,72,108]{2,1,0:T(8,128)(2,1)}, u32[]{:S(2)}) copy-start(bf16[3,72,108]{2,1,0:T(8,128)(2,1)} %constant.44.clone.band2) | copy-start | bytes 139972
  70.6 23.5 %collective-permute-start.6 = (bf16[32,512]{1,0:T(8,128)(2,1)S(1)}, bf16[32,512]{1,0:T(8,128)(2,1)S(1)}, u32[]{:S(2)}, u32[]{:S(2)}) collective-permute-start(bf16[32,512]{1,0:T(8,128)(2,1)S(1)} %get-tuple-element.8), channel_id=1, source_target_pairs={{32,128},{64,160},{96,192},{1,224},{33,129},{65,161},{97,193},{2,2... | collective-permute-start | bytes 98312 | tf_op jit(solution)/shard_map/ppermute | solution.py:399
  81.5 12.6 %collective-permute-start.5 = (bf16[32,512]{1,0:T(8,128)(2,1)S(1)}, bf16[32,512]{1,0:T(8,128)(2,1)S(1)}, u32[]{:S(2)}, u32[]{:S(2)}) collective-permute-start(bf16[32,512]{1,0:T(8,128)(2,1)S(1)} %get-tuple-element.8), channel_id=1, source_target_pairs={{32,0},{64,32},{96,64},{1,96},{33,1},{65,33},{97,65},{2,97},{34,2}... | collective-permute-start | bytes 98312 | tf_op jit(solution)/shard_map/ppermute | solution.py:399
  83.4 11.4 %collective-permute-start.4 = (bf16[32,512]{1,0:T(8,128)(2,1)S(1)}, bf16[32,512]{1,0:T(8,128)(2,1)S(1)}, u32[]{:S(2)}, u32[]{:S(2)}) collective-permute-start(bf16[32,512]{1,0:T(8,128)(2,1)S(1)} %get-tuple-element.9), channel_id=1, source_target_pairs={{0,160},{32,192},{64,224},{96,129},{1,161},{33,193},{65,225},{97,1... | collective-permute-start | bytes 98312 | tf_op jit(solution)/shard_map/ppermute | solution.py:399
  85.4 9.4 %collective-permute-start.3 = (bf16[32,512]{1,0:T(8,128)(2,1)S(1)}, bf16[32,512]{1,0:T(8,128)(2,1)S(1)}, u32[]{:S(2)}, u32[]{:S(2)}) collective-permute-start(bf16[32,512]{1,0:T(8,128)(2,1)S(1)} %get-tuple-element.9), channel_id=1, source_target_pairs={{0,32},{32,64},{64,96},{96,1},{1,33},{33,65},{65,97},{97,2},{2,34}... | collective-permute-start | bytes 98312 | tf_op jit(solution)/shard_map/ppermute | solution.py:399
  88.7 7.1 %collective-permute-start.2 = (bf16[64,512]{1,0:T(8,128)(2,1)S(1)}, bf16[64,512]{1,0:T(8,128)(2,1)S(1)}, u32[]{:S(2)}, u32[]{:S(2)}) collective-permute-start(bf16[64,512]{1,0:T(8,128)(2,1)S(1)} %reduce_sum.12.own), channel_id=1, source_target_pairs={{0,128},{32,160},{64,192},{96,224},{1,129},{33,161},{65,193},{97,2... | collective-permute-start | bytes 196616 | tf_op jit(solution)/shard_map/ppermute | solution.py:399
  109.0 24.3 %copy-start.3 = (bf16[2,2,8,16,512]{4,3,2,1,0:T(8,128)(2,1)S(1)}, bf16[2,2,8,16,512]{4,3,2,1,0:T(8,128)(2,1)}, u32[]{:S(2)}) copy-start(bf16[2,2,8,16,512]{4,3,2,1,0:T(8,128)(2,1)} %measured.3) | copy-start | bytes 1572868

commit v2 on v1

--- a/solution.py
+++ b/solution.py
@@ -20,6 +20,7 @@
 PAIRS = COILS * SLICES
 LANES = PAIRS * ROWS
 HROWS = ROWS + 2
+UNROLL = 2
 BF = jnp.bfloat16
 F32 = jnp.float32
 VMEM = pl.BlockSpec(memory_space=pltpu.VMEM)
@@ -147,9 +148,7 @@
                     ]
 
 
-def kspace_kernel(
-    edge, measured, halo, keep, first, second, band1, band2, cos, sin, out, w1, w2, x3, hidden, refined
-):
+def kspace_weights_kernel(edge, first, second, band1, band2, w1, w2):
     for r in range(HROWS):
         block = dot(first[...], band1[r])
         if r == 0:
@@ -160,7 +159,9 @@
     for pair in range(HROWS // 2):
         w2[:, pair * 128 : (pair + 1) * 128] = dot(band2[pair], second[...]).astype(BF)
 
-    def one(i, carry):
+
+def kspace_kernel(measured, halo, keep, w1, w2, cos, sin, out, refined, *scratch):
+    def one(i, x3, hidden):
         c, s = i // SLICES, i % SLICES
         mask = keep[s] > 0
         own = jnp.concatenate(
@@ -180,9 +181,13 @@
         row = pl.multiple_of(i * 16, 16)
         for h in range(2):
             refined[h, pl.ds(row, 16), :] = total[h * 16 : (h + 1) * 16]
+
+    def step(i, carry):
+        for k in range(UNROLL):
+            one(i * UNROLL + k, scratch[2 * k], scratch[2 * k + 1])
         return carry
 
-    lax.fori_loop(0, PAIRS, one, 0)
+    lax.fori_loop(0, PAIRS // UNROLL, step, 0)
     for part in range(2):
         rows = pl.ds(part * 256, 256)
         co, si = cos[rows, :], sin[rows, :]
@@ -217,7 +222,7 @@
 
 
 def image_kernel(
-    edge, own, other, before1, before2, after1, after2, first, second, band1, band2, out,
+    edge, previous, own, following, first, second, band1, band2, out,
     w1, w2, rows8, x3, acc, fin
 ):
     for x in range(6):
@@ -229,9 +234,8 @@
         w1[x * CH : (x + 1) * CH, :] = block.astype(BF)
     for pair in range(3):
         w2[:, pair * 128 : (pair + 1) * 128] = dot(band2[pair], second[...]).astype(BF)
-    for start, stop, a, b in ((0, 32, before1, before2), (32, 96, own, other), (96, 128, after1, after2)):
-        total = (a[...].astype(F32) + b[...].astype(F32)).astype(BF)
-        put(rows8, total.astype(F32), slice(start, stop))
+    for start, stop, source in ((0, 32, previous), (32, 96, own), (96, 128, following)):
+        put(rows8, source[...].astype(F32), slice(start, stop))
     x3[0:48] = jnp.zeros((48, N), BF)
     x3[432:480] = jnp.zeros((48, N), BF)
     for s in range(SLICES):
@@ -356,18 +360,20 @@
     zero = jnp.zeros_like(isecond)
     isecond = jnp.block([[isecond, zero], [zero, isecond]])
 
+    kw1, kw2 = call(
+        kspace_weights_kernel,
+        [arr(HROWS * CH, 128), arr(96, HROWS * CH)],
+        [],
+        1,
+        kedge, kfirst, ksecond, kband1, kband2,
+    )
     half_done = call(
         kspace_kernel,
         arr(SPACE, 2, ROWS, LANES),
-        [
-            pltpu.VMEM((HROWS * CH, 128), BF),
-            pltpu.VMEM((96, HROWS * CH), BF),
-            pltpu.VMEM((128, N), BF),
-            pltpu.VMEM((HROWS * CH, N), BF),
-            pltpu.VMEM((2, LANES, N), BF),
-        ],
-        1,
-        kedge, measured, halo, keep, kfirst, ksecond, kband1, kband2, cos, sin,
+        [pltpu.VMEM((2, LANES, N), BF)]
+        + [pltpu.VMEM((128, N), BF), pltpu.VMEM((HROWS * CH, N), BF)] * UNROLL,
+        0,
+        measured, halo, keep, kw1, kw2, cos, sin,
     )
     half_done = spread(half_done, "space")
     partial = call(
@@ -398,12 +404,10 @@
         ]
         return lax.ppermute(array, axes, pairs)
 
-    low, high = part[:32], part[32:]
-    before2 = moved(high, 1, 1)
-    after2 = moved(low, -1, 1)
     other = moved(part, 0, 1)
-    before1 = moved(high, 1, 0)
-    after1 = moved(low, -1, 0)
+    image_in = (part.astype(F32) + other.astype(F32)).astype(BF)
+    previous = moved(image_in[32:], 1, 0)
+    following = moved(image_in[:32], -1, 0)
     iedge = ends((space == 0) & (ring == 0), (space == SPACE - 1) & (ring == RING - 1))
     copies = call(
         image_kernel,
@@ -417,7 +421,7 @@
             pltpu.VMEM((4, SLICES * 8, 128), F32),
         ],
         1,
-        iedge, part, other, before1, before2, after1, after2, ifirst, isecond, iband1, iband2,
+        iedge, previous, image_in, following, ifirst, isecond, iband1, iband2,
     )
     gathered = spread(copies, "ring")
     midway, image_out = call(

time: 136 us -> 124 us (0.912)
  starting transfers between devices: 34.5 us -> 25.1 us
  Pallas kernels: 24.1 us -> 21.1 us
  waiting for transfers between devices: 10.2 us -> 11.8 us
    ppermute x5 -> x3, starting transfers between devices: 23.3 us -> 14.1 us  [moved(): return lax.ppermute(array, axes, pairs)]
    ppermute x5 -> x3, waiting for transfers between devices: 1.72 us -> 5.87 us  [moved(): return lax.ppermute(array, axes, pairs)]
    pallas_call x5 -> x6, Pallas kernels: 24.1 us -> 21.1 us  [call(): pl.pallas_call(kernel, out_shape=shapes, in_specs=[SMEM] * scalars + [VME...]
    ppermute x1, waiting for transfers between devices: 3.16 us -> 0.49 us  [local(): high = lax.ppermute(rim(0), 'space', down)]
    unnamed x30 -> x28, local copies, waits for them, and re-layouts: 4.24 us -> 3.27 us
  transfers between devices with their start and end apart: 8 -> 6, of which waited for: 4 -> 4; matrix products, arithmetic and copies ran while one was open for 1% -> 1% of each run, Pallas kernels for 0% -> 1%
where the time goes in v2:
time: 124 us; the launch traced here: 123 us
  blocking collectives  58.6 us (47%)
  starting transfers between devices  25.1 us (20%)
  Pallas kernels  21.1 us (17%)
  waiting for transfers between devices  11.8 us (10%)
  local copies, waits for them, and re-layouts  3.86 us (3%)
  other arithmetic  2.07 us (2%)
    all_to_all x3, blocking collectives, spread(): return lax.all_to_all(array, axis, split_axis=0, concat_axis=0, tiled=True)  58.6 us
    pallas_call x6, Pallas kernels, call(): pl.pallas_call(kernel, out_shape=shapes, in_specs=[SMEM] * scalars + [VME...  21.1 us
    ppermute x3, starting transfers between devices, moved(): return lax.ppermute(array, axes, pairs)  14.1 us
    ppermute x3, waiting for transfers between devices, moved(): return lax.ppermute(array, axes, pairs)  5.87 us
    all_to_all x1, waiting for transfers between devices, spread(): return lax.all_to_all(array, axis, split_axis=0, concat_axis=0, tiled=True)  5.39 us
    ppermute x1, starting transfers between devices, local(): low = lax.ppermute(rim(ROWS - 2), 'space', up)  4.92 us
    all_to_all x1, starting transfers between devices, spread(): return lax.all_to_all(array, axis, split_axis=0, concat_axis=0, tiled=True)  4.2 us
    unnamed x28, local copies, waits for them, and re-layouts  3.27 us
  transfers between devices with their start and end apart: 6, of which 4 were waited for; matrix products, arithmetic and copies ran while one was open for 1% of the time, Pallas kernels for 1%

profile of v2, /device:TPU:1, one launch (start us, length us, event | category | flops | bytes accessed | tf_op | source)
XLA Modules:
  0.0 123.4 jit_solution(1510863799068971537)
XLA Ops:
  0.6 0.0 copy-start.12
  0.7 0.7 copy-done.12
  1.3 0.0 copy-start.11
  1.3 0.3 compare_reduce_fusion
  1.6 0.0 copy-start.10
  1.6 0.1 fusion.9
  1.7 0.0 copy-start.2
  1.7 1.3 %fusion = (bf16[2,8,2,2,512]{4,3,1,2,0:T(2,128)(2,1)S(1)}, bf16[2,8,2,2,512]{4,3,1,2,0:T(2,128)(2,1)S(1)}) fusion(pred[8,2]{1,0:T(8,128)(4,1)S(1)} %get-tuple-element.14, bf16[2,2,8,16,512]{4,3,2,1,0:T(8,128)(2,1)} %measured.3, pred[8,2]{1,0:T(8,128)(4,1)S(1)} %get-tuple-element.15), kind=kLoop, calls=%fused_computation.4 | loop fusion | flops 65536 | bytes 262176 | tf_op jit(solution)/shard_map/transpose | solution.py:342
  3.0 4.9 %collective-permute-start = (bf16[2,8,2,2,512]{4,3,1,2,0:T(2,128)(2,1)S(1)}, bf16[2,8,2,2,512]{4,3,1,2,0:T(2,128)(2,1)S(1)}, u32[]{:S(2)}, u32[]{:S(2)}) collective-permute-start(bf16[2,8,2,2,512]{4,3,1,2,0:T(2,128)(2,1)S(1)} %get-tuple-element.10), channel_id=1, source_target_pairs={{0,1},{1,2},{2,3},{3,4},{4,5},{5,6},{6,7},{7,8},{8,9},{9,10},{10,1... | collective-permute-start | bytes 196616 | tf_op jit(solution)/shard_map/ppermute | solution.py:346
  7.9 1.9 %collective-permute-start.1 = (bf16[2,8,2,2,512]{4,3,1,2,0:T(2,128)(2,1)S(1)}, bf16[2,8,2,2,512]{4,3,1,2,0:T(2,128)(2,1)S(1)}, u32[]{:S(2)}, u32[]{:S(2)}) collective-permute-start(bf16[2,8,2,2,512]{4,3,1,2,0:T(2,128)(2,1)S(1)} %get-tuple-element.11), channel_id=1, source_target_pairs={{1,0},{2,1},{3,2},{4,3},{5,4},{6,5},{7,6},{8,7},{9,8},{10,9},{11,1... | collective-permute-start | bytes 196616 | tf_op jit(solution)/shard_map/ppermute | solution.py:347
  9.8 0.0 copy-done.10
  9.9 0.0 copy-done.11
  9.9 0.1 fusion.7.second
  10.0 0.1 copy.34.first
  10.1 0.1 copy.35.keep
  10.2 0.1 pad_maximum_fusion.2.edge
  10.3 0.0 copy-start.4
  10.3 0.9 copy-done.4
  11.3 0.0 copy-start.6
  11.3 0.9 copy-done.6
  12.2 0.0 copy-start
  12.2 0.0 copy-start.1
  12.2 0.8 shard_map.140
  13.0 0.0 collective-permute-done
  13.0 0.5 collective-permute-done.1
  13.5 0.1 pad_maximum_fusion
  13.7 0.0 copy-done.2
  13.7 0.0 copy-done
  13.7 0.0 copy-done.1
  13.8 11.5 %shard_map.141 = bf16[32,2,16,256]{3,2,1,0:T(8,128)(2,1)S(1)} custom-call(bf16[2,2,8,16,512]{4,3,2,1,0:T(8,128)(2,1)S(1)} %copy-done.2, bf16[16,8,512]{2,1,0:T(8,128)(2,1)S(1)} %reshape.35.halo, f32[8,16,1]{2,1,0:T(8,128)S(1)} %copy.35.keep, bf16[1152,128]{1,0:T(8,128)(2,1)S(1)} %get-tuple-element.6.w1, bf16[96,1152]{1,0:T(8,128)(2,1)S(1)} %get-tuple-element.7.w2, ...), custom_call_target="tpu_custom_call" | custom-call | tf_op jit(solution)/shard_map/pallas_call | solution.py:306
  25.3 0.0 copy-start.3
  25.3 25.9 %all_to_all.20.received = bf16[32,2,16,256]{3,2,1,0:T(8,128)(2,1)S(1)} all-to-all(bf16[32,2,16,256]{3,2,1,0:T(8,128)(2,1)S(1)} %shard_map.141), channel_id=1, replica_groups=mesh['half'=2,'ring'=4,'space'=32] {'space'}, dimensions={0} | all-to-all | bytes 1048576 | tf_op jit(solution)/shard_map/all_to_all | solution.py:317
  51.3 0.0 copy-done.3
  51.3 2.3 %shard_map.142 = bf16[4,64,512]{2,1,0:T(8,128)(2,1)} custom-call(bf16[32,2,16,256]{3,2,1,0:T(8,128)(2,1)S(1)} %all_to_all.20.received, bf16[2,2,8,16,512]{4,3,2,1,0:T(8,128)(2,1)S(1)} %copy-done.3, bf16[512,512]{1,0:T(8,128)(2,1)S(1)} %copy-done.1, bf16[512,512]{1,0:T(8,128)(2,1)S(1)} %copy-done), custom_call_target="tpu_custom_call" | custom-call | tf_op jit(solution)/shard_map/pallas_call | solution.py:306
  53.5 4.2 %all-to-all-start.1 = ((bf16[4,64,512]{2,1,0:T(8,128)(2,1)}), bf16[4,64,512]{2,1,0:T(8,128)(2,1)S(1)}, u32[]{:S(2)}, u32[]{:S(2)}) async-start(bf16[4,64,512]{2,1,0:T(8,128)(2,1)} %shard_map.142), calls=%async_computation.1 | async-start | bytes 524288 | tf_op jit(solution)/shard_map/all_to_all | solution.py:317
  57.7 0.0 copy-start.8
  57.7 0.7 copy-done.8
  58.5 5.4 %all-to-all-done.1 = bf16[4,64,512]{2,1,0:T(8,128)(2,1)S(1)} async-done(((bf16[4,64,512]{2,1,0:T(8,128)(2,1)}), bf16[4,64,512]{2,1,0:T(8,128)(2,1)S(1)}, u32[]{:S(2)}, u32[]{:S(2)}) %all-to-all-start.1) | async-done | bytes 262176 | tf_op jit(solution)/shard_map/all_to_all | solution.py:317
  63.9 7.0 %collective-permute-start.2 = (bf16[64,512]{1,0:T(8,128)(2,1)S(1)}, bf16[64,512]{1,0:T(8,128)(2,1)S(1)}, u32[]{:S(2)}, u32[]{:S(2)}) collective-permute-start(bf16[64,512]{1,0:T(8,128)(2,1)S(1)} %reduce_sum.12), channel_id=1, source_target_pairs={{0,128},{32,160},{64,192},{96,224},{1,129},{33,161},{65,193},{97,2... | collective-permute-start | bytes 196616 | tf_op jit(solution)/shard_map/ppermute | solution.py:405
  70.9 0.1 fusion.4.second
  71.0 0.0 copy-start.5
  71.0 1.6 %collective-permute-done.2 = bf16[64,512]{1,0:T(8,128)(2,1)S(1)} collective-permute-done((bf16[64,512]{1,0:T(8,128)(2,1)S(1)}, bf16[64,512]{1,0:T(8,128)(2,1)S(1)}, u32[]{:S(2)}, u32[]{:S(2)}) %collective-permute-start.2) | collective-permute-done | bytes 65568 | tf_op jit(solution)/shard_map/ppermute | solution.py:405
  72.6 0.0 copy-start.9
  72.6 0.0 copy-start.7
  72.6 5.2 %collective-permute-start.4 = (bf16[32,512]{1,0:T(8,128)(2,1)S(1)}, bf16[32,512]{1,0:T(8,128)(2,1)S(1)}, u32[]{:S(2)}, u32[]{:S(2)}) collective-permute-start(bf16[32,512]{1,0:T(8,128)(2,1)S(1)} %get-tuple-element.12), channel_id=1, source_target_pairs={{32,0},{64,32},{96,64},{1,96},{33,1},{65,33},{97,65},{2,97},{34,2}... | collective-permute-start | bytes 98312 | tf_op jit(solution)/shard_map/ppermute | solution.py:405
  77.8 1.9 %collective-permute-start.3 = (bf16[32,512]{1,0:T(8,128)(2,1)S(1)}, bf16[32,512]{1,0:T(8,128)(2,1)S(1)}, u32[]{:S(2)}, u32[]{:S(2)}) collective-permute-start(bf16[32,512]{1,0:T(8,128)(2,1)S(1)} %get-tuple-element.13), channel_id=1, source_target_pairs={{0,32},{32,64},{64,96},{96,1},{1,33},{33,65},{65,97},{97,2},{2,34}... | collective-permute-start | bytes 98312 | tf_op jit(solution)/shard_map/ppermute | solution.py:405
  79.7 0.1 pad_maximum_fusion.1.edge
  79.8 0.0 copy-done.9
  79.8 0.1 copy.38.first
  79.9 0.0 collective-permute-done.4.following
  79.9 4.3 %collective-permute-done.3.previous = bf16[32,512]{1,0:T(8,128)(2,1)S(1)} collective-permute-done((bf16[32,512]{1,0:T(8,128)(2,1)S(1)}, bf16[32,512]{1,0:T(8,128)(2,1)S(1)}, u32[]{:S(2)}, u32[]{:S(2)}) %collective-permute-start.3) | collective-permute-done | bytes 32800 | tf_op jit(solution)/shard_map/ppermute | solution.py:405
  84.2 0.0 copy-done.5
  84.2 0.0 copy-done.7
  84.2 3.0 %shard_map.143 = bf16[4,64,512]{2,1,0:T(8,128)(2,1)S(1)} custom-call(f32[2]{0:T(128)S(1)} %pad_maximum_fusion.1.edge, bf16[32,512]{1,0:T(8,128)(2,1)S(1)} %collective-permute-done.3.previous, bf16[64,512]{1,0:T(8,128)(2,1)S(1)} %add_convert_fusion.own, bf16[32,512]{1,0:T(8,128)(2,1)S(1)} %collective-permute-done.4.following, bf16[64,54]{1,0:T(8,128)(2,1)S(1)} %copy.38.first, ...), custom_call_target="tpu_custom_call" | custom-call | tf_op jit(solution)/shard_map/pallas_call | solution.py:306
  87.2 8.9 %all_to_all.21.gathered = bf16[4,64,512]{2,1,0:T(8,128)(2,1)S(1)} all-to-all(bf16[4,64,512]{2,1,0:T(8,128)(2,1)S(1)} %shard_map.143), channel_id=1, replica_groups=mesh['half'=2,'ring'=4,'space'=32] {'ring'}, dimensions={0} | all-to-all | bytes 524288 | tf_op jit(solution)/shard_map/all_to_all | solution.py:317
  96.1 1.4 %shard_map.144 = (bf16[32,2,16,256]{3,2,1,0:T(8,128)(2,1)S(1)}, bf16[2,8,16,512]{3,2,1,0:T(8,128)(2,1)}) custom-call(bf16[4,64,512]{2,1,0:T(8,128)(2,1)S(1)} %all_to_all.21.gathered, bf16[2,2,8,16,512]{4,3,2,1,0:T(8,128)(2,1)S(1)} %copy-done.3, bf16[512,512]{1,0:T(8,128)(2,1)S(1)} %copy-done.1, bf16[512,512]{1,0:T(8,128)(2,1)S(1)} %copy-done), custom_call_target="tpu_custom_call" | custom-call | tf_op jit(solution)/shard_map/pallas_call | solution.py:306
  97.6 23.7 %all_to_all.22.received = bf16[32,2,16,256]{3,2,1,0:T(8,128)(2,1)S(1)} all-to-all(bf16[32,2,16,256]{3,2,1,0:T(8,128)(2,1)S(1)} %get-tuple-element.8), channel_id=1, replica_groups=mesh['half'=2,'ring'=4,'space'=32] {'space'}, dimensions={0} | all-to-all | bytes 1048576 | tf_op jit(solution)/shard_map/all_to_all | solution.py:317
  121.3 2.1 %shard_map.145 = bf16[2,2,8,16,512]{4,3,2,1,0:T(8,128)(2,1)} custom-call(bf16[32,2,16,256]{3,2,1,0:T(8,128)(2,1)S(1)} %all_to_all.22.received, bf16[2,2,8,16,512]{4,3,2,1,0:T(8,128)(2,1)S(1)} %copy-done.2, f32[8,16,1]{2,1,0:T(8,128)S(1)} %copy.35.keep, bf16[512,512]{1,0:T(8,128)(2,1)S(1)} %copy-done.1, bf16[512,512]{1,0:T(8,128)(2,1)S(1)} %copy-done), custom_call_target="tpu_custom_call" | custom-call | tf_op jit(solution)/shard_map/pallas_call | solution.py:306
  (15 shorter events, 0.3 us)
Async XLA Ops:
  0.6 0.7 copy-start.12
  1.3 8.6 %copy-start.11 = (bf16[2,64,3,3]{1,0,3,2:T(2,128)(2,1)S(1)}, bf16[2,64,3,3]{1,0,3,2:T(2,128)(2,1)}, u32[]{:S(2)}) copy-start(bf16[2,64,3,3]{1,0,3,2:T(2,128)(2,1)} %param.17) | copy-start | bytes 6916
  1.6 8.2 %copy-start.10 = (bf16[64,2,3,3]{0,1,3,2:T(2,128)(2,1)S(1)}, bf16[64,2,3,3]{0,1,3,2:T(2,128)(2,1)}, u32[]{:S(2)}) copy-start(bf16[64,2,3,3]{0,1,3,2:T(2,128)(2,1)} %param.16) | copy-start | bytes 6916
  1.7 12.0 %copy-start.2 = (bf16[2,2,8,16,512]{4,3,2,1,0:T(8,128)(2,1)S(1)}, bf16[2,2,8,16,512]{4,3,2,1,0:T(8,128)(2,1)}, u32[]{:S(2)}) copy-start(bf16[2,2,8,16,512]{4,3,2,1,0:T(8,128)(2,1)} %measured.3) | copy-start | bytes 1572868
  3.0 10.0 %collective-permute-start = (bf16[2,8,2,2,512]{4,3,1,2,0:T(2,128)(2,1)S(1)}, bf16[2,8,2,2,512]{4,3,1,2,0:T(2,128)(2,1)S(1)}, u32[]{:S(2)}, u32[]{:S(2)}) collective-permute-start(bf16[2,8,2,2,512]{4,3,1,2,0:T(2,128)(2,1)S(1)} %get-tuple-element.10), channel_id=1, source_target_pairs={{0,1},{1,2},{2,3},{3,4},{4,5},{5,6},{6,7},{7,8},{8,9},{9,10},{10,1... | collective-permute-start | bytes 196616 | tf_op jit(solution)/shard_map/ppermute | solution.py:346
  7.9 5.6 %collective-permute-start.1 = (bf16[2,8,2,2,512]{4,3,1,2,0:T(2,128)(2,1)S(1)}, bf16[2,8,2,2,512]{4,3,1,2,0:T(2,128)(2,1)S(1)}, u32[]{:S(2)}, u32[]{:S(2)}) collective-permute-start(bf16[2,8,2,2,512]{4,3,1,2,0:T(2,128)(2,1)S(1)} %get-tuple-element.11), channel_id=1, source_target_pairs={{1,0},{2,1},{3,2},{4,3},{5,4},{6,5},{7,6},{8,7},{9,8},{10,9},{11,1... | collective-permute-start | bytes 196616 | tf_op jit(solution)/shard_map/ppermute | solution.py:347
  10.3 0.9 copy-start.4
  11.3 0.9 copy-start.6
  12.2 1.6 %copy-start = (bf16[512,512]{1,0:T(8,128)(2,1)S(1)}, bf16[512,512]{1,0:T(8,128)(2,1)}, u32[]{:S(2)}) copy-start(bf16[512,512]{1,0:T(8,128)(2,1)} %constant.40.clone.sin) | copy-start | bytes 1572868
  12.2 1.6 %copy-start.1 = (bf16[512,512]{1,0:T(8,128)(2,1)S(1)}, bf16[512,512]{1,0:T(8,128)(2,1)}, u32[]{:S(2)}) copy-start(bf16[512,512]{1,0:T(8,128)(2,1)} %constant.39.clone.cos) | copy-start | bytes 1572868
  25.3 26.0 %copy-start.3 = (bf16[2,2,8,16,512]{4,3,2,1,0:T(8,128)(2,1)S(1)}, bf16[2,2,8,16,512]{4,3,2,1,0:T(8,128)(2,1)}, u32[]{:S(2)}) copy-start(bf16[2,2,8,16,512]{4,3,2,1,0:T(8,128)(2,1)} %sens.3) | copy-start | bytes 1572868
  53.5 10.3 %all-to-all-start.1 = ((bf16[4,64,512]{2,1,0:T(8,128)(2,1)}), bf16[4,64,512]{2,1,0:T(8,128)(2,1)S(1)}, u32[]{:S(2)}, u32[]{:S(2)}) async-start(bf16[4,64,512]{2,1,0:T(8,128)(2,1)} %shard_map.142), calls=%async_computation.1 | async-start | bytes 524288 | tf_op jit(solution)/shard_map/all_to_all | solution.py:317
  57.7 0.7 copy-start.8
  63.9 8.6 %collective-permute-start.2 = (bf16[64,512]{1,0:T(8,128)(2,1)S(1)}, bf16[64,512]{1,0:T(8,128)(2,1)S(1)}, u32[]{:S(2)}, u32[]{:S(2)}) collective-permute-start(bf16[64,512]{1,0:T(8,128)(2,1)S(1)} %reduce_sum.12), channel_id=1, source_target_pairs={{0,128},{32,160},{64,192},{96,224},{1,129},{33,161},{65,193},{97,2... | collective-permute-start | bytes 196616 | tf_op jit(solution)/shard_map/ppermute | solution.py:405
  71.0 13.3 %copy-start.5 = (bf16[6,54,144]{2,1,0:T(8,128)(2,1)S(1)}, bf16[6,54,144]{2,1,0:T(8,128)(2,1)}, u32[]{:S(2)}) copy-start(bf16[6,54,144]{2,1,0:T(8,128)(2,1)} %constant.43.clone.band1) | copy-start | bytes 279940
  72.6 7.2 %copy-start.9 = (bf16[64,2,3,3,3]{0,1,4,3,2:T(2,128)(2,1)S(1)}, bf16[64,2,3,3,3]{0,1,4,3,2:T(2,128)(2,1)}, u32[]{:S(2)}) copy-start(bf16[64,2,3,3,3]{0,1,4,3,2:T(2,128)(2,1)} %param.18) | copy-start | bytes 20740
  72.6 11.6 %copy-start.7 = (bf16[3,72,108]{2,1,0:T(8,128)(2,1)S(1)}, bf16[3,72,108]{2,1,0:T(8,128)(2,1)}, u32[]{:S(2)}) copy-start(bf16[3,72,108]{2,1,0:T(8,128)(2,1)} %constant.44.clone.band2) | copy-start | bytes 139972
  72.6 7.3 %collective-permute-start.4 = (bf16[32,512]{1,0:T(8,128)(2,1)S(1)}, bf16[32,512]{1,0:T(8,128)(2,1)S(1)}, u32[]{:S(2)}, u32[]{:S(2)}) collective-permute-start(bf16[32,512]{1,0:T(8,128)(2,1)S(1)} %get-tuple-element.12), channel_id=1, source_target_pairs={{32,0},{64,32},{96,64},{1,96},{33,1},{65,33},{97,65},{2,97},{34,2}... | collective-permute-start | bytes 98312 | tf_op jit(solution)/shard_map/ppermute | solution.py:405
  77.8 6.4 %collective-permute-start.3 = (bf16[32,512]{1,0:T(8,128)(2,1)S(1)}, bf16[32,512]{1,0:T(8,128)(2,1)S(1)}, u32[]{:S(2)}, u32[]{:S(2)}) collective-permute-start(bf16[32,512]{1,0:T(8,128)(2,1)S(1)} %get-tuple-element.13), channel_id=1, source_target_pairs={{0,32},{32,64},{64,96},{96,1},{1,33},{33,65},{65,97},{97,2},{2,34}... | collective-permute-start | bytes 98312 | tf_op jit(solution)/shard_map/ppermute | solution.py:405

commit v3 on v2

--- a/solution.py
+++ b/solution.py
@@ -20,7 +20,7 @@
 PAIRS = COILS * SLICES
 LANES = PAIRS * ROWS
 HROWS = ROWS + 2
-UNROLL = 2
+UNROLL = 4
 BF = jnp.bfloat16
 F32 = jnp.float32
 VMEM = pl.BlockSpec(memory_space=pltpu.VMEM)
@@ -34,32 +34,53 @@
         2.0 * math.pi / N
     )
     factor = np.float32(1.0 / math.sqrt(N))
-    return (np.cos(angles) * factor).astype(BF), (np.sin(angles) * factor).astype(BF)
-
-
-def kspace_bands():
-    first = np.zeros((HROWS, 18, 128), np.float32)
+    cos, sin = (np.cos(angles) * factor).astype(BF), (np.sin(angles) * factor).astype(BF)
+    late = (position + np.where(position % ROWS < 2, ROWS, 0)) % N
+    return cos, sin, cos[late], sin[late]
+
+
+def iota(shape, dim):
+    return lax.broadcasted_iota(jnp.int32, shape, dim)
+
+
+def split(v, size, count):
+    quotient = sum((v >= size * n).astype(jnp.int32) for n in range(1, count))
+    return quotient, v - quotient * size
+
+
+def kspace_weights(edge, first, second, w1, w2):
+    h_row, rest = split(iota((18, 128), 0), 9, 2)
+    p_row, q_row = split(rest, 3, 3)
+    lane = iota((18, 128), 1)
+    late = lane >= 96
+    rest = jnp.where(late, lane - 96, lane)
+    q_lane = jnp.where(late, rest >> 3, rest >> 5)
+    h_lane = jnp.where(late, (rest >> 2) & 1, (rest >> 4) & 1)
+    row = jnp.where(late, ROWS + (rest & 3), rest & 15)
+    hidden_row = jnp.where((h_row == h_lane) & (q_row == q_lane), row - p_row, -1)
+    late = iota((CH, 128), 1) >= 96
     for r in range(HROWS):
-        for h in range(2):
-            for p in range(3):
-                for q in range(3):
-                    row = r + p
-                    if 2 <= row < 18:
-                        column = q * 32 + h * 16 + row - 2
-                    else:
-                        e = row if row < 2 else row - 16
-                        column = 96 + q * 8 + h * 4 + e
-                    first[r, h * 9 + p * 3 + q, column] = 1
-    second = np.zeros((HROWS // 2, 96, 36), np.float32)
+        band = jnp.where(hidden_row == r, 1.0, 0.0).astype(BF)
+        block = dot(first[...], band)
+        across = ~late if r + 1 >= ROWS else late
+        block = jnp.where(across, block * edge[1], block)
+        w1[r * CH : (r + 1) * CH, :] = block.astype(BF)
+    line, lane = iota((96, 36), 0), iota((96, 36), 1)
+    parity, rest = split(lane, 18, 2)
+    q_lane, rest = split(rest, 6, 3)
+    o_lane, p_lane = split(rest, 3, 2)
+    place = line & 15
+    place = jnp.where(place < 2, place + ROWS, place)
+    match = (line >> 5 == q_lane) & ((line >> 4) & 1 == o_lane)
+    pair_row = jnp.where(match, place + p_lane - 2 - parity, -1)
+    late = (iota((96, 128), 0) & 15) < 2
+    upper = iota((96, 128), 1) >= CH
     for pair in range(HROWS // 2):
-        for parity in range(2):
-            for q in range(3):
-                for o in range(2):
-                    for r in range(ROWS):
-                        p = 2 * pair + parity - r
-                        if 0 <= p < 3:
-                            second[pair, q * 32 + o * 16 + r, parity * 18 + q * 6 + o * 3 + p] = 1
-    return first.astype(BF), second.astype(BF)
+        band = jnp.where(pair_row == 2 * pair, 1.0, 0.0).astype(BF)
+        block = dot(band, second[...])
+        beyond = 2 * pair + 1 + upper.astype(jnp.int32) >= ROWS
+        block = jnp.where(late != beyond, block * edge[1], block)
+        w2[:, pair * 128 : (pair + 1) * 128] = block.astype(BF)
 
 
 def image_bands():
@@ -148,26 +169,24 @@
                     ]
 
 
-def kspace_weights_kernel(edge, first, second, band1, band2, w1, w2):
-    for r in range(HROWS):
-        block = dot(first[...], band1[r])
-        if r == 0:
-            block = block * edge[0]
-        if r == HROWS - 1:
-            block = block * edge[1]
-        w1[r * CH : (r + 1) * CH, :] = block.astype(BF)
-    for pair in range(HROWS // 2):
-        w2[:, pair * 128 : (pair + 1) * 128] = dot(band2[pair], second[...]).astype(BF)
-
-
-def kspace_kernel(measured, halo, keep, w1, w2, cos, sin, out, refined, *scratch):
+def kspace_kernel(measured, halo, keep, follow, w1, w2, cos, sin, out, refined, *scratch):
     def one(i, x3, hidden):
         c, s = i // SLICES, i % SLICES
         mask = keep[s] > 0
         own = jnp.concatenate(
             [jnp.where(mask, measured[c, h, s].astype(F32), 0.0) for h in range(2)], axis=0
         )
-        rim = halo[i].astype(F32)
+        rim = jnp.where(follow[s] > 0, halo[i].astype(F32)[0:8], 0.0)
+        two = iota((8, N), 0) < 2
+        held = jnp.concatenate(
+            [
+                jnp.where(two, rim, own[0:8]),
+                own[8:16],
+                jnp.where(two, pltpu.roll(rim, 4, 0), own[16:24]),
+                own[24:32],
+            ],
+            axis=0,
+        )
         x3[0:32] = before(own).astype(BF)
         x3[32:64] = own.astype(BF)
         x3[64:96] = after(own).astype(BF)
@@ -176,7 +195,7 @@
         ).astype(BF)
         hidden[...] = jnp.maximum(dot(w1[...], x3[...]).astype(BF), 0)
         spread = dot(w2[...], hidden[...])
-        total = own + before(spread[0:32]) + spread[32:64] + after(spread[64:96])
+        total = held + before(spread[0:32]) + spread[32:64] + after(spread[64:96])
         total = total.astype(BF)
         row = pl.multiple_of(i * 16, 16)
         for h in range(2):
@@ -197,7 +216,7 @@
         out[part * 16 : (part + 1) * 16, 1] = imag.astype(BF).reshape(16, 16, LANES)
 
 
-def combine_kernel(received, sens, cos, sin, out, left, image, partial):
+def combine_kernel(received, sens, halo, cos, sin, out, left, image, partial):
     regroup(received, left)
     for c in range(COILS):
         rows = slice(c * 128, (c + 1) * 128)
@@ -206,7 +225,13 @@
         for s in range(SLICES):
             rows = slice(s * 16, (s + 1) * 16)
             real, imag = image[0, rows], image[1, rows]
-            sr, si = sens[c, 0, s].astype(F32), sens[c, 1, s].astype(F32)
+            extra = halo[c * SLICES + s].astype(F32)
+            sr, si = (
+                jnp.concatenate(
+                    [extra[8 + 2 * h : 10 + 2 * h], sens[c, h, s].astype(F32)[2:]], axis=0
+                )
+                for h in range(2)
+            )
             pr = sr * real + si * imag
             pi = sr * imag - si * real
             if c:
@@ -215,14 +240,15 @@
             put(partial, pr, 0, rows)
             put(partial, pi, 1, rows)
     for x in range(ROWS):
+        place = (x + 2) % ROWS
         both = jnp.concatenate(
-            [wide(partial, h, pl.ds(x, 8, stride=16)) for h in range(2)], axis=0
+            [wide(partial, h, pl.ds(place, 8, stride=16)) for h in range(2)], axis=0
         )
         out[x // 4, x % 4 * 16 : (x % 4 + 1) * 16] = both.astype(BF)
 
 
 def image_kernel(
-    edge, previous, own, following, first, second, band1, band2, out,
+    edge, previous, own, first, second, band1, band2, out,
     w1, w2, rows8, x3, acc, fin
 ):
     for x in range(6):
@@ -234,8 +260,10 @@
         w1[x * CH : (x + 1) * CH, :] = block.astype(BF)
     for pair in range(3):
         w2[:, pair * 128 : (pair + 1) * 128] = dot(band2[pair], second[...]).astype(BF)
-    for start, stop, source in ((0, 32, previous), (32, 96, own), (96, 128, following)):
-        put(rows8, source[...].astype(F32), slice(start, stop))
+    put(rows8, previous[0:32].astype(F32) * edge[0], slice(0, 32))
+    put(rows8, previous[32:64].astype(F32), slice(32, 64))
+    put(rows8, own[0:32].astype(F32), slice(64, 96))
+    put(rows8, own[32:64].astype(F32) * edge[1], slice(96, 128))
     x3[0:48] = jnp.zeros((48, N), BF)
     x3[432:480] = jnp.zeros((48, N), BF)
     for s in range(SLICES):
@@ -325,27 +353,22 @@
     measured, sensitivity, sample_lines, kspace_first, kspace_second, image_first, image_second
 ):
     space, ring = lax.axis_index("space"), lax.axis_index("ring")
-    cos, sin = (jnp.asarray(t) for t in dft_tables())
-    kband1, kband2 = (jnp.asarray(t) for t in kspace_bands())
+    cos, sin, lcos, lsin = (jnp.asarray(t) for t in dft_tables())
     iband1, iband2 = (jnp.asarray(t) for t in image_bands())
 
-    rows = space * ROWS + jnp.arange(ROWS, dtype=jnp.int32)
-    sampled = jnp.any(sample_lines[:, :, None] == rows[None, None, :], axis=1)
-    keep = sampled.astype(F32)[:, :, None]
-
-    def rim(start):
-        part = jnp.where(
-            sampled[None, None, :, start : start + 2, None],
-            measured[:, :, :, start : start + 2, :],
-            jnp.zeros((), BF),
-        )
-        return part.transpose(0, 2, 1, 3, 4)
-
-    up = [(i, i + 1) for i in range(SPACE - 1)]
-    down = [(i + 1, i) for i in range(SPACE - 1)]
-    low = lax.ppermute(rim(ROWS - 2), "space", up)
-    high = lax.ppermute(rim(0), "space", down)
-    halo = jnp.concatenate([low, high], axis=3).reshape(PAIRS, 8, N)
+    rim = jnp.concatenate(
+        [
+            measured[:, :, :, :4].transpose(0, 2, 1, 3, 4).reshape(PAIRS, 8, N),
+            sensitivity[:, :, :, :2].transpose(0, 2, 1, 3, 4).reshape(PAIRS, 4, N),
+        ],
+        axis=1,
+    )
+    halo = lax.ppermute(rim, "space", [((i + 1) % SPACE, i) for i in range(SPACE)])
+
+    rows = (space * ROWS + jnp.arange(ROWS + 4, dtype=jnp.int32)) % N
+    sampled = jnp.any(sample_lines[:, :, None] == rows[None, None, :], axis=1).astype(F32)
+    keep = sampled[:, :ROWS, None]
+    follow = jnp.tile(sampled[:, ROWS:], (1, 2))[:, :, None]
 
     def ends(first, last):
         return jnp.stack([1 - first.astype(F32), 1 - last.astype(F32)])
@@ -361,11 +384,11 @@
     isecond = jnp.block([[isecond, zero], [zero, isecond]])
 
     kw1, kw2 = call(
-        kspace_weights_kernel,
+        kspace_weights,
         [arr(HROWS * CH, 128), arr(96, HROWS * CH)],
         [],
         1,
-        kedge, kfirst, ksecond, kband1, kband2,
+        kedge, kfirst, ksecond,
     )
     half_done = call(
         kspace_kernel,
@@ -373,7 +396,7 @@
         [pltpu.VMEM((2, LANES, N), BF)]
         + [pltpu.VMEM((128, N), BF), pltpu.VMEM((HROWS * CH, N), BF)] * UNROLL,
         0,
-        measured, halo, keep, kw1, kw2, cos, sin,
+        measured, halo, keep, follow, kw1, kw2, lcos, lsin,
     )
     half_done = spread(half_done, "space")
     partial = call(
@@ -385,7 +408,7 @@
             pltpu.VMEM((2, 4, 128, 128), F32),
         ],
         0,
-        half_done, sensitivity, cos, sin,
+        half_done, sensitivity, halo, lcos, lsin,
     )
     part = spread(partial, "ring").astype(F32).sum(axis=0).astype(BF)
 
@@ -397,17 +420,15 @@
 
     def moved(array, step, flip):
         pairs = [
-            (place(half, i), place(half ^ flip, i + step))
+            (place(half, i), place(half ^ flip, (i + step) % count))
             for half in range(HALVES)
             for i in range(count)
-            if 0 <= i + step < count
         ]
         return lax.ppermute(array, axes, pairs)
 
     other = moved(part, 0, 1)
     image_in = (part.astype(F32) + other.astype(F32)).astype(BF)
-    previous = moved(image_in[32:], 1, 0)
-    following = moved(image_in[:32], -1, 0)
+    previous = moved(image_in, 1, 0)
     iedge = ends((space == 0) & (ring == 0), (space == SPACE - 1) & (ring == RING - 1))
     copies = call(
         image_kernel,
@@ -421,7 +442,7 @@
             pltpu.VMEM((4, SLICES * 8, 128), F32),
         ],
         1,
-        iedge, previous, image_in, following, ifirst, isecond, iband1, iband2,
+        iedge, previous, image_in, ifirst, isecond, iband1, iband2,
     )
     gathered = spread(copies, "ring")
     midway, image_out = call(

time: 124 us -> 117 us (0.944)
  starting transfers between devices: 25.1 us -> 12.1 us
  blocking collectives: 58.6 us -> 64.1 us
  waiting for transfers between devices: 11.8 us -> 13.9 us
  Pallas kernels: 21.1 us -> 19.7 us
    ppermute x3 -> x2, starting transfers between devices: 14.1 us -> 4.67 us  [moved(): return lax.ppermute(array, axes, pairs)]
    all_to_all x3, blocking collectives: 58.6 us -> 64.1 us  [spread(): return lax.all_to_all(array, axis, split_axis=0, concat_axis=0, tiled=True)]
    ppermute x2 -> x1, starting transfers between devices: 6.84 us -> 3.28 us  [local(): lax.ppermute(rim, 'space', [((i + 1) % SPACE, i) for i in range(SPACE)])]
    transpose x0 -> x4, local copies, waits for them, and re-layouts: none -> 2.12 us  [the longest x2 1.09 us: local(): measured[:, :, :, :4].transpose(0, 2, 1, 3, 4).reshape(PAIRS, 8, N)]
    ppermute x3 -> x2, waiting for transfers between devices: 5.87 us -> 7.97 us  [moved(): return lax.ppermute(array, axes, pairs)]
    pallas_call x6, Pallas kernels: 21.1 us -> 19.7 us  [call(): pl.pallas_call(kernel, out_shape=shapes, in_specs=[SMEM] * scalars + [VME...]
    unnamed x28, local copies, waits for them, and re-layouts: 3.27 us -> 1.96 us
    transpose x1 -> x0, other arithmetic: 1.27 us -> none  [rim(): return part.transpose(0, 2, 1, 3, 4)]
  transfers between devices with their start and end apart: 6 -> 4, of which waited for: 4 -> 4; matrix products, arithmetic and copies ran while one was open for 1% -> 1% of each run, Pallas kernels for 1% -> 1%
where the time goes in v3:
time: 117 us; the launch traced here: 116 us
  blocking collectives  64.1 us (55%)
  Pallas kernels  19.7 us (17%)
  waiting for transfers between devices  13.9 us (12%)
  starting transfers between devices  12.1 us (10%)
  local copies, waits for them, and re-layouts  4.78 us (4%)
    all_to_all x3, blocking collectives, spread(): return lax.all_to_all(array, axis, split_axis=0, concat_axis=0, tiled=True)  64.1 us
    pallas_call x6, Pallas kernels, call(): pl.pallas_call(kernel, out_shape=shapes, in_specs=[SMEM] * scalars + [VME...  19.7 us
    ppermute x2, waiting for transfers between devices, moved(): return lax.ppermute(array, axes, pairs)  7.97 us
    ppermute x2, starting transfers between devices, moved(): return lax.ppermute(array, axes, pairs)  4.67 us
    all_to_all x1, waiting for transfers between devices, spread(): return lax.all_to_all(array, axis, split_axis=0, concat_axis=0, tiled=True)  4.62 us
    all_to_all x1, starting transfers between devices, spread(): return lax.all_to_all(array, axis, split_axis=0, concat_axis=0, tiled=True)  4.19 us
    ppermute x1, starting transfers between devices, local(): lax.ppermute(rim, 'space', [((i + 1) % SPACE, i) for i in range(SPACE)])  3.28 us
  transfers between devices with their start and end apart: 4, of which 4 were waited for; matrix products, arithmetic and copies ran while one was open for 1% of the time, Pallas kernels for 1%

profile of v3, /device:TPU:1, one launch (start us, length us, event | category | flops | bytes accessed | tf_op | source)
XLA Modules:
  0.0 116.4 jit_solution(7050892975003119015)
XLA Ops:
  0.6 1.0 slice_bitcast_fusion.1
  1.7 0.0 copy-start.5
  1.7 1.0 slice_bitcast_fusion
  2.8 0.0 copy-start.12
  2.8 0.0 copy-start.10
  2.8 0.0 copy-start.4
  2.9 0.0 copy-start
  3.0 3.3 %collective-permute-start = (bf16[16,12,512]{2,1,0:T(8,128)(2,1)S(1)}, bf16[16,12,512]{2,1,0:T(8,128)(2,1)S(1)}, u32[]{:S(2)}, u32[]{:S(2)}) collective-permute-start(bf16[16,12,512]{2,1,0:T(8,128)(2,1)S(1)} %pad_maximum_fusion), channel_id=1, source_target_pairs={{1,0},{2,1},{3,2},{4,3},{5,4},{6,5},{7,6},{8,7},{9,8},{10,9},{11,1... | collective-permute-start | bytes 589832 | tf_op jit(solution)/shard_map/ppermute | solution.py:366
  6.2 0.0 copy-done.12
  6.2 0.5 compare_reduce_fusion
  6.8 0.2 copy.43.keep
  7.0 0.1 copy.44.follow
  7.1 0.0 copy-done.10
  7.1 0.0 copy-start.11
  7.1 0.1 copy.42.first
  7.2 0.6 copy-done.11
  7.8 0.1 pad_maximum_fusion.2.edge
  7.9 0.1 fusion.5.second
  8.0 0.8 shard_map.140
  8.8 1.3 %collective-permute-done.halo = bf16[16,12,512]{2,1,0:T(8,128)(2,1)S(1)} collective-permute-done((bf16[16,12,512]{2,1,0:T(8,128)(2,1)S(1)}, bf16[16,12,512]{2,1,0:T(8,128)(2,1)S(1)}, u32[]{:S(2)}, u32[]{:S(2)}) %collective-permute-start) | collective-permute-done | bytes 196640 | tf_op jit(solution)/shard_map/ppermute | solution.py:366
  10.1 0.0 copy-done.5
  10.1 0.0 copy-done.4
  10.1 0.0 copy-done
  10.1 10.2 %shard_map.141 = bf16[32,2,16,256]{3,2,1,0:T(8,128)(2,1)S(1)} custom-call(bf16[2,2,8,16,512]{4,3,2,1,0:T(8,128)(2,1)S(1)} %copy-done, bf16[16,12,512]{2,1,0:T(8,128)(2,1)S(1)} %collective-permute-done.halo, f32[8,16,1]{2,1,0:T(8,128)S(1)} %copy.43.keep, f32[8,8,1]{2,1,0:T(8,128)S(1)} %copy.44.follow, bf16[1152,128]{1,0:T(8,128)(2,1)S(1)} %get-tuple-element.6.w1, ...), custom_call_target="tpu_custom_call" | custom-call | tf_op jit(solution)/shard_map/pallas_call | solution.py:334
  20.3 0.0 copy-start.1
  20.3 28.5 %all_to_all.20.received = bf16[32,2,16,256]{3,2,1,0:T(8,128)(2,1)S(1)} all-to-all(bf16[32,2,16,256]{3,2,1,0:T(8,128)(2,1)S(1)} %shard_map.141), channel_id=1, replica_groups=mesh['half'=2,'ring'=4,'space'=32] {'space'}, dimensions={0} | all-to-all | bytes 1048576 | tf_op jit(solution)/shard_map/all_to_all | solution.py:345
  48.8 0.0 copy-done.1
  48.8 2.3 %shard_map.142 = bf16[4,64,512]{2,1,0:T(8,128)(2,1)} custom-call(bf16[32,2,16,256]{3,2,1,0:T(8,128)(2,1)S(1)} %all_to_all.20.received, bf16[2,2,8,16,512]{4,3,2,1,0:T(8,128)(2,1)S(1)} %copy-done.1, bf16[16,12,512]{2,1,0:T(8,128)(2,1)S(1)} %collective-permute-done.halo, bf16[512,512]{1,0:T(8,128)(2,1)S(1)} %copy-done.4, bf16[512,512]{1,0:T(8,128)(2,1)S(1)} %copy-done.5), custom_call_target="tpu_custom_call" | custom-call | tf_op jit(solution)/shard_map/pallas_call | solution.py:334
  51.1 4.2 %all-to-all-start.1 = ((bf16[4,64,512]{2,1,0:T(8,128)(2,1)}), bf16[4,64,512]{2,1,0:T(8,128)(2,1)S(1)}, u32[]{:S(2)}, u32[]{:S(2)}) async-start(bf16[4,64,512]{2,1,0:T(8,128)(2,1)} %shard_map.142), calls=%async_computation.1 | async-start | bytes 524288 | tf_op jit(solution)/shard_map/all_to_all | solution.py:345
  55.3 0.0 copy-start.8
  55.3 0.7 copy-done.8
  56.0 0.0 copy-start.9
  56.0 0.1 copy.47.first
  56.1 0.6 copy-done.9
  56.8 4.6 %all-to-all-done.1 = bf16[4,64,512]{2,1,0:T(8,128)(2,1)S(1)} async-done(((bf16[4,64,512]{2,1,0:T(8,128)(2,1)}), bf16[4,64,512]{2,1,0:T(8,128)(2,1)S(1)}, u32[]{:S(2)}, u32[]{:S(2)}) %all-to-all-start.1) | async-done | bytes 262176 | tf_op jit(solution)/shard_map/all_to_all | solution.py:345
  61.4 0.0 copy-start.6
  61.4 4.3 %collective-permute-start.1 = (bf16[64,512]{1,0:T(8,128)(2,1)S(1)}, bf16[64,512]{1,0:T(8,128)(2,1)S(1)}, u32[]{:S(2)}, u32[]{:S(2)}) collective-permute-start(bf16[64,512]{1,0:T(8,128)(2,1)S(1)} %reduce_sum.12), channel_id=1, source_target_pairs={{0,128},{32,160},{64,192},{96,224},{1,129},{33,161},{65,193},{97,2... | collective-permute-start | bytes 196616 | tf_op jit(solution)/shard_map/ppermute | solution.py:427
  65.7 0.1 fusion.2.second
  65.8 0.0 copy-start.7
  65.8 2.8 %collective-permute-done.1 = bf16[64,512]{1,0:T(8,128)(2,1)S(1)} collective-permute-done((bf16[64,512]{1,0:T(8,128)(2,1)S(1)}, bf16[64,512]{1,0:T(8,128)(2,1)S(1)}, u32[]{:S(2)}, u32[]{:S(2)}) %collective-permute-start.1) | collective-permute-done | bytes 65568 | tf_op jit(solution)/shard_map/ppermute | solution.py:427
  68.7 0.4 collective-permute-start.2
  69.0 0.1 pad_maximum_fusion.1.edge
  69.1 0.0 copy-start.2
  69.1 0.0 copy-start.3
  69.1 5.1 %collective-permute-done.2.previous = bf16[64,512]{1,0:T(8,128)(2,1)S(1)} collective-permute-done((bf16[64,512]{1,0:T(8,128)(2,1)S(1)}, bf16[64,512]{1,0:T(8,128)(2,1)S(1)}, u32[]{:S(2)}, u32[]{:S(2)}) %collective-permute-start.2) | collective-permute-done | bytes 65568 | tf_op jit(solution)/shard_map/ppermute | solution.py:427
  74.3 0.0 copy-done.6
  74.3 0.0 copy-done.7
  74.3 3.0 %shard_map.143 = bf16[4,64,512]{2,1,0:T(8,128)(2,1)S(1)} custom-call(f32[2]{0:T(128)S(1)} %pad_maximum_fusion.1.edge, bf16[64,512]{1,0:T(8,128)(2,1)S(1)} %collective-permute-done.2.previous, bf16[64,512]{1,0:T(8,128)(2,1)S(1)} %add_convert_fusion.own, bf16[64,54]{1,0:T(8,128)(2,1)S(1)} %copy.47.first, bf16[108,128]{1,0:T(8,128)(2,1)S(1)} %fusion.2.second, ...), custom_call_target="tpu_custom_call" | custom-call | tf_op jit(solution)/shard_map/pallas_call | solution.py:334
  77.2 7.9 %all_to_all.21.gathered = bf16[4,64,512]{2,1,0:T(8,128)(2,1)S(1)} all-to-all(bf16[4,64,512]{2,1,0:T(8,128)(2,1)S(1)} %shard_map.143), channel_id=1, replica_groups=mesh['half'=2,'ring'=4,'space'=32] {'ring'}, dimensions={0} | all-to-all | bytes 524288 | tf_op jit(solution)/shard_map/all_to_all | solution.py:345
  85.2 0.0 copy-done.2
  85.2 0.0 copy-done.3
  85.2 1.4 %shard_map.144 = (bf16[32,2,16,256]{3,2,1,0:T(8,128)(2,1)S(1)}, bf16[2,8,16,512]{3,2,1,0:T(8,128)(2,1)}) custom-call(bf16[4,64,512]{2,1,0:T(8,128)(2,1)S(1)} %all_to_all.21.gathered, bf16[2,2,8,16,512]{4,3,2,1,0:T(8,128)(2,1)S(1)} %copy-done.1, bf16[512,512]{1,0:T(8,128)(2,1)S(1)} %copy-done.2, bf16[512,512]{1,0:T(8,128)(2,1)S(1)} %copy-done.3), custom_call_target="tpu_custom_call" | custom-call | tf_op jit(solution)/shard_map/pallas_call | solution.py:334
  86.6 27.7 %all_to_all.22.received = bf16[32,2,16,256]{3,2,1,0:T(8,128)(2,1)S(1)} all-to-all(bf16[32,2,16,256]{3,2,1,0:T(8,128)(2,1)S(1)} %get-tuple-element.8), channel_id=1, replica_groups=mesh['half'=2,'ring'=4,'space'=32] {'space'}, dimensions={0} | all-to-all | bytes 1048576 | tf_op jit(solution)/shard_map/all_to_all | solution.py:345
  114.3 2.1 %shard_map.145 = bf16[2,2,8,16,512]{4,3,2,1,0:T(8,128)(2,1)} custom-call(bf16[32,2,16,256]{3,2,1,0:T(8,128)(2,1)S(1)} %all_to_all.22.received, bf16[2,2,8,16,512]{4,3,2,1,0:T(8,128)(2,1)S(1)} %copy-done, f32[8,16,1]{2,1,0:T(8,128)S(1)} %copy.43.keep, bf16[512,512]{1,0:T(8,128)(2,1)S(1)} %copy-done.2, bf16[512,512]{1,0:T(8,128)(2,1)S(1)} %copy-done.3), custom_call_target="tpu_custom_call" | custom-call | tf_op jit(solution)/shard_map/pallas_call | solution.py:334
  (20 shorter events, 0.4 us)
Async XLA Ops:
  1.7 8.4 %copy-start.5 = (bf16[512,512]{1,0:T(8,128)(2,1)S(1)}, bf16[512,512]{1,0:T(8,128)(2,1)}, u32[]{:S(2)}) copy-start(bf16[512,512]{1,0:T(8,128)(2,1)} %constant.55.clone.sin) | copy-start | bytes 1572868
  2.8 3.5 %copy-start.12 = (s32[8,128]{1,0:T(8,128)S(1)}, s32[8,128]{1,0:T(8,128)}, u32[]{:S(2)}) copy-start(s32[8,128]{1,0:T(8,128)} %param.15) | copy-start | bytes 12292
  2.8 4.3 %copy-start.10 = (bf16[64,2,3,3]{0,1,3,2:T(2,128)(2,1)S(1)}, bf16[64,2,3,3]{0,1,3,2:T(2,128)(2,1)}, u32[]{:S(2)}) copy-start(bf16[64,2,3,3]{0,1,3,2:T(2,128)(2,1)} %param.16) | copy-start | bytes 6916
  2.8 7.3 %copy-start.4 = (bf16[512,512]{1,0:T(8,128)(2,1)S(1)}, bf16[512,512]{1,0:T(8,128)(2,1)}, u32[]{:S(2)}) copy-start(bf16[512,512]{1,0:T(8,128)(2,1)} %constant.54.clone.cos) | copy-start | bytes 1572868
  2.9 7.2 %copy-start = (bf16[2,2,8,16,512]{4,3,2,1,0:T(8,128)(2,1)S(1)}, bf16[2,2,8,16,512]{4,3,2,1,0:T(8,128)(2,1)}, u32[]{:S(2)}) copy-start(bf16[2,2,8,16,512]{4,3,2,1,0:T(8,128)(2,1)} %measured.3) | copy-start | bytes 1572868
  3.0 7.2 %collective-permute-start = (bf16[16,12,512]{2,1,0:T(8,128)(2,1)S(1)}, bf16[16,12,512]{2,1,0:T(8,128)(2,1)S(1)}, u32[]{:S(2)}, u32[]{:S(2)}) collective-permute-start(bf16[16,12,512]{2,1,0:T(8,128)(2,1)S(1)} %pad_maximum_fusion), channel_id=1, source_target_pairs={{1,0},{2,1},{3,2},{4,3},{5,4},{6,5},{7,6},{8,7},{9,8},{10,9},{11,1... | collective-permute-start | bytes 589832 | tf_op jit(solution)/shard_map/ppermute | solution.py:366
  7.1 0.7 copy-start.11
  20.3 28.5 %copy-start.1 = (bf16[2,2,8,16,512]{4,3,2,1,0:T(8,128)(2,1)S(1)}, bf16[2,2,8,16,512]{4,3,2,1,0:T(8,128)(2,1)}, u32[]{:S(2)}) copy-start(bf16[2,2,8,16,512]{4,3,2,1,0:T(8,128)(2,1)} %sens.3) | copy-start | bytes 1572868
  51.1 10.3 %all-to-all-start.1 = ((bf16[4,64,512]{2,1,0:T(8,128)(2,1)}), bf16[4,64,512]{2,1,0:T(8,128)(2,1)S(1)}, u32[]{:S(2)}, u32[]{:S(2)}) async-start(bf16[4,64,512]{2,1,0:T(8,128)(2,1)} %shard_map.142), calls=%async_computation.1 | async-start | bytes 524288 | tf_op jit(solution)/shard_map/all_to_all | solution.py:345
  55.3 0.7 copy-start.8
  56.0 0.7 copy-start.9
  61.4 12.8 %copy-start.6 = (bf16[6,54,144]{2,1,0:T(8,128)(2,1)S(1)}, bf16[6,54,144]{2,1,0:T(8,128)(2,1)}, u32[]{:S(2)}) copy-start(bf16[6,54,144]{2,1,0:T(8,128)(2,1)} %constant.56.clone.band1) | copy-start | bytes 279940
  61.4 7.2 %collective-permute-start.1 = (bf16[64,512]{1,0:T(8,128)(2,1)S(1)}, bf16[64,512]{1,0:T(8,128)(2,1)S(1)}, u32[]{:S(2)}, u32[]{:S(2)}) collective-permute-start(bf16[64,512]{1,0:T(8,128)(2,1)S(1)} %reduce_sum.12), channel_id=1, source_target_pairs={{0,128},{32,160},{64,192},{96,224},{1,129},{33,161},{65,193},{97,2... | collective-permute-start | bytes 196616 | tf_op jit(solution)/shard_map/ppermute | solution.py:427
  65.8 8.5 %copy-start.7 = (bf16[3,72,108]{2,1,0:T(8,128)(2,1)S(1)}, bf16[3,72,108]{2,1,0:T(8,128)(2,1)}, u32[]{:S(2)}) copy-start(bf16[3,72,108]{2,1,0:T(8,128)(2,1)} %constant.57.clone.band2) | copy-start | bytes 139972
  68.7 5.6 %collective-permute-start.2 = (bf16[64,512]{1,0:T(8,128)(2,1)S(1)}, bf16[64,512]{1,0:T(8,128)(2,1)S(1)}, u32[]{:S(2)}, u32[]{:S(2)}) collective-permute-start(bf16[64,512]{1,0:T(8,128)(2,1)S(1)} %add_convert_fusion.own), channel_id=1, source_target_pairs={{0,32},{32,64},{64,96},{96,1},{1,33},{33,65},{65,97},{97,2},{2,34}... | collective-permute-start | bytes 196616 | tf_op jit(solution)/shard_map/ppermute | solution.py:427
  69.1 16.0 %copy-start.2 = (bf16[512,512]{1,0:T(8,128)(2,1)S(1)}, bf16[512,512]{1,0:T(8,128)(2,1)}, u32[]{:S(2)}) copy-start(bf16[512,512]{1,0:T(8,128)(2,1)} %constant.52.clone.cos) | copy-start | bytes 1572868
  69.1 16.0 %copy-start.3 = (bf16[512,512]{1,0:T(8,128)(2,1)S(1)}, bf16[512,512]{1,0:T(8,128)(2,1)}, u32[]{:S(2)}) copy-start(bf16[512,512]{1,0:T(8,128)(2,1)} %constant.53.clone.sin) | copy-start | bytes 1572868

commit v4 on v3

--- a/solution.py
+++ b/solution.py
@@ -20,7 +20,7 @@
 PAIRS = COILS * SLICES
 LANES = PAIRS * ROWS
 HROWS = ROWS + 2
-UNROLL = 4
+UNROLL = 8
 BF = jnp.bfloat16
 F32 = jnp.float32
 VMEM = pl.BlockSpec(memory_space=pltpu.VMEM)
@@ -151,22 +151,31 @@
         ref[(*lead, b, rows, slice(None))] = value[:, b * 128 : (b + 1) * 128]
 
 
-def regroup(received, left):
+def regroup(received, left, coil):
     for octet in range(SPACE // 8):
-        for coil in range(COILS):
-            tiles = [
-                received[octet * 8 + i, :, :, coil * 128 : (coil + 1) * 128]
-                .astype(F32)
-                .reshape(32, 128)
-                for i in range(8)
-            ]
-            for s, tile in enumerate(blocks_swapped(tiles)):
-                row = coil * 128 + s * 16
-                tile = tile.astype(BF)
-                for h in range(2):
-                    left[h, row : row + 16, octet * 128 : (octet + 1) * 128] = tile[
-                        h * 16 : (h + 1) * 16
-                    ]
+        tiles = [
+            received[octet * 8 + i, :, :, coil * 128 : (coil + 1) * 128]
+            .astype(F32)
+            .reshape(32, 128)
+            for i in range(8)
+        ]
+        for s, tile in enumerate(blocks_swapped(tiles)):
+            row = coil * 128 + s * 16
+            tile = tile.astype(BF)
+            for h in range(2):
+                left[h, row : row + 16, octet * 128 : (octet + 1) * 128] = tile[
+                    h * 16 : (h + 1) * 16
+                ]
+
+
+def pack_kernel(measured, sens, out):
+    for i in range(PAIRS):
+        c, s = i // SLICES, i % SLICES
+        out[i] = jnp.concatenate(
+            [measured[c, h, s].astype(F32)[:4] for h in range(2)]
+            + [sens[c, h, s].astype(F32)[:2] for h in range(2)],
+            axis=0,
+        ).astype(BF)
 
 
 def kspace_kernel(measured, halo, keep, follow, w1, w2, cos, sin, out, refined, *scratch):
@@ -217,14 +226,14 @@
 
 
 def combine_kernel(received, sens, halo, cos, sin, out, left, image, partial):
-    regroup(received, left)
     for c in range(COILS):
+        regroup(received, left, c)
         rows = slice(c * 128, (c + 1) * 128)
-        image[0] = dot(left[0, rows], cos[...]) - dot(left[1, rows], sin[...])
-        image[1] = dot(left[0, rows], sin[...]) + dot(left[1, rows], cos[...])
+        image[c, 0] = dot(left[0, rows], cos[...]) - dot(left[1, rows], sin[...])
+        image[c, 1] = dot(left[0, rows], sin[...]) + dot(left[1, rows], cos[...])
         for s in range(SLICES):
             rows = slice(s * 16, (s + 1) * 16)
-            real, imag = image[0, rows], image[1, rows]
+            real, imag = image[c, 0, rows], image[c, 1, rows]
             extra = halo[c * SLICES + s].astype(F32)
             sr, si = (
                 jnp.concatenate(
@@ -247,10 +256,7 @@
         out[x // 4, x % 4 * 16 : (x % 4 + 1) * 16] = both.astype(BF)
 
 
-def image_kernel(
-    edge, previous, own, first, second, band1, band2, out,
-    w1, w2, rows8, x3, acc, fin
-):
+def image_weights(edge, first, second, band1, band2, w1, w2):
     for x in range(6):
         block = dot(first[...], band1[x])
         if x == 0:
@@ -260,6 +266,9 @@
         w1[x * CH : (x + 1) * CH, :] = block.astype(BF)
     for pair in range(3):
         w2[:, pair * 128 : (pair + 1) * 128] = dot(band2[pair], second[...]).astype(BF)
+
+
+def image_kernel(edge, previous, own, w1, w2, out, rows8, x3, acc, fin):
     put(rows8, previous[0:32].astype(F32) * edge[0], slice(0, 32))
     put(rows8, previous[32:64].astype(F32), slice(32, 64))
     put(rows8, own[0:32].astype(F32), slice(64, 96))
@@ -315,8 +324,8 @@
 
 
 def finish_kernel(received, measured, keep, cos, sin, out, left):
-    regroup(received, left)
     for c in range(COILS):
+        regroup(received, left, c)
         rows = slice(c * 128, (c + 1) * 128)
         real = dot(left[0, rows], cos[...]) + dot(left[1, rows], sin[...])
         imag = dot(left[1, rows], cos[...]) - dot(left[0, rows], sin[...])
@@ -356,13 +365,10 @@
     cos, sin, lcos, lsin = (jnp.asarray(t) for t in dft_tables())
     iband1, iband2 = (jnp.asarray(t) for t in image_bands())
 
-    rim = jnp.concatenate(
-        [
-            measured[:, :, :, :4].transpose(0, 2, 1, 3, 4).reshape(PAIRS, 8, N),
-            sensitivity[:, :, :, :2].transpose(0, 2, 1, 3, 4).reshape(PAIRS, 4, N),
-        ],
-        axis=1,
-    )
+    eight = pl.BlockSpec((COILS, 2, SLICES, 8, N), lambda i: (0, 0, 0, 0, 0))
+    rim = pl.pallas_call(
+        pack_kernel, grid=(1,), out_shape=arr(PAIRS, 12, N), in_specs=[eight, eight]
+    )(measured, sensitivity)
     halo = lax.ppermute(rim, "space", [((i + 1) % SPACE, i) for i in range(SPACE)])
 
     rows = (space * ROWS + jnp.arange(ROWS + 4, dtype=jnp.int32)) % N
@@ -404,7 +410,7 @@
         arr(RING, 64, N),
         [
             pltpu.VMEM((2, LANES, N), BF),
-            pltpu.VMEM((2, 128, N), F32),
+            pltpu.VMEM((COILS, 2, 128, N), F32),
             pltpu.VMEM((2, 4, 128, 128), F32),
         ],
         0,
@@ -430,19 +436,24 @@
     image_in = (part.astype(F32) + other.astype(F32)).astype(BF)
     previous = moved(image_in, 1, 0)
     iedge = ends((space == 0) & (ring == 0), (space == SPACE - 1) & (ring == RING - 1))
+    iw1, iw2 = call(
+        image_weights,
+        [arr(6 * CH, 144), arr(72, 6 * CH)],
+        [],
+        1,
+        iedge, ifirst, isecond, iband1, iband2,
+    )
     copies = call(
         image_kernel,
         arr(RING, 64, N),
         [
-            pltpu.VMEM((6 * CH, 144), BF),
-            pltpu.VMEM((72, 6 * CH), BF),
             pltpu.VMEM((4, 128, 128), F32),
             pltpu.VMEM((480, N), BF),
             pltpu.VMEM((SLICES * 24, N), F32),
             pltpu.VMEM((4, SLICES * 8, 128), F32),
         ],
         1,
-        iedge, previous, image_in, ifirst, isecond, iband1, iband2,
+        iedge, previous, image_in, iw1, iw2,
     )
     gathered = spread(copies, "ring")
     midway, image_out = call(

time: 117 us -> 116 us (level)
  Pallas kernels: 19.7 us -> 21.7 us
  waiting for transfers between devices: 13.9 us -> 11.9 us
  local copies, waits for them, and re-layouts: 4.78 us -> 3.37 us
    transpose x4 -> x0, local copies, waits for them, and re-layouts: 2.12 us -> none  [the longest x2 1.09 us: local(): measured[:, :, :, :4].transpose(0, 2, 1, 3, 4).reshape(PAIRS, 8, N)]
    pallas_call x0 -> x1, Pallas kernels: none -> 1.92 us  [local(): pl.pallas_call(pack_kernel, grid=(1,), out_shape=arr(PAIRS, 12, N), in_sp...]
    ppermute x1, waiting for transfers between devices: 1.28 us -> 0.01 us  [local(): lax.ppermute(rim, 'space', [((i + 1) % SPACE, i) for i in range(SPACE)])]
    pallas_call x6 -> x7, Pallas kernels: 19.7 us -> 19.8 us  [call(): pl.pallas_call(kernel, out_shape=shapes, in_specs=[SMEM] * scalars + [VME...]
  transfers between devices with their start and end apart: 4 -> 4, of which waited for: 4 -> 3; matrix products, arithmetic and copies ran while one was open for 1% -> 3% of each run, Pallas kernels for 1% -> 1%
where the time goes in v4:
time: 116 us; the launch traced here: 115 us
  blocking collectives  64.1 us (55%)
  Pallas kernels  21.7 us (19%)
  starting transfers between devices  12.1 us (10%)
  waiting for transfers between devices  11.9 us (10%)
  local copies, waits for them, and re-layouts  3.37 us (3%)
  other arithmetic  1.56 us (1%)
    all_to_all x3, blocking collectives, spread(): return lax.all_to_all(array, axis, split_axis=0, concat_axis=0, tiled=True)  64.1 us
    pallas_call x7, Pallas kernels, call(): pl.pallas_call(kernel, out_shape=shapes, in_specs=[SMEM] * scalars + [VME...  19.8 us
    ppermute x2, waiting for transfers between devices, moved(): return lax.ppermute(array, axes, pairs)  7.22 us
    ppermute x2, starting transfers between devices, moved(): return lax.ppermute(array, axes, pairs)  4.67 us
    all_to_all x1, waiting for transfers between devices, spread(): return lax.all_to_all(array, axis, split_axis=0, concat_axis=0, tiled=True)  4.62 us
    all_to_all x1, starting transfers between devices, spread(): return lax.all_to_all(array, axis, split_axis=0, concat_axis=0, tiled=True)  4.19 us
    ppermute x1, starting transfers between devices, local(): lax.ppermute(rim, 'space', [((i + 1) % SPACE, i) for i in range(SPACE)])  3.2 us
  transfers between devices with their start and end apart: 4, of which 3 were waited for; matrix products, arithmetic and copies ran while one was open for 3% of the time, Pallas kernels for 1%

profile of v4, /device:TPU:1, one launch (start us, length us, event | category | flops | bytes accessed | tf_op | source)
XLA Modules:
  0.0 115.4 jit_solution(16371036594996462095)
XLA Ops:
  0.6 0.0 copy-start.4
  0.6 0.0 copy-start.5
  0.7 0.0 copy-start.1
  0.7 1.9 %shard_map.140 = bf16[16,12,512]{2,1,0:T(8,128)(2,1)} custom-call(bf16[2,2,8,16,512]{4,3,2,1,0:T(8,128)(2,1)} %measured.5, bf16[2,2,8,16,512]{4,3,2,1,0:T(8,128)(2,1)} %sens.5), custom_call_target="tpu_custom_call" | custom-call | tf_op jit(solution)/shard_map/pallas_call | solution.py:369
  2.6 3.2 %collective-permute-start = (bf16[16,12,512]{2,1,0:T(8,128)(2,1)}, bf16[16,12,512]{2,1,0:T(8,128)(2,1)S(1)}, u32[]{:S(2)}, u32[]{:S(2)}) collective-permute-start(bf16[16,12,512]{2,1,0:T(8,128)(2,1)} %shard_map.140), channel_id=1, source_target_pairs={{1,0},{2,1},{3,2},{4,3},{5,4},{6,5},{7,6},{8,7},{9,8},{10,9},{11,1... | collective-permute-start | bytes 589832 | tf_op jit(solution)/shard_map/ppermute | solution.py:372
  5.8 1.2 %compare_reduce_fusion = pred[8,20]{0,1:T(8,128)(4,1)S(1)} fusion(s32[8,128]{1,0:T(8,128)} %param.15, s32[20]{0:T(128)S(1)} %and_select_fusion), kind=kLoop, calls=%fused_computation.1 | loop fusion | flops 40800 | bytes 4336 | tf_op jit(solution)/shard_map/reduce_or | solution.py:375
  7.0 0.2 copy.37.keep
  7.2 0.1 copy.38.follow
  7.3 0.7 copy.34
  8.0 0.1 copy.36.first
  8.2 0.7 copy.35
  8.9 0.1 pad_maximum_fusion.1.edge
  8.9 0.1 fusion.5.second
  9.0 0.8 shard_map.141
  9.9 0.0 collective-permute-done.halo
  9.9 0.0 copy-done.4
  9.9 0.0 copy-done.5
  9.9 0.0 copy-done.1
  9.9 9.4 %shard_map.142 = bf16[32,2,16,256]{3,2,1,0:T(8,128)(2,1)S(1)} custom-call(bf16[2,2,8,16,512]{4,3,2,1,0:T(8,128)(2,1)S(1)} %copy-done.1, bf16[16,12,512]{2,1,0:T(8,128)(2,1)S(1)} %collective-permute-done.halo, f32[8,16,1]{2,1,0:T(8,128)S(1)} %copy.37.keep, f32[8,8,1]{2,1,0:T(8,128)S(1)} %copy.38.follow, bf16[1152,128]{1,0:T(8,128)(2,1)S(1)} %get-tuple-element.8.w1, ...), custom_call_target="tpu_custom_call" | custom-call | tf_op jit(solution)/shard_map/pallas_call | solution.py:343
  19.3 0.0 copy-start
  19.3 28.5 %all_to_all.20.received = bf16[32,2,16,256]{3,2,1,0:T(8,128)(2,1)S(1)} all-to-all(bf16[32,2,16,256]{3,2,1,0:T(8,128)(2,1)S(1)} %shard_map.142), channel_id=1, replica_groups=mesh['half'=2,'ring'=4,'space'=32] {'space'}, dimensions={0} | all-to-all | bytes 1048576 | tf_op jit(solution)/shard_map/all_to_all | solution.py:354
  47.9 0.0 copy-done
  47.9 2.3 %shard_map.143 = bf16[4,64,512]{2,1,0:T(8,128)(2,1)} custom-call(bf16[32,2,16,256]{3,2,1,0:T(8,128)(2,1)S(1)} %all_to_all.20.received, bf16[2,2,8,16,512]{4,3,2,1,0:T(8,128)(2,1)S(1)} %copy-done, bf16[16,12,512]{2,1,0:T(8,128)(2,1)S(1)} %collective-permute-done.halo, bf16[512,512]{1,0:T(8,128)(2,1)S(1)} %copy-done.4, bf16[512,512]{1,0:T(8,128)(2,1)S(1)} %copy-done.5), custom_call_target="tpu_custom_call" | custom-call | tf_op jit(solution)/shard_map/pallas_call | solution.py:343
  50.1 4.2 %all-to-all-start.1 = ((bf16[4,64,512]{2,1,0:T(8,128)(2,1)}), bf16[4,64,512]{2,1,0:T(8,128)(2,1)S(1)}, u32[]{:S(2)}, u32[]{:S(2)}) async-start(bf16[4,64,512]{2,1,0:T(8,128)(2,1)} %shard_map.143), calls=%async_computation.1 | async-start | bytes 524288 | tf_op jit(solution)/shard_map/all_to_all | solution.py:354
  54.3 0.0 copy-start.8
  54.3 0.7 copy-done.8
  55.0 0.0 copy-start.9
  55.1 0.1 copy.41.first
  55.2 0.6 copy-done.9
  55.8 4.6 %all-to-all-done.1 = bf16[4,64,512]{2,1,0:T(8,128)(2,1)S(1)} async-done(((bf16[4,64,512]{2,1,0:T(8,128)(2,1)}), bf16[4,64,512]{2,1,0:T(8,128)(2,1)S(1)}, u32[]{:S(2)}, u32[]{:S(2)}) %all-to-all-start.1) | async-done | bytes 262176 | tf_op jit(solution)/shard_map/all_to_all | solution.py:354
  60.5 0.0 copy-start.6
  60.5 4.3 %collective-permute-start.1 = (bf16[64,512]{1,0:T(8,128)(2,1)S(1)}, bf16[64,512]{1,0:T(8,128)(2,1)S(1)}, u32[]{:S(2)}, u32[]{:S(2)}) collective-permute-start(bf16[64,512]{1,0:T(8,128)(2,1)S(1)} %reduce_sum.12), channel_id=1, source_target_pairs={{0,128},{32,160},{64,192},{96,224},{1,129},{33,161},{65,193},{97,2... | collective-permute-start | bytes 196616 | tf_op jit(solution)/shard_map/ppermute | solution.py:433
  64.8 0.1 fusion.2.second
  64.8 0.0 copy-start.7
  64.8 2.8 %collective-permute-done.1 = bf16[64,512]{1,0:T(8,128)(2,1)S(1)} collective-permute-done((bf16[64,512]{1,0:T(8,128)(2,1)S(1)}, bf16[64,512]{1,0:T(8,128)(2,1)S(1)}, u32[]{:S(2)}, u32[]{:S(2)}) %collective-permute-start.1) | collective-permute-done | bytes 65568 | tf_op jit(solution)/shard_map/ppermute | solution.py:433
  67.7 0.4 collective-permute-start.2
  68.1 0.1 pad_maximum_fusion.edge
  68.1 0.0 copy-done.6
  68.1 0.0 copy-done.7
  68.2 0.8 shard_map.144
  68.9 4.4 %collective-permute-done.2.previous = bf16[64,512]{1,0:T(8,128)(2,1)S(1)} collective-permute-done((bf16[64,512]{1,0:T(8,128)(2,1)S(1)}, bf16[64,512]{1,0:T(8,128)(2,1)S(1)}, u32[]{:S(2)}, u32[]{:S(2)}) %collective-permute-start.2) | collective-permute-done | bytes 65568 | tf_op jit(solution)/shard_map/ppermute | solution.py:433
  73.3 0.0 copy-start.2
  73.3 0.0 copy-start.3
  73.3 2.9 %shard_map.145 = bf16[4,64,512]{2,1,0:T(8,128)(2,1)S(1)} custom-call(f32[2]{0:T(128)S(1)} %pad_maximum_fusion.edge, bf16[64,512]{1,0:T(8,128)(2,1)S(1)} %collective-permute-done.2.previous, bf16[64,512]{1,0:T(8,128)(2,1)S(1)} %add_convert_fusion.own, bf16[384,144]{1,0:T(8,128)(2,1)S(1)} %get-tuple-element.10.w1, bf16[72,384]{1,0:T(8,128)(2,1)S(1)} %get-tuple-element.11.w2), custom_call_target="tpu_custom_call" | custom-call | tf_op jit(solution)/shard_map/pallas_call | solution.py:343
  76.2 7.9 %all_to_all.21.gathered = bf16[4,64,512]{2,1,0:T(8,128)(2,1)S(1)} all-to-all(bf16[4,64,512]{2,1,0:T(8,128)(2,1)S(1)} %shard_map.145), channel_id=1, replica_groups=mesh['half'=2,'ring'=4,'space'=32] {'ring'}, dimensions={0} | all-to-all | bytes 524288 | tf_op jit(solution)/shard_map/all_to_all | solution.py:354
  84.1 0.0 copy-done.2
  84.1 0.0 copy-done.3
  84.1 1.4 %shard_map.146 = (bf16[32,2,16,256]{3,2,1,0:T(8,128)(2,1)S(1)}, bf16[2,8,16,512]{3,2,1,0:T(8,128)(2,1)}) custom-call(bf16[4,64,512]{2,1,0:T(8,128)(2,1)S(1)} %all_to_all.21.gathered, bf16[2,2,8,16,512]{4,3,2,1,0:T(8,128)(2,1)S(1)} %copy-done, bf16[512,512]{1,0:T(8,128)(2,1)S(1)} %copy-done.2, bf16[512,512]{1,0:T(8,128)(2,1)S(1)} %copy-done.3), custom_call_target="tpu_custom_call" | custom-call | tf_op jit(solution)/shard_map/pallas_call | solution.py:343
  85.6 27.7 %all_to_all.22.received = bf16[32,2,16,256]{3,2,1,0:T(8,128)(2,1)S(1)} all-to-all(bf16[32,2,16,256]{3,2,1,0:T(8,128)(2,1)S(1)} %get-tuple-element.12), channel_id=1, replica_groups=mesh['half'=2,'ring'=4,'space'=32] {'space'}, dimensions={0} | all-to-all | bytes 1048576 | tf_op jit(solution)/shard_map/all_to_all | solution.py:354
  113.3 2.1 %shard_map.147 = bf16[2,2,8,16,512]{4,3,2,1,0:T(8,128)(2,1)} custom-call(bf16[32,2,16,256]{3,2,1,0:T(8,128)(2,1)S(1)} %all_to_all.22.received, bf16[2,2,8,16,512]{4,3,2,1,0:T(8,128)(2,1)S(1)} %copy-done.1, f32[8,16,1]{2,1,0:T(8,128)S(1)} %copy.37.keep, bf16[512,512]{1,0:T(8,128)(2,1)S(1)} %copy-done.2, bf16[512,512]{1,0:T(8,128)(2,1)S(1)} %copy-done.3), custom_call_target="tpu_custom_call" | custom-call | tf_op jit(solution)/shard_map/pallas_call | solution.py:343
  (13 shorter events, 0.2 us)
Async XLA Ops:
  0.6 9.2 %copy-start.4 = (bf16[512,512]{1,0:T(8,128)(2,1)S(1)}, bf16[512,512]{1,0:T(8,128)(2,1)}, u32[]{:S(2)}) copy-start(bf16[512,512]{1,0:T(8,128)(2,1)} %constant.54.clone.cos) | copy-start | bytes 1572868
  0.6 9.2 %copy-start.5 = (bf16[512,512]{1,0:T(8,128)(2,1)S(1)}, bf16[512,512]{1,0:T(8,128)(2,1)}, u32[]{:S(2)}) copy-start(bf16[512,512]{1,0:T(8,128)(2,1)} %constant.55.clone.sin) | copy-start | bytes 1572868
  0.7 9.2 %copy-start.1 = (bf16[2,2,8,16,512]{4,3,2,1,0:T(8,128)(2,1)S(1)}, bf16[2,2,8,16,512]{4,3,2,1,0:T(8,128)(2,1)}, u32[]{:S(2)}) copy-start(bf16[2,2,8,16,512]{4,3,2,1,0:T(8,128)(2,1)} %measured.5) | copy-start | bytes 1572868
  2.6 7.3 %collective-permute-start = (bf16[16,12,512]{2,1,0:T(8,128)(2,1)}, bf16[16,12,512]{2,1,0:T(8,128)(2,1)S(1)}, u32[]{:S(2)}, u32[]{:S(2)}) collective-permute-start(bf16[16,12,512]{2,1,0:T(8,128)(2,1)} %shard_map.140), channel_id=1, source_target_pairs={{1,0},{2,1},{3,2},{4,3},{5,4},{6,5},{7,6},{8,7},{9,8},{10,9},{11,1... | collective-permute-start | bytes 589832 | tf_op jit(solution)/shard_map/ppermute | solution.py:372
  19.3 28.5 %copy-start = (bf16[2,2,8,16,512]{4,3,2,1,0:T(8,128)(2,1)S(1)}, bf16[2,2,8,16,512]{4,3,2,1,0:T(8,128)(2,1)}, u32[]{:S(2)}) copy-start(bf16[2,2,8,16,512]{4,3,2,1,0:T(8,128)(2,1)} %sens.5) | copy-start | bytes 1572868
  50.1 10.3 %all-to-all-start.1 = ((bf16[4,64,512]{2,1,0:T(8,128)(2,1)}), bf16[4,64,512]{2,1,0:T(8,128)(2,1)S(1)}, u32[]{:S(2)}, u32[]{:S(2)}) async-start(bf16[4,64,512]{2,1,0:T(8,128)(2,1)} %shard_map.143), calls=%async_computation.1 | async-start | bytes 524288 | tf_op jit(solution)/shard_map/all_to_all | solution.py:354
  54.3 0.7 copy-start.8
  55.0 0.7 copy-start.9
  60.5 7.7 %copy-start.6 = (bf16[6,54,144]{2,1,0:T(8,128)(2,1)S(1)}, bf16[6,54,144]{2,1,0:T(8,128)(2,1)}, u32[]{:S(2)}) copy-start(bf16[6,54,144]{2,1,0:T(8,128)(2,1)} %constant.56.clone.band1) | copy-start | bytes 279940
  60.5 7.2 %collective-permute-start.1 = (bf16[64,512]{1,0:T(8,128)(2,1)S(1)}, bf16[64,512]{1,0:T(8,128)(2,1)S(1)}, u32[]{:S(2)}, u32[]{:S(2)}) collective-permute-start(bf16[64,512]{1,0:T(8,128)(2,1)S(1)} %reduce_sum.12), channel_id=1, source_target_pairs={{0,128},{32,160},{64,192},{96,224},{1,129},{33,161},{65,193},{97,2... | collective-permute-start | bytes 196616 | tf_op jit(solution)/shard_map/ppermute | solution.py:433
  64.8 3.3 %copy-start.7 = (bf16[3,72,108]{2,1,0:T(8,128)(2,1)S(1)}, bf16[3,72,108]{2,1,0:T(8,128)(2,1)}, u32[]{:S(2)}) copy-start(bf16[3,72,108]{2,1,0:T(8,128)(2,1)} %constant.57.clone.band2) | copy-start | bytes 139972
  67.7 5.6 %collective-permute-start.2 = (bf16[64,512]{1,0:T(8,128)(2,1)S(1)}, bf16[64,512]{1,0:T(8,128)(2,1)S(1)}, u32[]{:S(2)}, u32[]{:S(2)}) collective-permute-start(bf16[64,512]{1,0:T(8,128)(2,1)S(1)} %add_convert_fusion.own), channel_id=1, source_target_pairs={{0,32},{32,64},{64,96},{96,1},{1,33},{33,65},{65,97},{97,2},{2,34}... | collective-permute-start | bytes 196616 | tf_op jit(solution)/shard_map/ppermute | solution.py:433
  73.3 10.8 %copy-start.2 = (bf16[512,512]{1,0:T(8,128)(2,1)S(1)}, bf16[512,512]{1,0:T(8,128)(2,1)}, u32[]{:S(2)}) copy-start(bf16[512,512]{1,0:T(8,128)(2,1)} %constant.52.clone.cos) | copy-start | bytes 1572868
  73.3 10.8 %copy-start.3 = (bf16[512,512]{1,0:T(8,128)(2,1)S(1)}, bf16[512,512]{1,0:T(8,128)(2,1)}, u32[]{:S(2)}) copy-start(bf16[512,512]{1,0:T(8,128)(2,1)} %constant.53.clone.sin) | copy-start | bytes 1572868

commit v5 on v4

--- a/solution.py
+++ b/solution.py
@@ -26,6 +26,7 @@
 VMEM = pl.BlockSpec(memory_space=pltpu.VMEM)
 SMEM = pl.BlockSpec(memory_space=pltpu.SMEM)
 NT = (((1,), (1,)), ((), ()))
+TN = (((0,), (0,)), ((), ()))
 
 
 def dft_tables():
@@ -48,9 +49,31 @@
     return quotient, v - quotient * size
 
 
-def kspace_weights(edge, first, second, w1, w2):
-    h_row, rest = split(iota((18, 128), 0), 9, 2)
-    p_row, q_row = split(rest, 3, 3)
+def rows_of(ref, *dims):
+    return jnp.concatenate([ref[where].astype(F32) for where in np.ndindex(*dims)], axis=0).astype(BF)
+
+
+def doubled(block):
+    zero = jnp.zeros_like(block)
+    return jnp.concatenate(
+        [jnp.concatenate([block, zero], axis=1), jnp.concatenate([zero, block], axis=1)], axis=0
+    )
+
+
+def kspace_weights(spot, lines, first, second, w1, w2, keep, follow):
+    row = spot[0] * ROWS + iota((24, 128), 0)
+    row = jnp.where(iota((24, 128), 0) >= ROWS + 4, row - 4, row)
+    row = jnp.where(row >= N, row - N, row)
+    for s in range(SLICES):
+        hit = jnp.where(lines[s : s + 1, :] == row, 1.0, 0.0)
+        hit = jnp.max(hit, axis=1, keepdims=True)
+        keep[s] = hit[:ROWS]
+        follow[s] = hit[ROWS:]
+    whole = jnp.where(spot[0] == SPACE - 1, 0.0, 1.0)
+    rest = iota((18, 128), 0)
+    h_row = rest & 1
+    p_row, q_row = split(rest >> 1, 3, 3)
+    matrix = rows_of(first, 3, 3)
     lane = iota((18, 128), 1)
     late = lane >= 96
     rest = jnp.where(late, lane - 96, lane)
@@ -61,14 +84,15 @@
     late = iota((CH, 128), 1) >= 96
     for r in range(HROWS):
         band = jnp.where(hidden_row == r, 1.0, 0.0).astype(BF)
-        block = dot(first[...], band)
+        block = dot_tn(matrix, band)
         across = ~late if r + 1 >= ROWS else late
-        block = jnp.where(across, block * edge[1], block)
+        block = jnp.where(across, block * whole, block)
         w1[r * CH : (r + 1) * CH, :] = block.astype(BF)
     line, lane = iota((96, 36), 0), iota((96, 36), 1)
     parity, rest = split(lane, 18, 2)
-    q_lane, rest = split(rest, 6, 3)
-    o_lane, p_lane = split(rest, 3, 2)
+    o_lane = rest & 1
+    p_lane, q_lane = split(rest >> 1, 3, 3)
+    matrix = doubled(rows_of(second, 3, 3))
     place = line & 15
     place = jnp.where(place < 2, place + ROWS, place)
     match = (line >> 5 == q_lane) & ((line >> 4) & 1 == o_lane)
@@ -77,9 +101,9 @@
     upper = iota((96, 128), 1) >= CH
     for pair in range(HROWS // 2):
         band = jnp.where(pair_row == 2 * pair, 1.0, 0.0).astype(BF)
-        block = dot(band, second[...])
+        block = dot(band, matrix)
         beyond = 2 * pair + 1 + upper.astype(jnp.int32) >= ROWS
-        block = jnp.where(late != beyond, block * edge[1], block)
+        block = jnp.where(late != beyond, block * whole, block)
         w2[:, pair * 128 : (pair + 1) * 128] = block.astype(BF)
 
 
@@ -90,7 +114,7 @@
             for a in range(3):
                 for p in range(3):
                     for q in range(3):
-                        first[x, h * 27 + a * 9 + p * 3 + q, a * 48 + q * 16 + (x + p) * 2 + h] = 1
+                        first[x, a * 18 + p * 6 + q * 2 + h, a * 48 + q * 16 + (x + p) * 2 + h] = 1
     second = np.zeros((3, 72, 108), np.float32)
     for pair in range(3):
         for parity in range(2):
@@ -103,13 +127,17 @@
                                 second[
                                     pair,
                                     a * 24 + q * 8 + o * 4 + e,
-                                    parity * 54 + o * 27 + a * 9 + p * 3 + q,
+                                    parity * 54 + a * 18 + p * 6 + q * 2 + o,
                                 ] = 1
     return first.astype(BF), second.astype(BF)
 
 
 def dot(a, b):
     return jnp.dot(a, b, preferred_element_type=F32)
+
+
+def dot_tn(a, b):
+    return lax.dot_general(a, b, TN, preferred_element_type=F32)
 
 
 def dot_nt(a, b):
@@ -168,17 +196,34 @@
                 ]
 
 
-def pack_kernel(measured, sens, out):
+def pack_kernel(measured, sens, out, mine, maps, sems):
+    copies = [
+        pltpu.make_async_copy(source.at[:, :, :, pl.ds(0, 8), :], target, sems.at[n])
+        for n, (source, target) in enumerate(((measured, mine), (sens, maps)))
+    ]
+    for copy in copies:
+        copy.start()
+    for copy in copies:
+        copy.wait()
     for i in range(PAIRS):
         c, s = i // SLICES, i % SLICES
         out[i] = jnp.concatenate(
-            [measured[c, h, s].astype(F32)[:4] for h in range(2)]
-            + [sens[c, h, s].astype(F32)[:2] for h in range(2)],
+            [mine[c, h, s].astype(F32)[:4] for h in range(2)]
+            + [maps[c, h, s].astype(F32)[:2] for h in range(2)],
             axis=0,
         ).astype(BF)
 
 
-def kspace_kernel(measured, halo, keep, follow, w1, w2, cos, sin, out, refined, *scratch):
+def kspace_kernel(
+    measured, halo, keep, follow, w1, w2, far_cos, far_sin, out, refined, cos, sin, sems, *scratch
+):
+    tables = [
+        pltpu.make_async_copy(source, target, sems.at[n])
+        for n, (source, target) in enumerate(((far_cos, cos), (far_sin, sin)))
+    ]
+    for table in tables:
+        table.start()
+
     def one(i, x3, hidden):
         c, s = i // SLICES, i % SLICES
         mask = keep[s] > 0
@@ -216,6 +261,8 @@
         return carry
 
     lax.fori_loop(0, PAIRS // UNROLL, step, 0)
+    for table in tables:
+        table.wait()
     for part in range(2):
         rows = pl.ds(part * 256, 256)
         co, si = cos[rows, :], sin[rows, :]
@@ -225,7 +272,7 @@
         out[part * 16 : (part + 1) * 16, 1] = imag.astype(BF).reshape(16, 16, LANES)
 
 
-def combine_kernel(received, sens, halo, cos, sin, out, left, image, partial):
+def combine_kernel(spot, received, sens, halo, cos, sin, out, left, image, partial):
     for c in range(COILS):
         regroup(received, left, c)
         rows = slice(c * 128, (c + 1) * 128)
@@ -248,27 +295,39 @@
                 pi = pi + wide(partial, 1, rows)
             put(partial, pr, 0, rows)
             put(partial, pi, 1, rows)
+    turn = RING - spot[0] % RING
     for x in range(ROWS):
         place = (x + 2) % ROWS
         both = jnp.concatenate(
             [wide(partial, h, pl.ds(place, 8, stride=16)) for h in range(2)], axis=0
         )
-        out[x // 4, x % 4 * 16 : (x % 4 + 1) * 16] = both.astype(BF)
-
-
-def image_weights(edge, first, second, band1, band2, w1, w2):
+        out[(x // 4 + turn) % RING, x % 4 * 16 : (x % 4 + 1) * 16] = both.astype(BF)
+
+
+def outer(spot):
+    quarter = (spot[0] + spot[1]) % RING
+    first = jnp.where((spot[0] == 0) & (quarter == 0), 0.0, 1.0)
+    last = jnp.where((spot[0] == SPACE - 1) & (quarter == RING - 1), 0.0, 1.0)
+    return first, last
+
+
+def image_weights(spot, first, second, band1, band2, w1, w2):
+    edge = outer(spot)
+    matrix = rows_of(first, 3, 3, 3)
     for x in range(6):
-        block = dot(first[...], band1[x])
+        block = dot_tn(matrix, band1[x])
         if x == 0:
             block = block * edge[0]
         if x == 5:
             block = block * edge[1]
         w1[x * CH : (x + 1) * CH, :] = block.astype(BF)
+    matrix = doubled(rows_of(second, 3, 3, 3))
     for pair in range(3):
-        w2[:, pair * 128 : (pair + 1) * 128] = dot(band2[pair], second[...]).astype(BF)
-
-
-def image_kernel(edge, previous, own, w1, w2, out, rows8, x3, acc, fin):
+        w2[:, pair * 128 : (pair + 1) * 128] = dot(band2[pair], matrix).astype(BF)
+
+
+def image_kernel(spot, previous, own, w1, w2, out, rows8, x3, acc, fin):
+    edge = outer(spot)
     put(rows8, previous[0:32].astype(F32) * edge[0], slice(0, 32))
     put(rows8, previous[32:64].astype(F32), slice(32, 64))
     put(rows8, own[0:32].astype(F32), slice(64, 96))
@@ -299,9 +358,10 @@
             out[y, e * 16 : (e + 1) * 16] = value
 
 
-def expand_kernel(gathered, sens, cos, sin, out, image_out, image, data):
+def expand_kernel(spot, gathered, sens, cos, sin, out, image_out, image, data):
+    turn = RING - spot[0] % RING
     for x in range(ROWS):
-        both = gathered[x // 4, x % 4 * 16 : (x % 4 + 1) * 16].astype(F32)
+        both = gathered[(x // 4 + turn) % RING, x % 4 * 16 : (x % 4 + 1) * 16].astype(F32)
         for h in range(2):
             put(image, both[h * 8 : (h + 1) * 8], h, pl.ds(x, 8, stride=16))
     for s in range(SLICES):
@@ -338,12 +398,14 @@
                 ).astype(BF)
 
 
-def call(kernel, shapes, scratch, scalars, *operands):
+def call(kernel, shapes, scratch, scalars, *operands, far=0):
     single = not isinstance(shapes, list)
     return pl.pallas_call(
         kernel,
         out_shape=shapes,
-        in_specs=[SMEM] * scalars + [VMEM] * (len(operands) - scalars),
+        in_specs=[SMEM] * scalars
+        + [VMEM] * (len(operands) - scalars - far)
+        + [pl.BlockSpec(memory_space=pl.ANY)] * far,
         out_specs=VMEM if single else [VMEM] * len(shapes),
         scratch_shapes=scratch,
         compiler_params=pltpu.CompilerParams(vmem_limit_bytes=40 * 1024 * 1024),
@@ -365,44 +427,42 @@
     cos, sin, lcos, lsin = (jnp.asarray(t) for t in dft_tables())
     iband1, iband2 = (jnp.asarray(t) for t in image_bands())
 
-    eight = pl.BlockSpec((COILS, 2, SLICES, 8, N), lambda i: (0, 0, 0, 0, 0))
+    spot = jnp.stack([space, ring])
     rim = pl.pallas_call(
-        pack_kernel, grid=(1,), out_shape=arr(PAIRS, 12, N), in_specs=[eight, eight]
+        pack_kernel,
+        out_shape=arr(PAIRS, 12, N),
+        in_specs=[pl.BlockSpec(memory_space=pl.ANY)] * 2,
+        out_specs=VMEM,
+        scratch_shapes=[pltpu.VMEM((COILS, 2, SLICES, 8, N), BF)] * 2
+        + [pltpu.SemaphoreType.DMA((2,))],
     )(measured, sensitivity)
     halo = lax.ppermute(rim, "space", [((i + 1) % SPACE, i) for i in range(SPACE)])
 
-    rows = (space * ROWS + jnp.arange(ROWS + 4, dtype=jnp.int32)) % N
-    sampled = jnp.any(sample_lines[:, :, None] == rows[None, None, :], axis=1).astype(F32)
-    keep = sampled[:, :ROWS, None]
-    follow = jnp.tile(sampled[:, ROWS:], (1, 2))[:, :, None]
-
-    def ends(first, last):
-        return jnp.stack([1 - first.astype(F32), 1 - last.astype(F32)])
-
-    kedge = ends(space == 0, space == SPACE - 1)
-    kfirst = kspace_first.reshape(CH, 18)
-    ksecond = kspace_second.transpose(3, 0, 2, 1).reshape(18, CH)
-    zero = jnp.zeros_like(ksecond)
-    ksecond = jnp.block([[ksecond, zero], [zero, ksecond]])
-    ifirst = image_first.reshape(CH, 54)
-    isecond = image_second.transpose(0, 2, 3, 4, 1).reshape(54, CH)
-    zero = jnp.zeros_like(isecond)
-    isecond = jnp.block([[isecond, zero], [zero, isecond]])
-
-    kw1, kw2 = call(
+    kw1, kw2, keep, follow = call(
         kspace_weights,
-        [arr(HROWS * CH, 128), arr(96, HROWS * CH)],
+        [
+            arr(HROWS * CH, 128),
+            arr(96, HROWS * CH),
+            arr(SLICES, ROWS, 1, dtype=F32),
+            arr(SLICES, 8, 1, dtype=F32),
+        ],
         [],
         1,
-        kedge, kfirst, ksecond,
+        spot, sample_lines, kspace_first.transpose(2, 3, 1, 0), kspace_second.transpose(2, 3, 0, 1),
     )
     half_done = call(
         kspace_kernel,
         arr(SPACE, 2, ROWS, LANES),
-        [pltpu.VMEM((2, LANES, N), BF)]
+        [
+            pltpu.VMEM((2, LANES, N), BF),
+            pltpu.VMEM((N, N), BF),
+            pltpu.VMEM((N, N), BF),
+            pltpu.SemaphoreType.DMA((2,)),
+        ]
         + [pltpu.VMEM((128, N), BF), pltpu.VMEM((HROWS * CH, N), BF)] * UNROLL,
         0,
         measured, halo, keep, follow, kw1, kw2, lcos, lsin,
+        far=2,
     )
     half_done = spread(half_done, "space")
     partial = call(
@@ -413,35 +473,32 @@
             pltpu.VMEM((COILS, 2, 128, N), F32),
             pltpu.VMEM((2, 4, 128, 128), F32),
         ],
-        0,
-        half_done, sensitivity, halo, lcos, lsin,
+        1,
+        spot, half_done, sensitivity, halo, lcos, lsin,
     )
     part = spread(partial, "ring").astype(F32).sum(axis=0).astype(BF)
 
     def place(half, i):
-        return (half * RING + i % RING) * SPACE + i // RING
-
+        block, quarter = i // RING % SPACE, i % RING
+        return (half * RING + (quarter - block) % RING) * SPACE + block
+
+    axes = ("half", "ring", "space")
     count = RING * SPACE
-    axes = ("half", "ring", "space")
-
-    def moved(array, step, flip):
-        pairs = [
-            (place(half, i), place(half ^ flip, (i + step) % count))
-            for half in range(HALVES)
-            for i in range(count)
-        ]
-        return lax.ppermute(array, axes, pairs)
-
-    other = moved(part, 0, 1)
+    exchange = [(place(half, i), place(1 - half, i)) for half in range(HALVES) for i in range(count)]
+    forward = [
+        (place(half ^ (i % (8 * RING) == 8 * RING - 1), i), place(half, i + 1))
+        for half in range(HALVES)
+        for i in range(count)
+    ]
+    other = lax.ppermute(part, axes, exchange)
     image_in = (part.astype(F32) + other.astype(F32)).astype(BF)
-    previous = moved(image_in, 1, 0)
-    iedge = ends((space == 0) & (ring == 0), (space == SPACE - 1) & (ring == RING - 1))
+    previous = lax.ppermute(image_in, axes, forward)
     iw1, iw2 = call(
         image_weights,
         [arr(6 * CH, 144), arr(72, 6 * CH)],
         [],
         1,
-        iedge, ifirst, isecond, iband1, iband2,
+        spot, image_first.transpose(2, 3, 4, 1, 0), image_second.transpose(2, 3, 4, 0, 1), iband1, iband2,
     )
     copies = call(
         image_kernel,
@@ -453,15 +510,15 @@
             pltpu.VMEM((4, SLICES * 8, 128), F32),
         ],
         1,
-        iedge, previous, image_in, iw1, iw2,
+        spot, previous, image_in, iw1, iw2,
     )
     gathered = spread(copies, "ring")
     midway, image_out = call(
         expand_kernel,
         [arr(SPACE, 2, ROWS, LANES), arr(2, SLICES, ROWS, N)],
         [pltpu.VMEM((2, 4, 128, 128), F32), pltpu.VMEM((2, LANES, N), BF)],
-        0,
-        gathered, sensitivity, cos, sin,
+        1,
+        spot, gathered, sensitivity, cos, sin,
     )
     midway = spread(midway, "space")
     kspace_out = call(

time: 116 us -> 115 us (level)
  blocking collectives: 64.1 us -> 73.1 us
  starting transfers between devices: 12.1 us -> 7.94 us
  waiting for transfers between devices: 11.9 us -> 8.48 us
  local copies, waits for them, and re-layouts: 3.37 us -> 1.74 us
  other arithmetic: 1.56 us -> 0.14 us
    all_to_all x3 -> x4, blocking collectives: 64.1 us -> 73.1 us  [spread(): return lax.all_to_all(array, axis, split_axis=0, concat_axis=0, tiled=True)]
    all_to_all x1 -> x0, waiting for transfers between devices: 4.62 us -> none  [spread(): return lax.all_to_all(array, axis, split_axis=0, concat_axis=0, tiled=True)]
    all_to_all x1 -> x0, starting transfers between devices: 4.19 us -> none  [spread(): return lax.all_to_all(array, axis, split_axis=0, concat_axis=0, tiled=True)]
    ppermute x1, waiting for transfers between devices: 0.01 us -> 2.46 us  [local(): lax.ppermute(rim, 'space', [((i + 1) % SPACE, i) for i in range(SPACE)])]
    ppermute x2, waiting for transfers between devices: 7.22 us -> 6.02 us  [the longest x1 3.2 us: local(): previous = lax.ppermute(image_in, axes, forward)]
    reduce_or x1 -> x0, other arithmetic: 1.17 us -> none  [local(): jnp.any(sample_lines[:, :, None] == rows[None, None, :], axis=1).astype(F32)]
  transfers between devices with their start and end apart: 4 -> 3, of which waited for: 3 -> 3; matrix products, arithmetic and copies ran while one was open for 3% -> 0% of each run, Pallas kernels for 1% -> 1%
where the time goes in v5:
time: 115 us
  blocking collectives  73.1 us (64%)
  Pallas kernels  22.5 us (20%)
  waiting for transfers between devices  8.48 us (7%)
  starting transfers between devices  7.94 us (7%)
  local copies, waits for them, and re-layouts  1.74 us (2%)
    all_to_all x4, blocking collectives, spread(): return lax.all_to_all(array, axis, split_axis=0, concat_axis=0, tiled=True)  73.1 us
    pallas_call x7, Pallas kernels, call(): pl.pallas_call(kernel, out_shape=shapes, in_specs=[SMEM] * scalars + [VME...  20.6 us
    ppermute x1, starting transfers between devices, local(): other = lax.ppermute(part, axes, exchange)  4.3 us
    ppermute x1, starting transfers between devices, local(): lax.ppermute(rim, 'space', [((i + 1) % SPACE, i) for i in range(SPACE)])  3.28 us
    ppermute x1, waiting for transfers between devices, local(): previous = lax.ppermute(image_in, axes, forward)  3.2 us
    ppermute x1, waiting for transfers between devices, local(): other = lax.ppermute(part, axes, exchange)  2.81 us
    ppermute x1, waiting for transfers between devices, local(): lax.ppermute(rim, 'space', [((i + 1) % SPACE, i) for i in range(SPACE)])  2.46 us
  transfers between devices with their start and end apart: 3, of which 3 were waited for; matrix products, arithmetic and copies ran while one was open for 0% of the time, Pallas kernels for 1%

profile of v5, /device:TPU:1, one launch (start us, length us, event | category | flops | bytes accessed | tf_op | source)
XLA Modules:
  0.0 114.7 jit_solution(1824747997272112880)
XLA Ops:
  0.6 0.0 copy-start.4
  0.6 0.0 copy-start.1
  0.7 1.9 %shard_map.140 = bf16[16,12,512]{2,1,0:T(8,128)(2,1)} custom-call(bf16[2,2,8,16,512]{4,3,2,1,0:T(8,128)(2,1)} %measured.5, bf16[2,2,8,16,512]{4,3,2,1,0:T(8,128)(2,1)} %sens.5), custom_call_target="tpu_custom_call" | custom-call | tf_op jit(solution)/shard_map/pallas_call | solution.py:431
  2.6 3.3 %collective-permute-start = (bf16[16,12,512]{2,1,0:T(8,128)(2,1)}, bf16[16,12,512]{2,1,0:T(8,128)(2,1)S(1)}, u32[]{:S(2)}, u32[]{:S(2)}) collective-permute-start(bf16[16,12,512]{2,1,0:T(8,128)(2,1)} %shard_map.140), channel_id=1, source_target_pairs={{1,0},{2,1},{3,2},{4,3},{5,4},{6,5},{7,6},{8,7},{9,8},{10,9},{11,1... | collective-permute-start | bytes 589832 | tf_op jit(solution)/shard_map/ppermute | solution.py:439
  5.8 0.0 copy-start.13
  5.9 0.0 copy-start.11
  5.9 0.0 copy-start.12
  5.9 0.1 pad_add_fusion.spot
  5.9 0.6 copy-done.13
  6.5 0.0 copy-done.11
  6.6 0.0 copy-done.12
  6.6 0.9 shard_map.141
  7.5 2.5 %collective-permute-done.halo = bf16[16,12,512]{2,1,0:T(8,128)(2,1)S(1)} collective-permute-done((bf16[16,12,512]{2,1,0:T(8,128)(2,1)}, bf16[16,12,512]{2,1,0:T(8,128)(2,1)S(1)}, u32[]{:S(2)}, u32[]{:S(2)}) %collective-permute-start) | collective-permute-done | bytes 196640 | tf_op jit(solution)/shard_map/ppermute | solution.py:439
  9.9 0.0 copy-done.4
  9.9 0.0 copy-done.1
  9.9 0.0 copy-start.5
  9.9 1.0 copy-done.5
  11.0 9.6 %shard_map.142 = bf16[32,2,16,256]{3,2,1,0:T(8,128)(2,1)S(1)} custom-call(bf16[2,2,8,16,512]{4,3,2,1,0:T(8,128)(2,1)S(1)} %copy-done.1, bf16[16,12,512]{2,1,0:T(8,128)(2,1)S(1)} %collective-permute-done.halo, f32[8,16,1]{2,1,0:T(8,128)S(1)} %get-tuple-element.10.keep, f32[8,8,1]{2,1,0:T(8,128)S(1)} %get-tuple-element.11.follow, ...), custom_call_target="tpu_custom_call" | custom-call | tf_op jit(solution)/shard_map/pallas_call | solution.py:403
  20.6 0.0 copy-start
  20.6 0.0 copy-start.6
  20.6 28.5 %all_to_all.20.received = bf16[32,2,16,256]{3,2,1,0:T(8,128)(2,1)S(1)} all-to-all(bf16[32,2,16,256]{3,2,1,0:T(8,128)(2,1)S(1)} %shard_map.142), channel_id=1, replica_groups=mesh['half'=2,'ring'=4,'space'=32] {'space'}, dimensions={0} | all-to-all | bytes 1048576 | tf_op jit(solution)/shard_map/all_to_all | solution.py:416
  49.1 0.0 copy-done
  49.1 0.0 copy-done.6
  49.1 2.1 %shard_map.143 = bf16[4,64,512]{2,1,0:T(8,128)(2,1)S(1)} custom-call(s32[2]{0:T(128)S(1)} %pad_add_fusion.spot, bf16[32,2,16,256]{3,2,1,0:T(8,128)(2,1)S(1)} %all_to_all.20.received, bf16[2,2,8,16,512]{4,3,2,1,0:T(8,128)(2,1)S(1)} %copy-done, bf16[16,12,512]{2,1,0:T(8,128)(2,1)S(1)} %collective-permute-done.halo, bf16[512,512]{1,0:T(8,128)(2,1)S(1)} %copy-done.4, ...), custom_call_target="tpu_custom_call" | custom-call | tf_op jit(solution)/shard_map/pallas_call | solution.py:403
  51.3 10.4 %all_to_all.21 = bf16[4,64,512]{2,1,0:T(8,128)(2,1)S(1)} all-to-all(bf16[4,64,512]{2,1,0:T(8,128)(2,1)S(1)} %shard_map.143), channel_id=1, replica_groups=mesh['half'=2,'ring'=4,'space'=32] {'ring'}, dimensions={0} | all-to-all | bytes 524288 | tf_op jit(solution)/shard_map/all_to_all | solution.py:416
  61.7 0.0 copy-start.8
  61.8 0.0 copy-start.7
  61.8 0.0 copy-start.9
  61.8 0.0 copy-start.10
  61.8 4.3 %collective-permute-start.1 = (bf16[64,512]{1,0:T(8,128)(2,1)S(1)}, bf16[64,512]{1,0:T(8,128)(2,1)S(1)}, u32[]{:S(2)}, u32[]{:S(2)}) collective-permute-start(bf16[64,512]{1,0:T(8,128)(2,1)S(1)} %reduce_sum.12), channel_id=1, source_target_pairs={{0,128},{32,160},{64,192},{96,224},{97,225},{1,129},{33,161},{65,1... | collective-permute-start | bytes 196616 | tf_op jit(solution)/shard_map/ppermute | solution.py:493
  66.1 2.8 %collective-permute-done.1 = bf16[64,512]{1,0:T(8,128)(2,1)S(1)} collective-permute-done((bf16[64,512]{1,0:T(8,128)(2,1)S(1)}, bf16[64,512]{1,0:T(8,128)(2,1)S(1)}, u32[]{:S(2)}, u32[]{:S(2)}) %collective-permute-start.1) | collective-permute-done | bytes 65568 | tf_op jit(solution)/shard_map/ppermute | solution.py:493
  68.9 0.4 collective-permute-start.2
  69.3 0.0 copy-done.8
  69.3 0.0 copy-done.7
  69.3 0.0 copy-done.9
  69.3 0.0 copy-done.10
  69.3 0.8 shard_map.144
  70.1 3.2 %collective-permute-done.2.previous = bf16[64,512]{1,0:T(8,128)(2,1)S(1)} collective-permute-done((bf16[64,512]{1,0:T(8,128)(2,1)S(1)}, bf16[64,512]{1,0:T(8,128)(2,1)S(1)}, u32[]{:S(2)}, u32[]{:S(2)}) %collective-permute-start.2) | collective-permute-done | bytes 65568 | tf_op jit(solution)/shard_map/ppermute | solution.py:495
  73.3 0.0 copy-start.2
  73.3 0.0 copy-start.3
  73.3 2.9 %shard_map.145 = bf16[4,64,512]{2,1,0:T(8,128)(2,1)S(1)} custom-call(s32[2]{0:T(128)S(1)} %pad_add_fusion.spot, bf16[64,512]{1,0:T(8,128)(2,1)S(1)} %collective-permute-done.2.previous, bf16[64,512]{1,0:T(8,128)(2,1)S(1)} %add_convert_fusion.own, bf16[384,144]{1,0:T(8,128)(2,1)S(1)} %get-tuple-element.14.w1, bf16[72,384]{1,0:T(8,128)(2,1)S(1)} %get-tuple-element.15.w2), custom_call_target="tpu_custom_call" | custom-call | tf_op jit(solution)/shard_map/pallas_call | solution.py:403
  76.3 7.9 %all_to_all.22.gathered = bf16[4,64,512]{2,1,0:T(8,128)(2,1)S(1)} all-to-all(bf16[4,64,512]{2,1,0:T(8,128)(2,1)S(1)} %shard_map.145), channel_id=1, replica_groups=mesh['half'=2,'ring'=4,'space'=32] {'ring'}, dimensions={0} | all-to-all | bytes 524288 | tf_op jit(solution)/shard_map/all_to_all | solution.py:416
  84.2 0.0 copy-done.2
  84.2 0.0 copy-done.3
  84.2 2.0 %shard_map.146 = (bf16[32,2,16,256]{3,2,1,0:T(8,128)(2,1)S(1)}, bf16[2,8,16,512]{3,2,1,0:T(8,128)(2,1)}) custom-call(s32[2]{0:T(128)S(1)} %pad_add_fusion.spot, bf16[4,64,512]{2,1,0:T(8,128)(2,1)S(1)} %all_to_all.22.gathered, bf16[2,2,8,16,512]{4,3,2,1,0:T(8,128)(2,1)S(1)} %copy-done, bf16[512,512]{1,0:T(8,128)(2,1)S(1)} %copy-done.2, ...), custom_call_target="tpu_custom_call" | custom-call | tf_op jit(solution)/shard_map/pallas_call | solution.py:403
  86.2 26.2 %all_to_all.23.received = bf16[32,2,16,256]{3,2,1,0:T(8,128)(2,1)S(1)} all-to-all(bf16[32,2,16,256]{3,2,1,0:T(8,128)(2,1)S(1)} %get-tuple-element.16), channel_id=1, replica_groups=mesh['half'=2,'ring'=4,'space'=32] {'space'}, dimensions={0} | all-to-all | bytes 1048576 | tf_op jit(solution)/shard_map/all_to_all | solution.py:416
  112.5 2.2 %shard_map.147 = bf16[2,2,8,16,512]{4,3,2,1,0:T(8,128)(2,1)} custom-call(bf16[32,2,16,256]{3,2,1,0:T(8,128)(2,1)S(1)} %all_to_all.23.received, bf16[2,2,8,16,512]{4,3,2,1,0:T(8,128)(2,1)S(1)} %copy-done.1, f32[8,16,1]{2,1,0:T(8,128)S(1)} %get-tuple-element.10.keep, bf16[512,512]{1,0:T(8,128)(2,1)S(1)} %copy-done.2, bf16[512,512]{1,0:T(8,128)(2,1)S(1)} %copy-done.3), custom_call_target="tpu_custom_call" | custom-call | tf_op jit(solution)/shard_map/pallas_call | solution.py:403
  (2 shorter events, 0.1 us)
Async XLA Ops:
  0.6 9.3 %copy-start.4 = (bf16[512,512]{1,0:T(8,128)(2,1)S(1)}, bf16[512,512]{1,0:T(8,128)(2,1)}, u32[]{:S(2)}) copy-start(bf16[512,512]{1,0:T(8,128)(2,1)} %constant.26.clone.far_cos.cos) | copy-start | bytes 1572868
  0.6 9.3 %copy-start.1 = (bf16[2,2,8,16,512]{4,3,2,1,0:T(8,128)(2,1)S(1)}, bf16[2,2,8,16,512]{4,3,2,1,0:T(8,128)(2,1)}, u32[]{:S(2)}) copy-start(bf16[2,2,8,16,512]{4,3,2,1,0:T(8,128)(2,1)} %measured.5) | copy-start | bytes 1572868
  2.6 7.4 %collective-permute-start = (bf16[16,12,512]{2,1,0:T(8,128)(2,1)}, bf16[16,12,512]{2,1,0:T(8,128)(2,1)S(1)}, u32[]{:S(2)}, u32[]{:S(2)}) collective-permute-start(bf16[16,12,512]{2,1,0:T(8,128)(2,1)} %shard_map.140), channel_id=1, source_target_pairs={{1,0},{2,1},{3,2},{4,3},{5,4},{6,5},{7,6},{8,7},{9,8},{10,9},{11,1... | collective-permute-start | bytes 589832 | tf_op jit(solution)/shard_map/ppermute | solution.py:439
  5.8 0.7 copy-start.13
  5.9 0.7 copy-start.11
  5.9 0.7 copy-start.12
  9.9 1.0 copy-start.5
  20.6 28.6 %copy-start = (bf16[2,2,8,16,512]{4,3,2,1,0:T(8,128)(2,1)S(1)}, bf16[2,2,8,16,512]{4,3,2,1,0:T(8,128)(2,1)}, u32[]{:S(2)}) copy-start(bf16[2,2,8,16,512]{4,3,2,1,0:T(8,128)(2,1)} %sens.5) | copy-start | bytes 1572868
  20.6 28.5 %copy-start.6 = (bf16[512,512]{1,0:T(8,128)(2,1)S(1)}, bf16[512,512]{1,0:T(8,128)(2,1)}, u32[]{:S(2)}) copy-start(bf16[512,512]{1,0:T(8,128)(2,1)} %constant.27.clone.far_sin.sin) | copy-start | bytes 1572868
  61.7 7.6 %copy-start.8 = (bf16[3,72,108]{2,1,0:T(8,128)(2,1)S(1)}, bf16[3,72,108]{2,1,0:T(8,128)(2,1)}, u32[]{:S(2)}) copy-start(bf16[3,72,108]{2,1,0:T(8,128)(2,1)} %constant.29.clone.band2) | copy-start | bytes 139972
  61.8 7.5 %copy-start.7 = (bf16[6,54,144]{2,1,0:T(8,128)(2,1)S(1)}, bf16[6,54,144]{2,1,0:T(8,128)(2,1)}, u32[]{:S(2)}) copy-start(bf16[6,54,144]{2,1,0:T(8,128)(2,1)} %constant.28.clone.band1) | copy-start | bytes 279940
  61.8 7.5 %copy-start.9 = (bf16[64,2,3,3,3]{0,1,4,3,2:T(2,128)(2,1)S(1)}, bf16[64,2,3,3,3]{0,1,4,3,2:T(2,128)(2,1)}, u32[]{:S(2)}) copy-start(bf16[64,2,3,3,3]{0,1,4,3,2:T(2,128)(2,1)} %param.18) | copy-start | bytes 20740
  61.8 7.5 %copy-start.10 = (bf16[2,64,3,3,3]{1,0,4,3,2:T(2,128)(2,1)S(1)}, bf16[2,64,3,3,3]{1,0,4,3,2:T(2,128)(2,1)}, u32[]{:S(2)}) copy-start(bf16[2,64,3,3,3]{1,0,4,3,2:T(2,128)(2,1)} %param.19) | copy-start | bytes 20740
  61.8 7.1 %collective-permute-start.1 = (bf16[64,512]{1,0:T(8,128)(2,1)S(1)}, bf16[64,512]{1,0:T(8,128)(2,1)S(1)}, u32[]{:S(2)}, u32[]{:S(2)}) collective-permute-start(bf16[64,512]{1,0:T(8,128)(2,1)S(1)} %reduce_sum.12), channel_id=1, source_target_pairs={{0,128},{32,160},{64,192},{96,224},{97,225},{1,129},{33,161},{65,1... | collective-permute-start | bytes 196616 | tf_op jit(solution)/shard_map/ppermute | solution.py:493
  68.9 4.4 %collective-permute-start.2 = (bf16[64,512]{1,0:T(8,128)(2,1)S(1)}, bf16[64,512]{1,0:T(8,128)(2,1)S(1)}, u32[]{:S(2)}, u32[]{:S(2)}) collective-permute-start(bf16[64,512]{1,0:T(8,128)(2,1)S(1)} %add_convert_fusion.own), channel_id=1, source_target_pairs={{0,32},{32,64},{64,96},{96,97},{97,1},{1,33},{33,65},{65,66},{66,9... | collective-permute-start | bytes 196616 | tf_op jit(solution)/shard_map/ppermute | solution.py:495
  73.3 10.8 %copy-start.2 = (bf16[512,512]{1,0:T(8,128)(2,1)S(1)}, bf16[512,512]{1,0:T(8,128)(2,1)}, u32[]{:S(2)}) copy-start(bf16[512,512]{1,0:T(8,128)(2,1)} %constant.24.clone.cos) | copy-start | bytes 1572868
  73.3 10.8 %copy-start.3 = (bf16[512,512]{1,0:T(8,128)(2,1)S(1)}, bf16[512,512]{1,0:T(8,128)(2,1)}, u32[]{:S(2)}) copy-start(bf16[512,512]{1,0:T(8,128)(2,1)} %constant.25.clone.sin) | copy-start | bytes 1572868

commit v6 on v5

--- a/solution.py
+++ b/solution.py
@@ -19,12 +19,13 @@
 HALVES = 2
 PAIRS = COILS * SLICES
 LANES = PAIRS * ROWS
+MIB = 1024 * 1024
 HROWS = ROWS + 2
 UNROLL = 8
 BF = jnp.bfloat16
 F32 = jnp.float32
 VMEM = pl.BlockSpec(memory_space=pltpu.VMEM)
-SMEM = pl.BlockSpec(memory_space=pltpu.SMEM)
+HBM = pl.BlockSpec(memory_space=pltpu.HBM)
 NT = (((1,), (1,)), ((), ()))
 TN = (((0,), (0,)), ((), ()))
 
@@ -37,7 +38,8 @@
     factor = np.float32(1.0 / math.sqrt(N))
     cos, sin = (np.cos(angles) * factor).astype(BF), (np.sin(angles) * factor).astype(BF)
     late = (position + np.where(position % ROWS < 2, ROWS, 0)) % N
-    return cos, sin, cos[late], sin[late]
+    plain = np.stack([cos, sin])
+    return plain, plain[:, late]
 
 
 def iota(shape, dim):
@@ -60,8 +62,9 @@
     )
 
 
-def kspace_weights(spot, lines, first, second, w1, w2, keep, follow):
-    row = spot[0] * ROWS + iota((24, 128), 0)
+def kspace_weights(lines, first, second, table, w1, w2, keep, follow):
+    space = lax.axis_index("space")
+    row = space * ROWS + iota((24, 128), 0)
     row = jnp.where(iota((24, 128), 0) >= ROWS + 4, row - 4, row)
     row = jnp.where(row >= N, row - N, row)
     for s in range(SLICES):
@@ -69,7 +72,7 @@
         hit = jnp.max(hit, axis=1, keepdims=True)
         keep[s] = hit[:ROWS]
         follow[s] = hit[ROWS:]
-    whole = jnp.where(spot[0] == SPACE - 1, 0.0, 1.0)
+    whole = jnp.where(space == SPACE - 1, 0.0, 1.0)
     rest = iota((18, 128), 0)
     h_row = rest & 1
     p_row, q_row = split(rest >> 1, 3, 3)
@@ -214,15 +217,8 @@
         ).astype(BF)
 
 
-def kspace_kernel(
-    measured, halo, keep, follow, w1, w2, far_cos, far_sin, out, refined, cos, sin, sems, *scratch
-):
-    tables = [
-        pltpu.make_async_copy(source, target, sems.at[n])
-        for n, (source, target) in enumerate(((far_cos, cos), (far_sin, sin)))
-    ]
-    for table in tables:
-        table.start()
+def kspace_kernel(measured, halo, keep, follow, w1, w2, table, out, refined, *scratch):
+    cos, sin = table.at[0], table.at[1]
 
     def one(i, x3, hidden):
         c, s = i // SLICES, i % SLICES
@@ -261,8 +257,6 @@
         return carry
 
     lax.fori_loop(0, PAIRS // UNROLL, step, 0)
-    for table in tables:
-        table.wait()
     for part in range(2):
         rows = pl.ds(part * 256, 256)
         co, si = cos[rows, :], sin[rows, :]
@@ -272,7 +266,8 @@
         out[part * 16 : (part + 1) * 16, 1] = imag.astype(BF).reshape(16, 16, LANES)
 
 
-def combine_kernel(spot, received, sens, halo, cos, sin, out, left, image, partial):
+def combine_kernel(received, sens, halo, table, out, left, image, partial):
+    cos, sin = table.at[0], table.at[1]
     for c in range(COILS):
         regroup(received, left, c)
         rows = slice(c * 128, (c + 1) * 128)
@@ -295,7 +290,7 @@
                 pi = pi + wide(partial, 1, rows)
             put(partial, pr, 0, rows)
             put(partial, pi, 1, rows)
-    turn = RING - spot[0] % RING
+    turn = RING - lax.axis_index("space") % RING
     for x in range(ROWS):
         place = (x + 2) % ROWS
         both = jnp.concatenate(
@@ -304,15 +299,16 @@
         out[(x // 4 + turn) % RING, x % 4 * 16 : (x % 4 + 1) * 16] = both.astype(BF)
 
 
-def outer(spot):
-    quarter = (spot[0] + spot[1]) % RING
-    first = jnp.where((spot[0] == 0) & (quarter == 0), 0.0, 1.0)
-    last = jnp.where((spot[0] == SPACE - 1) & (quarter == RING - 1), 0.0, 1.0)
+def outer():
+    space = lax.axis_index("space")
+    quarter = (space + lax.axis_index("ring")) % RING
+    first = jnp.where((space == 0) & (quarter == 0), 0.0, 1.0)
+    last = jnp.where((space == SPACE - 1) & (quarter == RING - 1), 0.0, 1.0)
     return first, last
 
 
-def image_weights(spot, first, second, band1, band2, w1, w2):
-    edge = outer(spot)
+def image_weights(first, second, band1, band2, w1, w2):
+    edge = outer()
     matrix = rows_of(first, 3, 3, 3)
     for x in range(6):
         block = dot_tn(matrix, band1[x])
@@ -326,8 +322,8 @@
         w2[:, pair * 128 : (pair + 1) * 128] = dot(band2[pair], matrix).astype(BF)
 
 
-def image_kernel(spot, previous, own, w1, w2, out, rows8, x3, acc, fin):
-    edge = outer(spot)
+def image_kernel(previous, own, w1, w2, out, rows8, x3, acc, fin):
+    edge = outer()
     put(rows8, previous[0:32].astype(F32) * edge[0], slice(0, 32))
     put(rows8, previous[32:64].astype(F32), slice(32, 64))
     put(rows8, own[0:32].astype(F32), slice(64, 96))
@@ -358,8 +354,9 @@
             out[y, e * 16 : (e + 1) * 16] = value
 
 
-def expand_kernel(spot, gathered, sens, cos, sin, out, image_out, image, data):
-    turn = RING - spot[0] % RING
+def expand_kernel(gathered, sens, table, out, image_out, image, data):
+    cos, sin = table.at[0], table.at[1]
+    turn = RING - lax.axis_index("space") % RING
     for x in range(ROWS):
         both = gathered[(x // 4 + turn) % RING, x % 4 * 16 : (x % 4 + 1) * 16].astype(F32)
         for h in range(2):
@@ -383,7 +380,8 @@
         out[part * 16 : (part + 1) * 16, 1] = imag.astype(BF).reshape(16, 16, LANES)
 
 
-def finish_kernel(received, measured, keep, cos, sin, out, left):
+def finish_kernel(received, measured, keep, table, out, left):
+    cos, sin = table.at[0], table.at[1]
     for c in range(COILS):
         regroup(received, left, c)
         rows = slice(c * 128, (c + 1) * 128)
@@ -398,17 +396,15 @@
                 ).astype(BF)
 
 
-def call(kernel, shapes, scratch, scalars, *operands, far=0):
+def call(kernel, shapes, scratch, *operands, mib=12):
     single = not isinstance(shapes, list)
     return pl.pallas_call(
         kernel,
         out_shape=shapes,
-        in_specs=[SMEM] * scalars
-        + [VMEM] * (len(operands) - scalars - far)
-        + [pl.BlockSpec(memory_space=pl.ANY)] * far,
+        in_specs=[VMEM] * len(operands),
         out_specs=VMEM if single else [VMEM] * len(shapes),
         scratch_shapes=scratch,
-        compiler_params=pltpu.CompilerParams(vmem_limit_bytes=40 * 1024 * 1024),
+        compiler_params=pltpu.CompilerParams(vmem_limit_bytes=mib * MIB),
     )(*operands)
 
 
@@ -423,15 +419,13 @@
 def local(
     measured, sensitivity, sample_lines, kspace_first, kspace_second, image_first, image_second
 ):
-    space, ring = lax.axis_index("space"), lax.axis_index("ring")
-    cos, sin, lcos, lsin = (jnp.asarray(t) for t in dft_tables())
+    plain, late = (jnp.asarray(t) for t in dft_tables())
     iband1, iband2 = (jnp.asarray(t) for t in image_bands())
 
-    spot = jnp.stack([space, ring])
     rim = pl.pallas_call(
         pack_kernel,
         out_shape=arr(PAIRS, 12, N),
-        in_specs=[pl.BlockSpec(memory_space=pl.ANY)] * 2,
+        in_specs=[HBM] * 2,
         out_specs=VMEM,
         scratch_shapes=[pltpu.VMEM((COILS, 2, SLICES, 8, N), BF)] * 2
         + [pltpu.SemaphoreType.DMA((2,))],
@@ -447,22 +441,17 @@
             arr(SLICES, 8, 1, dtype=F32),
         ],
         [],
-        1,
-        spot, sample_lines, kspace_first.transpose(2, 3, 1, 0), kspace_second.transpose(2, 3, 0, 1),
+        sample_lines, kspace_first.transpose(2, 3, 1, 0), kspace_second.transpose(2, 3, 0, 1), late,
     )
     half_done = call(
         kspace_kernel,
         arr(SPACE, 2, ROWS, LANES),
         [
             pltpu.VMEM((2, LANES, N), BF),
-            pltpu.VMEM((N, N), BF),
-            pltpu.VMEM((N, N), BF),
-            pltpu.SemaphoreType.DMA((2,)),
         ]
         + [pltpu.VMEM((128, N), BF), pltpu.VMEM((HROWS * CH, N), BF)] * UNROLL,
-        0,
-        measured, halo, keep, follow, kw1, kw2, lcos, lsin,
-        far=2,
+        measured, halo, keep, follow, kw1, kw2, late,
+        mib=28,
     )
     half_done = spread(half_done, "space")
     partial = call(
@@ -473,8 +462,7 @@
             pltpu.VMEM((COILS, 2, 128, N), F32),
             pltpu.VMEM((2, 4, 128, 128), F32),
         ],
-        1,
-        spot, half_done, sensitivity, halo, lcos, lsin,
+        half_done, sensitivity, halo, late,
     )
     part = spread(partial, "ring").astype(F32).sum(axis=0).astype(BF)
 
@@ -497,8 +485,7 @@
         image_weights,
         [arr(6 * CH, 144), arr(72, 6 * CH)],
         [],
-        1,
-        spot, image_first.transpose(2, 3, 4, 1, 0), image_second.transpose(2, 3, 4, 0, 1), iband1, iband2,
+        image_first.transpose(2, 3, 4, 1, 0), image_second.transpose(2, 3, 4, 0, 1), iband1, iband2,
     )
     copies = call(
         image_kernel,
@@ -509,24 +496,21 @@
             pltpu.VMEM((SLICES * 24, N), F32),
             pltpu.VMEM((4, SLICES * 8, 128), F32),
         ],
-        1,
-        spot, previous, image_in, iw1, iw2,
+        previous, image_in, iw1, iw2,
     )
     gathered = spread(copies, "ring")
     midway, image_out = call(
         expand_kernel,
         [arr(SPACE, 2, ROWS, LANES), arr(2, SLICES, ROWS, N)],
         [pltpu.VMEM((2, 4, 128, 128), F32), pltpu.VMEM((2, LANES, N), BF)],
-        1,
-        spot, gathered, sensitivity, cos, sin,
+        gathered, sensitivity, plain,
     )
     midway = spread(midway, "space")
     kspace_out = call(
         finish_kernel,
         arr(COILS, 2, SLICES, ROWS, N),
         [pltpu.VMEM((2, LANES, N), BF)],
-        0,
-        midway, measured, keep, cos, sin,
+        midway, measured, keep, plain,
     )
     return kspace_out, image_out
 

time: 115 us -> 112 us (0.974)
  Pallas kernels: 22.5 us -> 19.4 us
  waiting for transfers between devices: 8.48 us -> 10.3 us
  local copies, waits for them, and re-layouts: 1.74 us -> 0.06 us
    pallas_call x8, Pallas kernels: 22.5 us -> 19.4 us  [the longest x7 17.5 us: call(): pl.pallas_call(kernel, out_shape=shapes, in_specs=[VMEM] * len(operands),...]
    unnamed x28 -> x22, local copies, waits for them, and re-layouts: 1.74 us -> 0.06 us
    ppermute x1, waiting for transfers between devices: 2.46 us -> 3.72 us  [local(): lax.ppermute(rim, 'space', [((i + 1) % SPACE, i) for i in range(SPACE)])]
where the time goes in v6:
time: 112 us
  blocking collectives  73.3 us (65%)
  Pallas kernels  19.4 us (17%)
  waiting for transfers between devices  10.3 us (9%)
  starting transfers between devices  7.94 us (7%)
    all_to_all x4, blocking collectives, spread(): return lax.all_to_all(array, axis, split_axis=0, concat_axis=0, tiled=True)  73.3 us
    pallas_call x7, Pallas kernels, call(): pl.pallas_call(kernel, out_shape=shapes, in_specs=[VMEM] * len(operands),...  17.5 us
    ppermute x1, starting transfers between devices, local(): other = lax.ppermute(part, axes, exchange)  4.3 us
    ppermute x1, waiting for transfers between devices, local(): previous = lax.ppermute(image_in, axes, forward)  3.74 us
    ppermute x1, waiting for transfers between devices, local(): lax.ppermute(rim, 'space', [((i + 1) % SPACE, i) for i in range(SPACE)])  3.72 us
    ppermute x1, starting transfers between devices, local(): lax.ppermute(rim, 'space', [((i + 1) % SPACE, i) for i in range(SPACE)])  3.28 us
    ppermute x1, waiting for transfers between devices, local(): other = lax.ppermute(part, axes, exchange)  2.81 us
  transfers between devices with their start and end apart: 3, of which 3 were waited for; matrix products, arithmetic and copies ran while one was open for 0% of the time, Pallas kernels for 1%

profile of v6, /device:TPU:1, one launch (start us, length us, event | category | flops | bytes accessed | tf_op | source)
XLA Modules:
  0.0 111.8 jit_solution(7659801727917509055)
XLA Ops:
  0.6 0.0 copy-start
  0.6 0.0 copy-start.8
  0.7 0.0 copy-start.9
  0.7 0.0 copy-start.10
  0.7 1.9 %shard_map.122 = bf16[16,12,512]{2,1,0:T(8,128)(2,1)} custom-call(bf16[2,2,8,16,512]{4,3,2,1,0:T(8,128)(2,1)} %measured.5, bf16[2,2,8,16,512]{4,3,2,1,0:T(8,128)(2,1)} %sens.5), custom_call_target="tpu_custom_call" | custom-call | tf_op jit(solution)/shard_map/pallas_call | solution.py:425
  2.6 3.3 %collective-permute-start = (bf16[16,12,512]{2,1,0:T(8,128)(2,1)}, bf16[16,12,512]{2,1,0:T(8,128)(2,1)S(1)}, u32[]{:S(2)}, u32[]{:S(2)}) collective-permute-start(bf16[16,12,512]{2,1,0:T(8,128)(2,1)} %shard_map.122), channel_id=1, source_target_pairs={{1,0},{2,1},{3,2},{4,3},{5,4},{6,5},{7,6},{8,7},{9,8},{10,9},{11,1... | collective-permute-start | bytes 589832 | tf_op jit(solution)/shard_map/ppermute | solution.py:433
  5.9 0.0 copy-done
  5.9 0.0 copy-done.8
  5.9 0.0 copy-done.9
  5.9 0.0 copy-done.10
  5.9 0.0 copy-start.2
  5.9 0.3 shard_map.123
  6.2 3.7 %collective-permute-done.halo = bf16[16,12,512]{2,1,0:T(8,128)(2,1)S(1)} collective-permute-done((bf16[16,12,512]{2,1,0:T(8,128)(2,1)}, bf16[16,12,512]{2,1,0:T(8,128)(2,1)S(1)}, u32[]{:S(2)}, u32[]{:S(2)}) %collective-permute-start) | collective-permute-done | bytes 196640 | tf_op jit(solution)/shard_map/ppermute | solution.py:433
  10.0 0.0 copy-done.2
  10.0 9.4 %shard_map.124 = bf16[32,2,16,256]{3,2,1,0:T(8,128)(2,1)S(1)} custom-call(bf16[2,2,8,16,512]{4,3,2,1,0:T(8,128)(2,1)S(1)} %copy-done.2, bf16[16,12,512]{2,1,0:T(8,128)(2,1)S(1)} %collective-permute-done.halo, f32[8,16,1]{2,1,0:T(8,128)S(1)} %get-tuple-element.10.keep, f32[8,8,1]{2,1,0:T(8,128)S(1)} %get-tuple-element.11.follow, ...), custom_call_target="tpu_custom_call" | custom-call | tf_op jit(solution)/shard_map/pallas_call | solution.py:401
  19.4 0.0 copy-start.1
  19.4 28.5 %all_to_all.20.received = bf16[32,2,16,256]{3,2,1,0:T(8,128)(2,1)S(1)} all-to-all(bf16[32,2,16,256]{3,2,1,0:T(8,128)(2,1)S(1)} %shard_map.124), channel_id=1, replica_groups=mesh['half'=2,'ring'=4,'space'=32] {'space'}, dimensions={0} | all-to-all | bytes 1048576 | tf_op jit(solution)/shard_map/all_to_all | solution.py:412
  47.9 0.0 copy-done.1
  47.9 1.5 %shard_map.125 = bf16[4,64,512]{2,1,0:T(8,128)(2,1)S(1)} custom-call(bf16[32,2,16,256]{3,2,1,0:T(8,128)(2,1)S(1)} %all_to_all.20.received, bf16[2,2,8,16,512]{4,3,2,1,0:T(8,128)(2,1)S(1)} %copy-done.1, bf16[16,12,512]{2,1,0:T(8,128)(2,1)S(1)} %collective-permute-done.halo, bf16[2,512,512]{2,1,0:T(8,128)(2,1)S(1)} %copy-done), custom_call_target="tpu_custom_call" | custom-call | tf_op jit(solution)/shard_map/pallas_call | solution.py:401
  49.5 0.0 copy-start.4
  49.5 0.0 copy-start.5
  49.5 0.0 copy-start.6
  49.5 0.0 copy-start.7
  49.5 10.5 %all_to_all.21 = bf16[4,64,512]{2,1,0:T(8,128)(2,1)S(1)} all-to-all(bf16[4,64,512]{2,1,0:T(8,128)(2,1)S(1)} %shard_map.125), channel_id=1, replica_groups=mesh['half'=2,'ring'=4,'space'=32] {'ring'}, dimensions={0} | all-to-all | bytes 524288 | tf_op jit(solution)/shard_map/all_to_all | solution.py:412
  60.1 0.0 copy-start.3
  60.1 4.3 %collective-permute-start.1 = (bf16[64,512]{1,0:T(8,128)(2,1)S(1)}, bf16[64,512]{1,0:T(8,128)(2,1)S(1)}, u32[]{:S(2)}, u32[]{:S(2)}) collective-permute-start(bf16[64,512]{1,0:T(8,128)(2,1)S(1)} %reduce_sum.12), channel_id=1, source_target_pairs={{0,128},{32,160},{64,192},{96,224},{97,225},{1,129},{33,161},{65,1... | collective-permute-start | bytes 196616 | tf_op jit(solution)/shard_map/ppermute | solution.py:481
  64.4 2.8 %collective-permute-done.1 = bf16[64,512]{1,0:T(8,128)(2,1)S(1)} collective-permute-done((bf16[64,512]{1,0:T(8,128)(2,1)S(1)}, bf16[64,512]{1,0:T(8,128)(2,1)S(1)}, u32[]{:S(2)}, u32[]{:S(2)}) %collective-permute-start.1) | collective-permute-done | bytes 65568 | tf_op jit(solution)/shard_map/ppermute | solution.py:481
  67.2 0.4 collective-permute-start.2
  67.6 0.0 copy-done.4
  67.6 0.0 copy-done.5
  67.6 0.0 copy-done.6
  67.6 0.0 copy-done.7
  67.6 0.3 shard_map.126
  67.9 3.7 %collective-permute-done.2.previous = bf16[64,512]{1,0:T(8,128)(2,1)S(1)} collective-permute-done((bf16[64,512]{1,0:T(8,128)(2,1)S(1)}, bf16[64,512]{1,0:T(8,128)(2,1)S(1)}, u32[]{:S(2)}, u32[]{:S(2)}) %collective-permute-start.2) | collective-permute-done | bytes 65568 | tf_op jit(solution)/shard_map/ppermute | solution.py:483
  71.7 2.4 %shard_map.127 = bf16[4,64,512]{2,1,0:T(8,128)(2,1)S(1)} custom-call(bf16[64,512]{1,0:T(8,128)(2,1)S(1)} %collective-permute-done.2.previous, bf16[64,512]{1,0:T(8,128)(2,1)S(1)} %add_convert_fusion.own, bf16[384,144]{1,0:T(8,128)(2,1)S(1)} %get-tuple-element.14.w1, bf16[72,384]{1,0:T(8,128)(2,1)S(1)} %get-tuple-element.15.w2), custom_call_target="tpu_custom_call" | custom-call | tf_op jit(solution)/shard_map/pallas_call | solution.py:401
  74.0 7.9 %all_to_all.22.gathered = bf16[4,64,512]{2,1,0:T(8,128)(2,1)S(1)} all-to-all(bf16[4,64,512]{2,1,0:T(8,128)(2,1)S(1)} %shard_map.127), channel_id=1, replica_groups=mesh['half'=2,'ring'=4,'space'=32] {'ring'}, dimensions={0} | all-to-all | bytes 524288 | tf_op jit(solution)/shard_map/all_to_all | solution.py:412
  82.0 0.0 copy-done.3
  82.0 1.4 %shard_map.128 = (bf16[32,2,16,256]{3,2,1,0:T(8,128)(2,1)S(1)}, bf16[2,8,16,512]{3,2,1,0:T(8,128)(2,1)}) custom-call(bf16[4,64,512]{2,1,0:T(8,128)(2,1)S(1)} %all_to_all.22.gathered, bf16[2,2,8,16,512]{4,3,2,1,0:T(8,128)(2,1)S(1)} %copy-done.1, bf16[2,512,512]{2,1,0:T(8,128)(2,1)S(1)} %copy-done.3), custom_call_target="tpu_custom_call" | custom-call | tf_op jit(solution)/shard_map/pallas_call | solution.py:401
  83.4 26.3 %all_to_all.23.received = bf16[32,2,16,256]{3,2,1,0:T(8,128)(2,1)S(1)} all-to-all(bf16[32,2,16,256]{3,2,1,0:T(8,128)(2,1)S(1)} %get-tuple-element.16), channel_id=1, replica_groups=mesh['half'=2,'ring'=4,'space'=32] {'space'}, dimensions={0} | all-to-all | bytes 1048576 | tf_op jit(solution)/shard_map/all_to_all | solution.py:412
  109.7 2.2 %shard_map.129 = bf16[2,2,8,16,512]{4,3,2,1,0:T(8,128)(2,1)} custom-call(bf16[32,2,16,256]{3,2,1,0:T(8,128)(2,1)S(1)} %all_to_all.23.received, bf16[2,2,8,16,512]{4,3,2,1,0:T(8,128)(2,1)S(1)} %copy-done.2, f32[8,16,1]{2,1,0:T(8,128)S(1)} %get-tuple-element.10.keep, bf16[2,512,512]{2,1,0:T(8,128)(2,1)S(1)} %copy-done.3), custom_call_target="tpu_custom_call" | custom-call | tf_op jit(solution)/shard_map/pallas_call | solution.py:401
  (2 shorter events, 0.1 us)
Async XLA Ops:
  0.6 5.2 %copy-start = (bf16[2,512,512]{2,1,0:T(8,128)(2,1)S(1)}, bf16[2,512,512]{2,1,0:T(8,128)(2,1)}, u32[]{:S(2)}) copy-start(bf16[2,512,512]{2,1,0:T(8,128)(2,1)} %constant.12.clone.table) | copy-start | bytes 3145732
  0.6 5.2 %copy-start.8 = (bf16[64,2,3,3]{0,1,3,2:T(2,128)(2,1)S(1)}, bf16[64,2,3,3]{0,1,3,2:T(2,128)(2,1)}, u32[]{:S(2)}) copy-start(bf16[64,2,3,3]{0,1,3,2:T(2,128)(2,1)} %param.14) | copy-start | bytes 6916
  0.7 5.2 %copy-start.9 = (bf16[2,64,3,3]{1,0,3,2:T(2,128)(2,1)S(1)}, bf16[2,64,3,3]{1,0,3,2:T(2,128)(2,1)}, u32[]{:S(2)}) copy-start(bf16[2,64,3,3]{1,0,3,2:T(2,128)(2,1)} %param.15) | copy-start | bytes 6916
  0.7 5.2 %copy-start.10 = (s32[8,128]{1,0:T(8,128)S(1)}, s32[8,128]{1,0:T(8,128)}, u32[]{:S(2)}) copy-start(s32[8,128]{1,0:T(8,128)} %lines.1) | copy-start | bytes 12292
  2.6 7.4 %collective-permute-start = (bf16[16,12,512]{2,1,0:T(8,128)(2,1)}, bf16[16,12,512]{2,1,0:T(8,128)(2,1)S(1)}, u32[]{:S(2)}, u32[]{:S(2)}) collective-permute-start(bf16[16,12,512]{2,1,0:T(8,128)(2,1)} %shard_map.122), channel_id=1, source_target_pairs={{1,0},{2,1},{3,2},{4,3},{5,4},{6,5},{7,6},{8,7},{9,8},{10,9},{11,1... | collective-permute-start | bytes 589832 | tf_op jit(solution)/shard_map/ppermute | solution.py:433
  5.9 4.1 %copy-start.2 = (bf16[2,2,8,16,512]{4,3,2,1,0:T(8,128)(2,1)S(1)}, bf16[2,2,8,16,512]{4,3,2,1,0:T(8,128)(2,1)}, u32[]{:S(2)}) copy-start(bf16[2,2,8,16,512]{4,3,2,1,0:T(8,128)(2,1)} %measured.5) | copy-start | bytes 1572868
  19.4 28.6 %copy-start.1 = (bf16[2,2,8,16,512]{4,3,2,1,0:T(8,128)(2,1)S(1)}, bf16[2,2,8,16,512]{4,3,2,1,0:T(8,128)(2,1)}, u32[]{:S(2)}) copy-start(bf16[2,2,8,16,512]{4,3,2,1,0:T(8,128)(2,1)} %sens.5) | copy-start | bytes 1572868
  49.5 18.1 %copy-start.4 = (bf16[6,54,144]{2,1,0:T(8,128)(2,1)S(1)}, bf16[6,54,144]{2,1,0:T(8,128)(2,1)}, u32[]{:S(2)}) copy-start(bf16[6,54,144]{2,1,0:T(8,128)(2,1)} %constant.13.clone.band1) | copy-start | bytes 279940
  49.5 18.1 %copy-start.5 = (bf16[3,72,108]{2,1,0:T(8,128)(2,1)S(1)}, bf16[3,72,108]{2,1,0:T(8,128)(2,1)}, u32[]{:S(2)}) copy-start(bf16[3,72,108]{2,1,0:T(8,128)(2,1)} %constant.14.clone.band2) | copy-start | bytes 139972
  49.5 18.1 %copy-start.6 = (bf16[64,2,3,3,3]{0,1,4,3,2:T(2,128)(2,1)S(1)}, bf16[64,2,3,3,3]{0,1,4,3,2:T(2,128)(2,1)}, u32[]{:S(2)}) copy-start(bf16[64,2,3,3,3]{0,1,4,3,2:T(2,128)(2,1)} %param.16) | copy-start | bytes 20740
  49.5 18.1 %copy-start.7 = (bf16[2,64,3,3,3]{1,0,4,3,2:T(2,128)(2,1)S(1)}, bf16[2,64,3,3,3]{1,0,4,3,2:T(2,128)(2,1)}, u32[]{:S(2)}) copy-start(bf16[2,64,3,3,3]{1,0,4,3,2:T(2,128)(2,1)} %param.17) | copy-start | bytes 20740
  60.1 21.9 %copy-start.3 = (bf16[2,512,512]{2,1,0:T(8,128)(2,1)S(1)}, bf16[2,512,512]{2,1,0:T(8,128)(2,1)}, u32[]{:S(2)}) copy-start(bf16[2,512,512]{2,1,0:T(8,128)(2,1)} %constant.11.clone.table) | copy-start | bytes 3145732
  60.1 7.1 %collective-permute-start.1 = (bf16[64,512]{1,0:T(8,128)(2,1)S(1)}, bf16[64,512]{1,0:T(8,128)(2,1)S(1)}, u32[]{:S(2)}, u32[]{:S(2)}) collective-permute-start(bf16[64,512]{1,0:T(8,128)(2,1)S(1)} %reduce_sum.12), channel_id=1, source_target_pairs={{0,128},{32,160},{64,192},{96,224},{97,225},{1,129},{33,161},{65,1... | collective-permute-start | bytes 196616 | tf_op jit(solution)/shard_map/ppermute | solution.py:481
  67.2 4.4 %collective-permute-start.2 = (bf16[64,512]{1,0:T(8,128)(2,1)S(1)}, bf16[64,512]{1,0:T(8,128)(2,1)S(1)}, u32[]{:S(2)}, u32[]{:S(2)}) collective-permute-start(bf16[64,512]{1,0:T(8,128)(2,1)S(1)} %add_convert_fusion.own), channel_id=1, source_target_pairs={{0,32},{32,64},{64,96},{96,97},{97,1},{1,33},{33,65},{65,66},{66,9... | collective-permute-start | bytes 196616 | tf_op jit(solution)/shard_map/ppermute | solution.py:483

commit v7 on v6

--- a/solution.py
+++ b/solution.py
@@ -21,6 +21,7 @@
 LANES = PAIRS * ROWS
 MIB = 1024 * 1024
 HROWS = ROWS + 2
+EARLY = 14
 UNROLL = 8
 BF = jnp.bfloat16
 F32 = jnp.float32
@@ -62,7 +63,34 @@
     )
 
 
-def kspace_weights(lines, first, second, table, w1, w2, keep, follow):
+def start_kernel(
+    far_measured, far_sens, far_lines, far_first, far_second,
+    rim, measured, w1, w2, w2b, keep, follow, sens, lines, first, second, sems,
+):
+    rows = pl.ds(0, 8)
+    copies = [
+        pltpu.make_async_copy(source, target, sems.at[n])
+        for n, (source, target) in enumerate(
+            (
+                (far_measured, measured),
+                (far_sens.at[:, :, :, rows, :], sens),
+                (far_lines, lines),
+                (far_first, first),
+                (far_second, second),
+            )
+        )
+    ]
+    for copy in copies:
+        copy.start()
+    for copy in copies:
+        copy.wait()
+    for i in range(PAIRS):
+        c, s = i // SLICES, i % SLICES
+        rim[i] = jnp.concatenate(
+            [measured[c, h, s].astype(F32)[:4] for h in range(2)]
+            + [sens[c, h, s].astype(F32)[:2] for h in range(2)],
+            axis=0,
+        ).astype(BF)
     space = lax.axis_index("space")
     row = space * ROWS + iota((24, 128), 0)
     row = jnp.where(iota((24, 128), 0) >= ROWS + 4, row - 4, row)
@@ -91,23 +119,33 @@
         across = ~late if r + 1 >= ROWS else late
         block = jnp.where(across, block * whole, block)
         w1[r * CH : (r + 1) * CH, :] = block.astype(BF)
-    line, lane = iota((96, 36), 0), iota((96, 36), 1)
+    matrix = doubled(rows_of(second, 3, 3))
+    place = iota((96, 36), 0) & 15
+    place = jnp.where(place < 2, place + ROWS, place)
+    band = second_band(place, 5)
+    for pair in range(EARLY // 2):
+        block = dot(jnp.where(band == 2 * pair, 1.0, 0.0).astype(BF), matrix)
+        w2[:, pair * 128 : (pair + 1) * 128] = block.astype(BF)
+    place = iota((48, 36), 0) & 7
+    place = jnp.where(place < 2, place + ROWS, jnp.where(place >= 6, place + 8, -64))
+    band = second_band(place, 4)
+    late = (iota((48, 128), 0) & 7) < 2
+    upper = iota((48, 128), 1) >= CH
+    for pair in range(EARLY // 2, HROWS // 2):
+        block = dot(jnp.where(band == 2 * pair, 1.0, 0.0).astype(BF), matrix)
+        beyond = 2 * pair + 1 + upper.astype(jnp.int32) >= ROWS
+        block = jnp.where(late != beyond, block * whole, block)
+        start = pair * 128 - EARLY * CH
+        w2b[:, start : start + 128] = block.astype(BF)
+
+
+def second_band(place, shift):
+    line, lane = iota(place.shape, 0), iota(place.shape, 1)
     parity, rest = split(lane, 18, 2)
     o_lane = rest & 1
     p_lane, q_lane = split(rest >> 1, 3, 3)
-    matrix = doubled(rows_of(second, 3, 3))
-    place = line & 15
-    place = jnp.where(place < 2, place + ROWS, place)
-    match = (line >> 5 == q_lane) & ((line >> 4) & 1 == o_lane)
-    pair_row = jnp.where(match, place + p_lane - 2 - parity, -1)
-    late = (iota((96, 128), 0) & 15) < 2
-    upper = iota((96, 128), 1) >= CH
-    for pair in range(HROWS // 2):
-        band = jnp.where(pair_row == 2 * pair, 1.0, 0.0).astype(BF)
-        block = dot(band, matrix)
-        beyond = 2 * pair + 1 + upper.astype(jnp.int32) >= ROWS
-        block = jnp.where(late != beyond, block * whole, block)
-        w2[:, pair * 128 : (pair + 1) * 128] = block.astype(BF)
+    match = (line >> shift == q_lane) & ((line >> (shift - 1)) & 1 == o_lane)
+    return jnp.where(match, place + p_lane - 2 - parity, -1)
 
 
 def image_bands():
@@ -199,64 +237,61 @@
                 ]
 
 
-def pack_kernel(measured, sens, out, mine, maps, sems):
-    copies = [
-        pltpu.make_async_copy(source.at[:, :, :, pl.ds(0, 8), :], target, sems.at[n])
-        for n, (source, target) in enumerate(((measured, mine), (sens, maps)))
-    ]
-    for copy in copies:
-        copy.start()
-    for copy in copies:
-        copy.wait()
-    for i in range(PAIRS):
-        c, s = i // SLICES, i % SLICES
-        out[i] = jnp.concatenate(
-            [mine[c, h, s].astype(F32)[:4] for h in range(2)]
-            + [maps[c, h, s].astype(F32)[:2] for h in range(2)],
-            axis=0,
-        ).astype(BF)
-
-
-def kspace_kernel(measured, halo, keep, follow, w1, w2, table, out, refined, *scratch):
-    cos, sin = table.at[0], table.at[1]
-
-    def one(i, x3, hidden):
+def unrolled(one):
+    def step(i, carry):
+        for k in range(UNROLL):
+            one(i * UNROLL + k, k)
+        return carry
+
+    lax.fori_loop(0, PAIRS // UNROLL, step, 0)
+
+
+def early_kernel(measured, keep, w1, w2, table, patches, total):
+    def one(i, k):
         c, s = i // SLICES, i % SLICES
         mask = keep[s] > 0
         own = jnp.concatenate(
             [jnp.where(mask, measured[c, h, s].astype(F32), 0.0) for h in range(2)], axis=0
         )
+        shifted = jnp.concatenate([before(own), own, after(own)], axis=0).astype(BF)
+        patches[i] = shifted
+        hidden = jnp.maximum(dot(w1[: EARLY * CH, :96], shifted).astype(BF), 0)
+        spread = dot(w2[...], hidden)
+        total[i] = own + before(spread[0:32]) + spread[32:64] + after(spread[64:96])
+
+    unrolled(one)
+
+
+def late_kernel(patches, total, halo, follow, w1, w2, table, out, refined, *scratch):
+    cos, sin = table.at[0], table.at[1]
+
+    def one(i, k):
+        x3 = scratch[k]
+        s = i % SLICES
         rim = jnp.where(follow[s] > 0, halo[i].astype(F32)[0:8], 0.0)
-        two = iota((8, N), 0) < 2
-        held = jnp.concatenate(
-            [
-                jnp.where(two, rim, own[0:8]),
-                own[8:16],
-                jnp.where(two, pltpu.roll(rim, 4, 0), own[16:24]),
-                own[24:32],
-            ],
-            axis=0,
-        )
-        x3[0:32] = before(own).astype(BF)
-        x3[32:64] = own.astype(BF)
-        x3[64:96] = after(own).astype(BF)
+        x3[0:96] = patches[i]
         x3[96:128] = jnp.concatenate(
             [before(rim), rim, after(rim), jnp.zeros_like(rim)], axis=0
         ).astype(BF)
-        hidden[...] = jnp.maximum(dot(w1[...], x3[...]).astype(BF), 0)
-        spread = dot(w2[...], hidden[...])
-        total = held + before(spread[0:32]) + spread[32:64] + after(spread[64:96])
-        total = total.astype(BF)
+        hidden = jnp.maximum(dot(w1[EARLY * CH :], x3[...]).astype(BF), 0)
+        spread = dot(w2[...], hidden)
+        more = before(spread[0:16]) + spread[16:32] + after(spread[32:48])
+        line = iota((8, N), 0)
         row = pl.multiple_of(i * 16, 16)
         for h in range(2):
-            refined[h, pl.ds(row, 16), :] = total[h * 16 : (h + 1) * 16]
-
-    def step(i, carry):
-        for k in range(UNROLL):
-            one(i * UNROLL + k, scratch[2 * k], scratch[2 * k + 1])
-        return carry
-
-    lax.fori_loop(0, PAIRS // UNROLL, step, 0)
+            extra = more[h * 8 : (h + 1) * 8]
+            rows = rim if h == 0 else pltpu.roll(rim, 4, 0)
+            done = total[i, h * 16 : (h + 1) * 16]
+            done = jnp.concatenate(
+                [
+                    jnp.where(line < 2, rows + extra, done[0:8]),
+                    jnp.where(line >= 6, done[8:16] + extra, done[8:16]),
+                ],
+                axis=0,
+            )
+            refined[h, pl.ds(row, 16), :] = done.astype(BF)
+
+    unrolled(one)
     for part in range(2):
         rows = pl.ds(part * 256, 256)
         co, si = cos[rows, :], sin[rows, :]
@@ -422,36 +457,52 @@
     plain, late = (jnp.asarray(t) for t in dft_tables())
     iband1, iband2 = (jnp.asarray(t) for t in image_bands())
 
-    rim = pl.pallas_call(
-        pack_kernel,
-        out_shape=arr(PAIRS, 12, N),
-        in_specs=[HBM] * 2,
-        out_specs=VMEM,
-        scratch_shapes=[pltpu.VMEM((COILS, 2, SLICES, 8, N), BF)] * 2
-        + [pltpu.SemaphoreType.DMA((2,))],
-    )(measured, sensitivity)
-    halo = lax.ppermute(rim, "space", [((i + 1) % SPACE, i) for i in range(SPACE)])
-
-    kw1, kw2, keep, follow = call(
-        kspace_weights,
-        [
+    eight = pltpu.VMEM((COILS, 2, SLICES, 8, N), BF)
+    small = pltpu.VMEM((3, 3, 2, CH), BF)
+    rim, near, kw1, kw2, kw2b, keep, follow = pl.pallas_call(
+        start_kernel,
+        out_shape=[
+            arr(PAIRS, 12, N),
+            arr(COILS, 2, SLICES, ROWS, N),
             arr(HROWS * CH, 128),
-            arr(96, HROWS * CH),
+            arr(96, EARLY * CH),
+            arr(48, (HROWS - EARLY) * CH),
             arr(SLICES, ROWS, 1, dtype=F32),
             arr(SLICES, 8, 1, dtype=F32),
         ],
+        in_specs=[HBM] * 5,
+        out_specs=[VMEM] * 7,
+        scratch_shapes=[
+            eight, pltpu.VMEM((SLICES, 128), jnp.int32), small, small,
+            pltpu.SemaphoreType.DMA((5,)),
+        ],
+        compiler_params=pltpu.CompilerParams(vmem_limit_bytes=12 * MIB),
+    )(
+        *(
+            pltpu.with_memory_space_constraint(v, pltpu.HBM)
+            for v in (
+                measured,
+                sensitivity,
+                sample_lines,
+                kspace_first.transpose(2, 3, 1, 0),
+                kspace_second.transpose(2, 3, 0, 1),
+            )
+        )
+    )
+    halo = lax.ppermute(rim, "space", [((i + 1) % SPACE, i) for i in range(SPACE)])
+    patches, total = call(
+        early_kernel,
+        [arr(PAIRS, 96, N), arr(PAIRS, 32, N, dtype=F32)],
         [],
-        sample_lines, kspace_first.transpose(2, 3, 1, 0), kspace_second.transpose(2, 3, 0, 1), late,
+        near, keep, kw1, kw2, late,
+        mib=28,
     )
     half_done = call(
-        kspace_kernel,
+        late_kernel,
         arr(SPACE, 2, ROWS, LANES),
-        [
-            pltpu.VMEM((2, LANES, N), BF),
-        ]
-        + [pltpu.VMEM((128, N), BF), pltpu.VMEM((HROWS * CH, N), BF)] * UNROLL,
-        measured, halo, keep, follow, kw1, kw2, late,
-        mib=28,
+        [pltpu.VMEM((2, LANES, N), BF)] + [pltpu.VMEM((128, N), BF)] * UNROLL,
+        patches, total, halo, follow, kw1, kw2b, late,
+        mib=20,
     )
     half_done = spread(half_done, "space")
     partial = call(

time: 112 us -> 107 us (0.955)
  waiting for transfers between devices: 10.3 us -> 6.56 us
  blocking collectives: 73.3 us -> 69.7 us
  Pallas kernels: 19.4 us -> 21.7 us
    ppermute x1, waiting for transfers between devices: 3.72 us -> 0.01 us  [local(): lax.ppermute(rim, 'space', [((i + 1) % SPACE, i) for i in range(SPACE)])]
    all_to_all x4, blocking collectives: 73.3 us -> 69.7 us  [spread(): return lax.all_to_all(array, axis, split_axis=0, concat_axis=0, tiled=True)]
    pallas_call x7, Pallas kernels: 17.5 us -> 20.1 us  [call(): pl.pallas_call(kernel, out_shape=shapes, in_specs=[VMEM] * len(operands),...]
  transfers between devices with their start and end apart: 3 -> 3, of which waited for: 3 -> 2; matrix products, arithmetic and copies ran while one was open for 0% -> 0% of each run, Pallas kernels for 1% -> 7%
where the time goes in v7:
time: 107 us
  blocking collectives  69.7 us (65%)
  Pallas kernels  21.7 us (20%)
  starting transfers between devices  7.94 us (7%)
  waiting for transfers between devices  6.56 us (6%)
    all_to_all x4, blocking collectives, spread(): return lax.all_to_all(array, axis, split_axis=0, concat_axis=0, tiled=True)  69.7 us
    pallas_call x7, Pallas kernels, call(): pl.pallas_call(kernel, out_shape=shapes, in_specs=[VMEM] * len(operands),...  20.1 us
    ppermute x1, starting transfers between devices, local(): other = lax.ppermute(part, axes, exchange)  4.3 us
    ppermute x1, waiting for transfers between devices, local(): previous = lax.ppermute(image_in, axes, forward)  3.74 us
    ppermute x1, starting transfers between devices, local(): lax.ppermute(rim, 'space', [((i + 1) % SPACE, i) for i in range(SPACE)])  3.28 us
    ppermute x1, waiting for transfers between devices, local(): other = lax.ppermute(part, axes, exchange)  2.81 us
  transfers between devices with their start and end apart: 3, of which 2 were waited for; matrix products, arithmetic and copies ran while one was open for 0% of the time, Pallas kernels for 7%

profile of v7, /device:TPU:1, one launch (start us, length us, event | category | flops | bytes accessed | tf_op | source)
XLA Modules:
  0.0 106.8 jit_solution(14501638514249643377)
XLA Ops:
  0.6 0.0 copy-start
  0.6 1.6 %shard_map.122 = (bf16[16,12,512]{2,1,0:T(8,128)(2,1)S(1)}, bf16[2,2,8,16,512]{4,3,2,1,0:T(8,128)(2,1)S(1)}, bf16[1152,128]{1,0:T(8,128)(2,1)S(1)}, bf16[96,896]...) custom-call(bf16[2,2,8,16,512]{4,3,2,1,0:T(8,128)(2,1)} %measured.1, ...), custom_call_target="tpu_custom_call" | custom-call | tf_op jit(solution)/shard_map/pallas_call | solution.py:462
  2.3 3.3 %collective-permute-start = (bf16[16,12,512]{2,1,0:T(8,128)(2,1)S(1)}, bf16[16,12,512]{2,1,0:T(8,128)(2,1)S(1)}, u32[]{:S(2)}, u32[]{:S(2)}) collective-permute-start(bf16[16,12,512]{2,1,0:T(8,128)(2,1)S(1)} %get-tuple-element.21), channel_id=1, source_target_pairs={{1,0},{2,1},{3,2},{4,3},{5,4},{6,5},{7,6},{8,7},{9,8},{10,9},{11,1... | collective-permute-start | bytes 589832 | tf_op jit(solution)/shard_map/ppermute | solution.py:492
  5.6 0.0 copy-done
  5.6 7.3 %shard_map.123 = (bf16[16,96,512]{2,1,0:T(8,128)(2,1)S(1)}, f32[16,32,512]{2,1,0:T(8,128)S(1)}) custom-call(bf16[2,2,8,16,512]{4,3,2,1,0:T(8,128)(2,1)S(1)} %get-tuple-element.15.measured, f32[8,16,1]{2,1,0:T(8,128)S(1)} %get-tuple-element.16.keep, bf16[1152,128]{1,0:T(8,128)(2,1)S(1)} %get-tuple-element.17.w1, bf16[96,896]{1,0:T(8,128)(2,1)S(1)} %get-tuple-element.18.w2, ...), custom_call_target="tpu_custom_call" | custom-call | tf_op jit(solution)/shard_map/pallas_call | solution.py:436
  12.8 0.0 collective-permute-done.halo
  12.8 0.0 copy-start.1
  12.8 5.0 %shard_map.124 = bf16[32,2,16,256]{3,2,1,0:T(8,128)(2,1)S(1)} custom-call(bf16[16,96,512]{2,1,0:T(8,128)(2,1)S(1)} %get-tuple-element.19.patches, f32[16,32,512]{2,1,0:T(8,128)S(1)} %get-tuple-element.20.total, bf16[16,12,512]{2,1,0:T(8,128)(2,1)S(1)} %collective-permute-done.halo, f32[8,8,1]{2,1,0:T(8,128)S(1)} %get-tuple-element.22.follow, ...), custom_call_target="tpu_custom_call" | custom-call | tf_op jit(solution)/shard_map/pallas_call | solution.py:436
  17.9 25.0 %all_to_all.20.received = bf16[32,2,16,256]{3,2,1,0:T(8,128)(2,1)S(1)} all-to-all(bf16[32,2,16,256]{3,2,1,0:T(8,128)(2,1)S(1)} %shard_map.124), channel_id=1, replica_groups=mesh['half'=2,'ring'=4,'space'=32] {'space'}, dimensions={0} | all-to-all | bytes 1048576 | tf_op jit(solution)/shard_map/all_to_all | solution.py:447
  42.9 0.0 copy-done.1
  42.9 0.0 copy-start.4
  42.9 0.0 copy-start.5
  42.9 0.0 copy-start.6
  42.9 0.0 copy-start.7
  42.9 1.5 %shard_map.125 = bf16[4,64,512]{2,1,0:T(8,128)(2,1)S(1)} custom-call(bf16[32,2,16,256]{3,2,1,0:T(8,128)(2,1)S(1)} %all_to_all.20.received, bf16[2,2,8,16,512]{4,3,2,1,0:T(8,128)(2,1)S(1)} %copy-done.1, bf16[16,12,512]{2,1,0:T(8,128)(2,1)S(1)} %collective-permute-done.halo, bf16[2,512,512]{2,1,0:T(8,128)(2,1)S(1)} %copy-done), custom_call_target="tpu_custom_call" | custom-call | tf_op jit(solution)/shard_map/pallas_call | solution.py:436
  44.4 0.0 copy-start.2
  44.5 10.5 %all_to_all.21 = bf16[4,64,512]{2,1,0:T(8,128)(2,1)S(1)} all-to-all(bf16[4,64,512]{2,1,0:T(8,128)(2,1)S(1)} %shard_map.125), channel_id=1, replica_groups=mesh['half'=2,'ring'=4,'space'=32] {'ring'}, dimensions={0} | all-to-all | bytes 524288 | tf_op jit(solution)/shard_map/all_to_all | solution.py:447
  55.0 4.3 %collective-permute-start.1 = (bf16[64,512]{1,0:T(8,128)(2,1)S(1)}, bf16[64,512]{1,0:T(8,128)(2,1)S(1)}, u32[]{:S(2)}, u32[]{:S(2)}) collective-permute-start(bf16[64,512]{1,0:T(8,128)(2,1)S(1)} %reduce_sum.12), channel_id=1, source_target_pairs={{0,128},{32,160},{64,192},{96,224},{97,225},{1,129},{33,161},{65,1... | collective-permute-start | bytes 196616 | tf_op jit(solution)/shard_map/ppermute | solution.py:532
  59.3 2.8 %collective-permute-done.1 = bf16[64,512]{1,0:T(8,128)(2,1)S(1)} collective-permute-done((bf16[64,512]{1,0:T(8,128)(2,1)S(1)}, bf16[64,512]{1,0:T(8,128)(2,1)S(1)}, u32[]{:S(2)}, u32[]{:S(2)}) %collective-permute-start.1) | collective-permute-done | bytes 65568 | tf_op jit(solution)/shard_map/ppermute | solution.py:532
  62.2 0.4 collective-permute-start.2
  62.5 0.0 copy-done.4
  62.5 0.0 copy-done.5
  62.5 0.0 copy-done.6
  62.5 0.0 copy-done.7
  62.6 0.3 shard_map.126
  62.8 3.7 %collective-permute-done.2.previous = bf16[64,512]{1,0:T(8,128)(2,1)S(1)} collective-permute-done((bf16[64,512]{1,0:T(8,128)(2,1)S(1)}, bf16[64,512]{1,0:T(8,128)(2,1)S(1)}, u32[]{:S(2)}, u32[]{:S(2)}) %collective-permute-start.2) | collective-permute-done | bytes 65568 | tf_op jit(solution)/shard_map/ppermute | solution.py:534
  66.6 2.4 %shard_map.127 = bf16[4,64,512]{2,1,0:T(8,128)(2,1)S(1)} custom-call(bf16[64,512]{1,0:T(8,128)(2,1)S(1)} %collective-permute-done.2.previous, bf16[64,512]{1,0:T(8,128)(2,1)S(1)} %add_convert_fusion.own, bf16[384,144]{1,0:T(8,128)(2,1)S(1)} %get-tuple-element.24.w1, bf16[72,384]{1,0:T(8,128)(2,1)S(1)} %get-tuple-element.25.w2), custom_call_target="tpu_custom_call" | custom-call | tf_op jit(solution)/shard_map/pallas_call | solution.py:436
  69.0 7.9 %all_to_all.22.gathered = bf16[4,64,512]{2,1,0:T(8,128)(2,1)S(1)} all-to-all(bf16[4,64,512]{2,1,0:T(8,128)(2,1)S(1)} %shard_map.127), channel_id=1, replica_groups=mesh['half'=2,'ring'=4,'space'=32] {'ring'}, dimensions={0} | all-to-all | bytes 524288 | tf_op jit(solution)/shard_map/all_to_all | solution.py:447
  76.9 0.0 copy-done.2
  76.9 0.0 copy-start.3
  76.9 1.4 %shard_map.128 = (bf16[32,2,16,256]{3,2,1,0:T(8,128)(2,1)S(1)}, bf16[2,8,16,512]{3,2,1,0:T(8,128)(2,1)}) custom-call(bf16[4,64,512]{2,1,0:T(8,128)(2,1)S(1)} %all_to_all.22.gathered, bf16[2,2,8,16,512]{4,3,2,1,0:T(8,128)(2,1)S(1)} %copy-done.1, bf16[2,512,512]{2,1,0:T(8,128)(2,1)S(1)} %copy-done.2), custom_call_target="tpu_custom_call" | custom-call | tf_op jit(solution)/shard_map/pallas_call | solution.py:436
  78.3 26.3 %all_to_all.23.received = bf16[32,2,16,256]{3,2,1,0:T(8,128)(2,1)S(1)} all-to-all(bf16[32,2,16,256]{3,2,1,0:T(8,128)(2,1)S(1)} %get-tuple-element.26), channel_id=1, replica_groups=mesh['half'=2,'ring'=4,'space'=32] {'space'}, dimensions={0} | all-to-all | bytes 1048576 | tf_op jit(solution)/shard_map/all_to_all | solution.py:447
  104.6 0.0 copy-done.3
  104.6 2.1 %shard_map.129 = bf16[2,2,8,16,512]{4,3,2,1,0:T(8,128)(2,1)} custom-call(bf16[32,2,16,256]{3,2,1,0:T(8,128)(2,1)S(1)} %all_to_all.23.received, bf16[2,2,8,16,512]{4,3,2,1,0:T(8,128)(2,1)S(1)} %copy-done.3, f32[8,16,1]{2,1,0:T(8,128)S(1)} %get-tuple-element.16.keep, bf16[2,512,512]{2,1,0:T(8,128)(2,1)S(1)} %copy-done.2), custom_call_target="tpu_custom_call" | custom-call | tf_op jit(solution)/shard_map/pallas_call | solution.py:436
  (2 shorter events, 0.1 us)
Async XLA Ops:
  0.6 4.9 %copy-start = (bf16[2,512,512]{2,1,0:T(8,128)(2,1)S(1)}, bf16[2,512,512]{2,1,0:T(8,128)(2,1)}, u32[]{:S(2)}) copy-start(bf16[2,512,512]{2,1,0:T(8,128)(2,1)} %constant.12.clone.table) | copy-start | bytes 3145732
  2.3 10.5 %collective-permute-start = (bf16[16,12,512]{2,1,0:T(8,128)(2,1)S(1)}, bf16[16,12,512]{2,1,0:T(8,128)(2,1)S(1)}, u32[]{:S(2)}, u32[]{:S(2)}) collective-permute-start(bf16[16,12,512]{2,1,0:T(8,128)(2,1)S(1)} %get-tuple-element.21), channel_id=1, source_target_pairs={{1,0},{2,1},{3,2},{4,3},{5,4},{6,5},{7,6},{8,7},{9,8},{10,9},{11,1... | collective-permute-start | bytes 589832 | tf_op jit(solution)/shard_map/ppermute | solution.py:492
  12.8 30.0 %copy-start.1 = (bf16[2,2,8,16,512]{4,3,2,1,0:T(8,128)(2,1)S(1)}, bf16[2,2,8,16,512]{4,3,2,1,0:T(8,128)(2,1)}, u32[]{:S(2)}) copy-start(bf16[2,2,8,16,512]{4,3,2,1,0:T(8,128)(2,1)} %sens.3) | copy-start | bytes 1572868
  42.9 19.7 %copy-start.4 = (bf16[6,54,144]{2,1,0:T(8,128)(2,1)S(1)}, bf16[6,54,144]{2,1,0:T(8,128)(2,1)}, u32[]{:S(2)}) copy-start(bf16[6,54,144]{2,1,0:T(8,128)(2,1)} %constant.13.clone.band1) | copy-start | bytes 279940
  42.9 19.7 %copy-start.5 = (bf16[3,72,108]{2,1,0:T(8,128)(2,1)S(1)}, bf16[3,72,108]{2,1,0:T(8,128)(2,1)}, u32[]{:S(2)}) copy-start(bf16[3,72,108]{2,1,0:T(8,128)(2,1)} %constant.14.clone.band2) | copy-start | bytes 139972
  42.9 19.7 %copy-start.6 = (bf16[64,2,3,3,3]{0,1,4,3,2:T(2,128)(2,1)S(1)}, bf16[64,2,3,3,3]{0,1,4,3,2:T(2,128)(2,1)}, u32[]{:S(2)}) copy-start(bf16[64,2,3,3,3]{0,1,4,3,2:T(2,128)(2,1)} %param.16) | copy-start | bytes 20740
  42.9 19.7 %copy-start.7 = (bf16[2,64,3,3,3]{1,0,4,3,2:T(2,128)(2,1)S(1)}, bf16[2,64,3,3,3]{1,0,4,3,2:T(2,128)(2,1)}, u32[]{:S(2)}) copy-start(bf16[2,64,3,3,3]{1,0,4,3,2:T(2,128)(2,1)} %param.17) | copy-start | bytes 20740
  44.4 32.4 %copy-start.2 = (bf16[2,512,512]{2,1,0:T(8,128)(2,1)S(1)}, bf16[2,512,512]{2,1,0:T(8,128)(2,1)}, u32[]{:S(2)}) copy-start(bf16[2,512,512]{2,1,0:T(8,128)(2,1)} %constant.11.clone.table) | copy-start | bytes 3145732
  55.0 7.1 %collective-permute-start.1 = (bf16[64,512]{1,0:T(8,128)(2,1)S(1)}, bf16[64,512]{1,0:T(8,128)(2,1)S(1)}, u32[]{:S(2)}, u32[]{:S(2)}) collective-permute-start(bf16[64,512]{1,0:T(8,128)(2,1)S(1)} %reduce_sum.12), channel_id=1, source_target_pairs={{0,128},{32,160},{64,192},{96,224},{97,225},{1,129},{33,161},{65,1... | collective-permute-start | bytes 196616 | tf_op jit(solution)/shard_map/ppermute | solution.py:532
  62.2 4.4 %collective-permute-start.2 = (bf16[64,512]{1,0:T(8,128)(2,1)S(1)}, bf16[64,512]{1,0:T(8,128)(2,1)S(1)}, u32[]{:S(2)}, u32[]{:S(2)}) collective-permute-start(bf16[64,512]{1,0:T(8,128)(2,1)S(1)} %add_convert_fusion.own), channel_id=1, source_target_pairs={{0,32},{32,64},{64,96},{96,97},{97,1},{1,33},{33,65},{65,66},{66,9... | collective-permute-start | bytes 196616 | tf_op jit(solution)/shard_map/ppermute | solution.py:534
  76.9 27.7 %copy-start.3 = (bf16[2,2,8,16,512]{4,3,2,1,0:T(8,128)(2,1)S(1)}, bf16[2,2,8,16,512]{4,3,2,1,0:T(8,128)(2,1)}, u32[]{:S(2)}) copy-start(bf16[2,2,8,16,512]{4,3,2,1,0:T(8,128)(2,1)} %measured.1) | copy-start | bytes 1572868

commit v8 on v7

--- a/solution.py
+++ b/solution.py
@@ -22,7 +22,9 @@
 MIB = 1024 * 1024
 HROWS = ROWS + 2
 EARLY = 14
-UNROLL = 8
+EARLY_GROUP = 1
+LATE_GROUP = 4
+LOOPS = 2
 BF = jnp.bfloat16
 F32 = jnp.float32
 VMEM = pl.BlockSpec(memory_space=pltpu.VMEM)
@@ -65,7 +67,7 @@
 
 def start_kernel(
     far_measured, far_sens, far_lines, far_first, far_second,
-    rim, measured, w1, w2, w2b, keep, follow, sens, lines, first, second, sems,
+    rim, measured, w1, w1b, w2, w2b, keep, follow, sens, lines, first, second, sems,
 ):
     rows = pl.ds(0, 8)
     copies = [
@@ -106,19 +108,21 @@
     p_row, q_row = split(rest >> 1, 3, 3)
     matrix = rows_of(first, 3, 3)
     lane = iota((18, 128), 1)
-    late = lane >= 96
-    rest = jnp.where(late, lane - 96, lane)
-    q_lane = jnp.where(late, rest >> 3, rest >> 5)
-    h_lane = jnp.where(late, (rest >> 2) & 1, (rest >> 4) & 1)
-    row = jnp.where(late, ROWS + (rest & 3), rest & 15)
-    hidden_row = jnp.where((h_row == h_lane) & (q_row == q_lane), row - p_row, -1)
-    late = iota((CH, 128), 1) >= 96
-    for r in range(HROWS):
-        band = jnp.where(hidden_row == r, 1.0, 0.0).astype(BF)
-        block = dot_tn(matrix, band)
-        across = ~late if r + 1 >= ROWS else late
+    band = first_band(h_row, p_row, q_row, lane >> 5, (lane >> 4) & 1, lane & 15)
+    for r in range(EARLY):
+        block = dot_tn(matrix, jnp.where(band == r, 1.0, 0.0).astype(BF))
+        w1[r * CH : (r + 1) * CH, :] = block[:, :96].astype(BF)
+    t = lane & 15
+    h_lane = jnp.where(t < 8, t >> 1, (t - 8) >> 2)
+    row = jnp.where(t < 8, ROWS - 2 + (t & 1), ROWS + (t & 3))
+    band = first_band(h_row, p_row, q_row, lane >> 4, h_lane, row)
+    following = (iota((CH, 128), 1) & 15) >= 8
+    for r in range(EARLY, HROWS):
+        block = dot_tn(matrix, jnp.where(band == r, 1.0, 0.0).astype(BF))
+        across = ~following if r + 1 >= ROWS else following
         block = jnp.where(across, block * whole, block)
-        w1[r * CH : (r + 1) * CH, :] = block.astype(BF)
+        start = (r - EARLY) * CH
+        w1b[start : start + CH, :] = block[:, :48].astype(BF)
     matrix = doubled(rows_of(second, 3, 3))
     place = iota((96, 36), 0) & 15
     place = jnp.where(place < 2, place + ROWS, place)
@@ -137,6 +141,10 @@
         block = jnp.where(late != beyond, block * whole, block)
         start = pair * 128 - EARLY * CH
         w2b[:, start : start + 128] = block.astype(BF)
+
+
+def first_band(h_row, p_row, q_row, q_lane, h_lane, row):
+    return jnp.where((h_row == h_lane) & (q_row == q_lane), row - p_row, -1)
 
 
 def second_band(place, shift):
@@ -237,61 +245,78 @@
                 ]
 
 
-def unrolled(one):
+def grouped(group, one):
     def step(i, carry):
-        for k in range(UNROLL):
-            one(i * UNROLL + k, k)
+        for k in range(PAIRS // LOOPS // group):
+            one([i * (PAIRS // LOOPS) + k * group + n for n in range(group)])
         return carry
 
-    lax.fori_loop(0, PAIRS // UNROLL, step, 0)
-
-
-def early_kernel(measured, keep, w1, w2, table, patches, total):
-    def one(i, k):
+    lax.fori_loop(0, LOOPS, step, 0)
+
+
+def side_by_side(blocks):
+    blocks = [jnp.concatenate([before(v), v, after(v)], axis=0).astype(BF) for v in blocks]
+    return jnp.concatenate(blocks, axis=1)
+
+
+def apart(spread, n):
+    third = spread.shape[0] // 3
+    left, middle, right = (
+        spread[q * third : (q + 1) * third, n * N : (n + 1) * N] for q in range(3)
+    )
+    return before(left) + middle + after(right)
+
+
+def early_kernel(measured, keep, w1, w2, table, tail, total):
+    def own_rows(i):
         c, s = i // SLICES, i % SLICES
         mask = keep[s] > 0
-        own = jnp.concatenate(
-            [jnp.where(mask, measured[c, h, s].astype(F32), 0.0) for h in range(2)], axis=0
+        return [jnp.where(mask, measured[c, h, s].astype(F32), 0.0) for h in range(2)]
+
+    def one(pairs):
+        owns = [own_rows(i) for i in pairs]
+        blocks = [jnp.concatenate(own, axis=0) for own in owns]
+        hidden = jnp.maximum(dot(w1[...], side_by_side(blocks)).astype(BF), 0)
+        spread = dot(w2[...], hidden)
+        for n, i in enumerate(pairs):
+            total[i] = blocks[n] + apart(spread, n)
+            tail[i] = jnp.concatenate(
+                [own[ROWS - 2 :] for own in owns[n]] + [jnp.zeros((4, N), F32)], axis=0
+            )
+
+    grouped(EARLY_GROUP, one)
+
+
+def late_kernel(tail, total, halo, follow, w1, w2, table, out, refined):
+    cos, sin = table.at[0], table.at[1]
+
+    def one(pairs):
+        rims = [
+            jnp.where(follow[i % SLICES] > 0, halo[i].astype(F32)[0:8], 0.0) for i in pairs
+        ]
+        patches = side_by_side(
+            [jnp.concatenate([tail[i], rim], axis=0) for i, rim in zip(pairs, rims)]
         )
-        shifted = jnp.concatenate([before(own), own, after(own)], axis=0).astype(BF)
-        patches[i] = shifted
-        hidden = jnp.maximum(dot(w1[: EARLY * CH, :96], shifted).astype(BF), 0)
+        hidden = jnp.maximum(dot(w1[...], patches).astype(BF), 0)
         spread = dot(w2[...], hidden)
-        total[i] = own + before(spread[0:32]) + spread[32:64] + after(spread[64:96])
-
-    unrolled(one)
-
-
-def late_kernel(patches, total, halo, follow, w1, w2, table, out, refined, *scratch):
-    cos, sin = table.at[0], table.at[1]
-
-    def one(i, k):
-        x3 = scratch[k]
-        s = i % SLICES
-        rim = jnp.where(follow[s] > 0, halo[i].astype(F32)[0:8], 0.0)
-        x3[0:96] = patches[i]
-        x3[96:128] = jnp.concatenate(
-            [before(rim), rim, after(rim), jnp.zeros_like(rim)], axis=0
-        ).astype(BF)
-        hidden = jnp.maximum(dot(w1[EARLY * CH :], x3[...]).astype(BF), 0)
-        spread = dot(w2[...], hidden)
-        more = before(spread[0:16]) + spread[16:32] + after(spread[32:48])
         line = iota((8, N), 0)
-        row = pl.multiple_of(i * 16, 16)
-        for h in range(2):
-            extra = more[h * 8 : (h + 1) * 8]
-            rows = rim if h == 0 else pltpu.roll(rim, 4, 0)
-            done = total[i, h * 16 : (h + 1) * 16]
-            done = jnp.concatenate(
-                [
-                    jnp.where(line < 2, rows + extra, done[0:8]),
-                    jnp.where(line >= 6, done[8:16] + extra, done[8:16]),
-                ],
-                axis=0,
-            )
-            refined[h, pl.ds(row, 16), :] = done.astype(BF)
-
-    unrolled(one)
+        for n, i in enumerate(pairs):
+            more = apart(spread, n)
+            row = i * 16 if isinstance(i, int) else pl.multiple_of(i * 16, 16)
+            for h in range(2):
+                extra = more[h * 8 : (h + 1) * 8]
+                rows = rims[n] if h == 0 else pltpu.roll(rims[n], 4, 0)
+                done = total[i, h * 16 : (h + 1) * 16]
+                done = jnp.concatenate(
+                    [
+                        jnp.where(line < 2, rows + extra, done[0:8]),
+                        jnp.where(line >= 6, done[8:16] + extra, done[8:16]),
+                    ],
+                    axis=0,
+                )
+                refined[h, pl.ds(row, 16), :] = done.astype(BF)
+
+    grouped(LATE_GROUP, one)
     for part in range(2):
         rows = pl.ds(part * 256, 256)
         co, si = cos[rows, :], sin[rows, :]
@@ -459,19 +484,20 @@
 
     eight = pltpu.VMEM((COILS, 2, SLICES, 8, N), BF)
     small = pltpu.VMEM((3, 3, 2, CH), BF)
-    rim, near, kw1, kw2, kw2b, keep, follow = pl.pallas_call(
+    rim, near, kw1, kw1b, kw2, kw2b, keep, follow = pl.pallas_call(
         start_kernel,
         out_shape=[
             arr(PAIRS, 12, N),
             arr(COILS, 2, SLICES, ROWS, N),
-            arr(HROWS * CH, 128),
+            arr(EARLY * CH, 96),
+            arr((HROWS - EARLY) * CH, 48),
             arr(96, EARLY * CH),
             arr(48, (HROWS - EARLY) * CH),
             arr(SLICES, ROWS, 1, dtype=F32),
             arr(SLICES, 8, 1, dtype=F32),
         ],
         in_specs=[HBM] * 5,
-        out_specs=[VMEM] * 7,
+        out_specs=[VMEM] * 8,
         scratch_shapes=[
             eight, pltpu.VMEM((SLICES, 128), jnp.int32), small, small,
             pltpu.SemaphoreType.DMA((5,)),
@@ -490,9 +516,9 @@
         )
     )
     halo = lax.ppermute(rim, "space", [((i + 1) % SPACE, i) for i in range(SPACE)])
-    patches, total = call(
+    tail, total = call(
         early_kernel,
-        [arr(PAIRS, 96, N), arr(PAIRS, 32, N, dtype=F32)],
+        [arr(PAIRS, 8, N, dtype=F32), arr(PAIRS, 32, N, dtype=F32)],
         [],
         near, keep, kw1, kw2, late,
         mib=28,
@@ -500,8 +526,8 @@
     half_done = call(
         late_kernel,
         arr(SPACE, 2, ROWS, LANES),
-        [pltpu.VMEM((2, LANES, N), BF)] + [pltpu.VMEM((128, N), BF)] * UNROLL,
-        patches, total, halo, follow, kw1, kw2b, late,
+        [pltpu.VMEM((2, LANES, N), BF)],
+        tail, total, halo, follow, kw1b, kw2b, late,
         mib=20,
     )
     half_done = spread(half_done, "space")

time: 107 us -> 106 us (level)
  Pallas kernels: 21.7 us -> 20.1 us
    pallas_call x7, Pallas kernels: 20.1 us -> 18.4 us  [call(): pl.pallas_call(kernel, out_shape=shapes, in_specs=[VMEM] * len(operands),...]
where the time goes in v8:
time: 106 us; the launch traced here: 105 us
  blocking collectives  70 us (66%)
  Pallas kernels  20.1 us (19%)
  starting transfers between devices  7.95 us (8%)
  waiting for transfers between devices  6.55 us (6%)
    all_to_all x4, blocking collectives, spread(): return lax.all_to_all(array, axis, split_axis=0, concat_axis=0, tiled=True)  70 us
    pallas_call x7, Pallas kernels, call(): pl.pallas_call(kernel, out_shape=shapes, in_specs=[VMEM] * len(operands),...  18.4 us
    ppermute x1, starting transfers between devices, local(): other = lax.ppermute(part, axes, exchange)  4.31 us
    ppermute x1, waiting for transfers between devices, local(): previous = lax.ppermute(image_in, axes, forward)  3.74 us
    ppermute x1, starting transfers between devices, local(): lax.ppermute(rim, 'space', [((i + 1) % SPACE, i) for i in range(SPACE)])  3.28 us
    ppermute x1, waiting for transfers between devices, local(): other = lax.ppermute(part, axes, exchange)  2.8 us
  transfers between devices with their start and end apart: 3, of which 2 were waited for; matrix products, arithmetic and copies ran while one was open for 0% of the time, Pallas kernels for 7%

profile of v8, /device:TPU:1, one launch (start us, length us, event | category | flops | bytes accessed | tf_op | source)
XLA Modules:
  0.0 105.4 jit_solution(11641097012815864776)
XLA Ops:
  0.6 0.0 copy-start
  0.6 1.6 %shard_map.122 = (bf16[16,12,512]{2,1,0:T(8,128)(2,1)S(1)}, bf16[2,2,8,16,512]{4,3,2,1,0:T(8,128)(2,1)S(1)}, bf16[896,96]{1,0:T(8,128)(2,1)S(1)}, bf16[256,48]{1...) custom-call(bf16[2,2,8,16,512]{4,3,2,1,0:T(8,128)(2,1)} %measured.1,, ...), custom_call_target="tpu_custom_call" | custom-call | tf_op jit(solution)/shard_map/pallas_call | solution.py:487
  2.3 3.3 %collective-permute-start = (bf16[16,12,512]{2,1,0:T(8,128)(2,1)S(1)}, bf16[16,12,512]{2,1,0:T(8,128)(2,1)S(1)}, u32[]{:S(2)}, u32[]{:S(2)}) collective-permute-start(bf16[16,12,512]{2,1,0:T(8,128)(2,1)S(1)} %get-tuple-element.22), channel_id=1, source_target_pairs={{1,0},{2,1},{3,2},{4,3},{5,4},{6,5},{7,6},{8,7},{9,8},{10,9},{11,1... | collective-permute-start | bytes 589832 | tf_op jit(solution)/shard_map/ppermute | solution.py:518
  5.6 0.0 copy-done
  5.6 7.3 %shard_map.123 = (f32[16,8,512]{2,1,0:T(8,128)S(1)}, f32[16,32,512]{2,1,0:T(8,128)S(1)}) custom-call(bf16[2,2,8,16,512]{4,3,2,1,0:T(8,128)(2,1)S(1)} %get-tuple-element.16.measured, f32[8,16,1]{2,1,0:T(8,128)S(1)} %get-tuple-element.17.keep, bf16[896,96]{1,0:T(8,128)(2,1)S(1)} %get-tuple-element.18.w1, bf16[96,896]{1,0:T(8,128)(2,1)S(1)} %get-tuple-element.19.w2, ...), custom_call_target="tpu_custom_call" | custom-call | tf_op jit(solution)/shard_map/pallas_call | solution.py:461
  12.8 0.0 collective-permute-done.halo
  12.8 3.4 %shard_map.124 = bf16[32,2,16,256]{3,2,1,0:T(8,128)(2,1)S(1)} custom-call(f32[16,8,512]{2,1,0:T(8,128)S(1)} %get-tuple-element.20.tail, f32[16,32,512]{2,1,0:T(8,128)S(1)} %get-tuple-element.21.total, bf16[16,12,512]{2,1,0:T(8,128)(2,1)S(1)} %collective-permute-done.halo, f32[8,8,1]{2,1,0:T(8,128)S(1)} %get-tuple-element.23.follow, ...), custom_call_target="tpu_custom_call" | custom-call | tf_op jit(solution)/shard_map/pallas_call | solution.py:461
  16.2 0.0 copy-start.1
  16.2 25.1 %all_to_all.20.received = bf16[32,2,16,256]{3,2,1,0:T(8,128)(2,1)S(1)} all-to-all(bf16[32,2,16,256]{3,2,1,0:T(8,128)(2,1)S(1)} %shard_map.124), channel_id=1, replica_groups=mesh['half'=2,'ring'=4,'space'=32] {'space'}, dimensions={0} | all-to-all | bytes 1048576 | tf_op jit(solution)/shard_map/all_to_all | solution.py:472
  41.3 0.0 copy-done.1
  41.3 1.5 %shard_map.125 = bf16[4,64,512]{2,1,0:T(8,128)(2,1)S(1)} custom-call(bf16[32,2,16,256]{3,2,1,0:T(8,128)(2,1)S(1)} %all_to_all.20.received, bf16[2,2,8,16,512]{4,3,2,1,0:T(8,128)(2,1)S(1)} %copy-done.1, bf16[16,12,512]{2,1,0:T(8,128)(2,1)S(1)} %collective-permute-done.halo, bf16[2,512,512]{2,1,0:T(8,128)(2,1)S(1)} %copy-done), custom_call_target="tpu_custom_call" | custom-call | tf_op jit(solution)/shard_map/pallas_call | solution.py:461
  42.9 0.0 copy-start.4
  42.9 0.0 copy-start.5
  42.9 0.0 copy-start.6
  42.9 0.0 copy-start.7
  42.9 10.5 %all_to_all.21 = bf16[4,64,512]{2,1,0:T(8,128)(2,1)S(1)} all-to-all(bf16[4,64,512]{2,1,0:T(8,128)(2,1)S(1)} %shard_map.125), channel_id=1, replica_groups=mesh['half'=2,'ring'=4,'space'=32] {'ring'}, dimensions={0} | all-to-all | bytes 524288 | tf_op jit(solution)/shard_map/all_to_all | solution.py:472
  53.5 0.0 copy-start.2
  53.5 4.3 %collective-permute-start.1 = (bf16[64,512]{1,0:T(8,128)(2,1)S(1)}, bf16[64,512]{1,0:T(8,128)(2,1)S(1)}, u32[]{:S(2)}, u32[]{:S(2)}) collective-permute-start(bf16[64,512]{1,0:T(8,128)(2,1)S(1)} %reduce_sum.12), channel_id=1, source_target_pairs={{0,128},{32,160},{64,192},{96,224},{97,225},{1,129},{33,161},{65,1... | collective-permute-start | bytes 196616 | tf_op jit(solution)/shard_map/ppermute | solution.py:558
  57.8 2.8 %collective-permute-done.1 = bf16[64,512]{1,0:T(8,128)(2,1)S(1)} collective-permute-done((bf16[64,512]{1,0:T(8,128)(2,1)S(1)}, bf16[64,512]{1,0:T(8,128)(2,1)S(1)}, u32[]{:S(2)}, u32[]{:S(2)}) %collective-permute-start.1) | collective-permute-done | bytes 65568 | tf_op jit(solution)/shard_map/ppermute | solution.py:558
  60.6 0.4 collective-permute-start.2
  61.0 0.0 copy-done.4
  61.0 0.0 copy-done.5
  61.0 0.0 copy-done.6
  61.0 0.0 copy-done.7
  61.0 0.3 shard_map.126
  61.3 3.7 %collective-permute-done.2.previous = bf16[64,512]{1,0:T(8,128)(2,1)S(1)} collective-permute-done((bf16[64,512]{1,0:T(8,128)(2,1)S(1)}, bf16[64,512]{1,0:T(8,128)(2,1)S(1)}, u32[]{:S(2)}, u32[]{:S(2)}) %collective-permute-start.2) | collective-permute-done | bytes 65568 | tf_op jit(solution)/shard_map/ppermute | solution.py:560
  65.1 2.4 %shard_map.127 = bf16[4,64,512]{2,1,0:T(8,128)(2,1)S(1)} custom-call(bf16[64,512]{1,0:T(8,128)(2,1)S(1)} %collective-permute-done.2.previous, bf16[64,512]{1,0:T(8,128)(2,1)S(1)} %add_convert_fusion.own, bf16[384,144]{1,0:T(8,128)(2,1)S(1)} %get-tuple-element.26.w1, bf16[72,384]{1,0:T(8,128)(2,1)S(1)} %get-tuple-element.27.w2), custom_call_target="tpu_custom_call" | custom-call | tf_op jit(solution)/shard_map/pallas_call | solution.py:461
  67.5 7.9 %all_to_all.22.gathered = bf16[4,64,512]{2,1,0:T(8,128)(2,1)S(1)} all-to-all(bf16[4,64,512]{2,1,0:T(8,128)(2,1)S(1)} %shard_map.127), channel_id=1, replica_groups=mesh['half'=2,'ring'=4,'space'=32] {'ring'}, dimensions={0} | all-to-all | bytes 524288 | tf_op jit(solution)/shard_map/all_to_all | solution.py:472
  75.4 0.0 copy-done.2
  75.4 1.4 %shard_map.128 = (bf16[32,2,16,256]{3,2,1,0:T(8,128)(2,1)S(1)}, bf16[2,8,16,512]{3,2,1,0:T(8,128)(2,1)}) custom-call(bf16[4,64,512]{2,1,0:T(8,128)(2,1)S(1)} %all_to_all.22.gathered, bf16[2,2,8,16,512]{4,3,2,1,0:T(8,128)(2,1)S(1)} %copy-done.1, bf16[2,512,512]{2,1,0:T(8,128)(2,1)S(1)} %copy-done.2), custom_call_target="tpu_custom_call" | custom-call | tf_op jit(solution)/shard_map/pallas_call | solution.py:461
  76.8 0.0 copy-start.3
  76.8 26.4 %all_to_all.23.received = bf16[32,2,16,256]{3,2,1,0:T(8,128)(2,1)S(1)} all-to-all(bf16[32,2,16,256]{3,2,1,0:T(8,128)(2,1)S(1)} %get-tuple-element.28), channel_id=1, replica_groups=mesh['half'=2,'ring'=4,'space'=32] {'space'}, dimensions={0} | all-to-all | bytes 1048576 | tf_op jit(solution)/shard_map/all_to_all | solution.py:472
  103.2 0.0 copy-done.3
  103.2 2.2 %shard_map.129 = bf16[2,2,8,16,512]{4,3,2,1,0:T(8,128)(2,1)} custom-call(bf16[32,2,16,256]{3,2,1,0:T(8,128)(2,1)S(1)} %all_to_all.23.received, bf16[2,2,8,16,512]{4,3,2,1,0:T(8,128)(2,1)S(1)} %copy-done.3, f32[8,16,1]{2,1,0:T(8,128)S(1)} %get-tuple-element.17.keep, bf16[2,512,512]{2,1,0:T(8,128)(2,1)S(1)} %copy-done.2), custom_call_target="tpu_custom_call" | custom-call | tf_op jit(solution)/shard_map/pallas_call | solution.py:461
  (2 shorter events, 0.1 us)
Async XLA Ops:
  0.6 4.9 %copy-start = (bf16[2,512,512]{2,1,0:T(8,128)(2,1)S(1)}, bf16[2,512,512]{2,1,0:T(8,128)(2,1)}, u32[]{:S(2)}) copy-start(bf16[2,512,512]{2,1,0:T(8,128)(2,1)} %constant.12.clone.table) | copy-start | bytes 3145732
  2.3 10.5 %collective-permute-start = (bf16[16,12,512]{2,1,0:T(8,128)(2,1)S(1)}, bf16[16,12,512]{2,1,0:T(8,128)(2,1)S(1)}, u32[]{:S(2)}, u32[]{:S(2)}) collective-permute-start(bf16[16,12,512]{2,1,0:T(8,128)(2,1)S(1)} %get-tuple-element.22), channel_id=1, source_target_pairs={{1,0},{2,1},{3,2},{4,3},{5,4},{6,5},{7,6},{8,7},{9,8},{10,9},{11,1... | collective-permute-start | bytes 589832 | tf_op jit(solution)/shard_map/ppermute | solution.py:518
  16.2 25.1 %copy-start.1 = (bf16[2,2,8,16,512]{4,3,2,1,0:T(8,128)(2,1)S(1)}, bf16[2,2,8,16,512]{4,3,2,1,0:T(8,128)(2,1)}, u32[]{:S(2)}) copy-start(bf16[2,2,8,16,512]{4,3,2,1,0:T(8,128)(2,1)} %sens.3) | copy-start | bytes 1572868
  42.9 18.1 %copy-start.4 = (bf16[6,54,144]{2,1,0:T(8,128)(2,1)S(1)}, bf16[6,54,144]{2,1,0:T(8,128)(2,1)}, u32[]{:S(2)}) copy-start(bf16[6,54,144]{2,1,0:T(8,128)(2,1)} %constant.13.clone.band1) | copy-start | bytes 279940
  42.9 18.1 %copy-start.5 = (bf16[3,72,108]{2,1,0:T(8,128)(2,1)S(1)}, bf16[3,72,108]{2,1,0:T(8,128)(2,1)}, u32[]{:S(2)}) copy-start(bf16[3,72,108]{2,1,0:T(8,128)(2,1)} %constant.14.clone.band2) | copy-start | bytes 139972
  42.9 18.1 %copy-start.6 = (bf16[64,2,3,3,3]{0,1,4,3,2:T(2,128)(2,1)S(1)}, bf16[64,2,3,3,3]{0,1,4,3,2:T(2,128)(2,1)}, u32[]{:S(2)}) copy-start(bf16[64,2,3,3,3]{0,1,4,3,2:T(2,128)(2,1)} %param.16) | copy-start | bytes 20740
  42.9 18.1 %copy-start.7 = (bf16[2,64,3,3,3]{1,0,4,3,2:T(2,128)(2,1)S(1)}, bf16[2,64,3,3,3]{1,0,4,3,2:T(2,128)(2,1)}, u32[]{:S(2)}) copy-start(bf16[2,64,3,3,3]{1,0,4,3,2:T(2,128)(2,1)} %param.17) | copy-start | bytes 20740
  53.5 21.9 %copy-start.2 = (bf16[2,512,512]{2,1,0:T(8,128)(2,1)S(1)}, bf16[2,512,512]{2,1,0:T(8,128)(2,1)}, u32[]{:S(2)}) copy-start(bf16[2,512,512]{2,1,0:T(8,128)(2,1)} %constant.11.clone.table) | copy-start | bytes 3145732
  53.5 7.1 %collective-permute-start.1 = (bf16[64,512]{1,0:T(8,128)(2,1)S(1)}, bf16[64,512]{1,0:T(8,128)(2,1)S(1)}, u32[]{:S(2)}, u32[]{:S(2)}) collective-permute-start(bf16[64,512]{1,0:T(8,128)(2,1)S(1)} %reduce_sum.12), channel_id=1, source_target_pairs={{0,128},{32,160},{64,192},{96,224},{97,225},{1,129},{33,161},{65,1... | collective-permute-start | bytes 196616 | tf_op jit(solution)/shard_map/ppermute | solution.py:558
  60.6 4.4 %collective-permute-start.2 = (bf16[64,512]{1,0:T(8,128)(2,1)S(1)}, bf16[64,512]{1,0:T(8,128)(2,1)S(1)}, u32[]{:S(2)}, u32[]{:S(2)}) collective-permute-start(bf16[64,512]{1,0:T(8,128)(2,1)S(1)} %add_convert_fusion.own), channel_id=1, source_target_pairs={{0,32},{32,64},{64,96},{96,97},{97,1},{1,33},{33,65},{65,66},{66,9... | collective-permute-start | bytes 196616 | tf_op jit(solution)/shard_map/ppermute | solution.py:560
  76.8 26.4 %copy-start.3 = (bf16[2,2,8,16,512]{4,3,2,1,0:T(8,128)(2,1)S(1)}, bf16[2,2,8,16,512]{4,3,2,1,0:T(8,128)(2,1)}, u32[]{:S(2)}) copy-start(bf16[2,2,8,16,512]{4,3,2,1,0:T(8,128)(2,1)} %measured.1) | copy-start | bytes 1572868

commit v9 on v8

--- a/solution.py
+++ b/solution.py
@@ -24,6 +24,7 @@
 EARLY = 14
 EARLY_GROUP = 1
 LATE_GROUP = 4
+IMAGE_GROUP = 2
 LOOPS = 2
 BF = jnp.bfloat16
 F32 = jnp.float32
@@ -74,25 +75,18 @@
         pltpu.make_async_copy(source, target, sems.at[n])
         for n, (source, target) in enumerate(
             (
-                (far_measured, measured),
-                (far_sens.at[:, :, :, rows, :], sens),
                 (far_lines, lines),
                 (far_first, first),
                 (far_second, second),
+                (far_measured, measured),
+                (far_sens.at[:, :, :, rows, :], sens),
             )
         )
     ]
     for copy in copies:
         copy.start()
-    for copy in copies:
+    for copy in copies[:3]:
         copy.wait()
-    for i in range(PAIRS):
-        c, s = i // SLICES, i % SLICES
-        rim[i] = jnp.concatenate(
-            [measured[c, h, s].astype(F32)[:4] for h in range(2)]
-            + [sens[c, h, s].astype(F32)[:2] for h in range(2)],
-            axis=0,
-        ).astype(BF)
     space = lax.axis_index("space")
     row = space * ROWS + iota((24, 128), 0)
     row = jnp.where(iota((24, 128), 0) >= ROWS + 4, row - 4, row)
@@ -141,6 +135,15 @@
         block = jnp.where(late != beyond, block * whole, block)
         start = pair * 128 - EARLY * CH
         w2b[:, start : start + 128] = block.astype(BF)
+    for copy in copies[3:]:
+        copy.wait()
+    for i in range(PAIRS):
+        c, s = i // SLICES, i % SLICES
+        rim[i] = jnp.concatenate(
+            [measured[c, h, s].astype(F32)[:4] for h in range(2)]
+            + [sens[c, h, s].astype(F32)[:2] for h in range(2)],
+            axis=0,
+        ).astype(BF)
 
 
 def first_band(h_row, p_row, q_row, q_lane, h_lane, row):
@@ -231,14 +234,11 @@
 def regroup(received, left, coil):
     for octet in range(SPACE // 8):
         tiles = [
-            received[octet * 8 + i, :, :, coil * 128 : (coil + 1) * 128]
-            .astype(F32)
-            .reshape(32, 128)
+            received[octet * 8 + i, :, :, coil * 128 : (coil + 1) * 128].reshape(32, 128)
             for i in range(8)
         ]
         for s, tile in enumerate(blocks_swapped(tiles)):
             row = coil * 128 + s * 16
-            tile = tile.astype(BF)
             for h in range(2):
                 left[h, row : row + 16, octet * 128 : (octet + 1) * 128] = tile[
                     h * 16 : (h + 1) * 16
@@ -397,13 +397,18 @@
         x3[base + 16 : base + 32] = v.astype(BF)
         x3[base + 32 : base + 48] = after(v).astype(BF)
     acc[...] = jnp.zeros_like(acc)
-    for t in range(SLICES):
-        hidden = jnp.maximum(dot(w1[...], x3[t * 48 : t * 48 + 144]).astype(BF), 0)
+    for start in range(0, SLICES, IMAGE_GROUP):
+        group = range(start, start + IMAGE_GROUP)
+        patches = jnp.concatenate([x3[t * 48 : t * 48 + 144] for t in group], axis=1)
+        hidden = jnp.maximum(dot(w1[...], patches).astype(BF), 0)
         spread = dot(w2[...], hidden)
-        for a in range(3):
-            s = t + 1 - a
-            if 0 <= s < SLICES:
-                acc[s * 24 : (s + 1) * 24] = acc[s * 24 : (s + 1) * 24] + spread[a * 24 : (a + 1) * 24]
+        for t in group:
+            columns = slice((t - start) * N, (t - start + 1) * N)
+            for a in range(3):
+                s = t + 1 - a
+                if 0 <= s < SLICES:
+                    rows = slice(s * 24, (s + 1) * 24)
+                    acc[rows] = acc[rows] + spread[a * 24 : (a + 1) * 24, columns]
     for s in range(SLICES):
         v = acc[s * 24 : (s + 1) * 24]
         put(fin, before(v[0:8]) + v[8:16] + after(v[16:24]), slice(s * 8, (s + 1) * 8))
@@ -440,8 +445,10 @@
         out[part * 16 : (part + 1) * 16, 1] = imag.astype(BF).reshape(16, 16, LANES)
 
 
-def finish_kernel(received, measured, keep, table, out, left):
+def finish_kernel(received, measured, keep, table, image, out, image_out, left, done, sems):
     cos, sin = table.at[0], table.at[1]
+    copies = [pltpu.make_async_copy(image, image_out, sems.at[COILS])]
+    copies[0].start()
     for c in range(COILS):
         regroup(received, left, c)
         rows = slice(c * 128, (c + 1) * 128)
@@ -451,9 +458,13 @@
             mask = keep[s] > 0
             rows = slice(s * 16, (s + 1) * 16)
             for h, value in enumerate((real, imag)):
-                out[c, h, s] = jnp.where(
+                done[c, h, s] = jnp.where(
                     mask, measured[c, h, s].astype(F32), value[rows]
                 ).astype(BF)
+        copies.append(pltpu.make_async_copy(done.at[c], out.at[c], sems.at[c]))
+        copies[-1].start()
+    for copy in copies:
+        copy.wait()
 
 
 def call(kernel, shapes, scratch, *operands, mib=12):
@@ -583,12 +594,19 @@
         gathered, sensitivity, plain,
     )
     midway = spread(midway, "space")
-    kspace_out = call(
+    whole = arr(COILS, 2, SLICES, ROWS, N)
+    kspace_out, image_out = pl.pallas_call(
         finish_kernel,
-        arr(COILS, 2, SLICES, ROWS, N),
-        [pltpu.VMEM((2, LANES, N), BF)],
-        midway, measured, keep, plain,
-    )
+        out_shape=[whole, arr(2, SLICES, ROWS, N)],
+        in_specs=[VMEM] * 5,
+        out_specs=[HBM] * 2,
+        scratch_shapes=[
+            pltpu.VMEM((2, LANES, N), BF),
+            pltpu.VMEM(whole.shape, BF),
+            pltpu.SemaphoreType.DMA((COILS + 1,)),
+        ],
+        compiler_params=pltpu.CompilerParams(vmem_limit_bytes=12 * MIB),
+    )(midway, measured, keep, plain, image_out)
     return kspace_out, image_out
 
 

time: 106 us -> 104 us (0.981)
  Pallas kernels: 20.1 us -> 18.5 us
    pallas_call x7 -> x6, Pallas kernels: 18.4 us -> 15.1 us  [call(): pl.pallas_call(kernel, out_shape=shapes, in_specs=[VMEM] * len(operands),...]
    pallas_call x0 -> x1, Pallas kernels: none -> 1.97 us  [local(): pl.pallas_call(finish_kernel, out_shape=[whole, arr(2, SLICES, ROWS, N)],...]
where the time goes in v9:
time: 104 us
  blocking collectives  70 us (67%)
  Pallas kernels  18.5 us (18%)
  starting transfers between devices  7.94 us (8%)
  waiting for transfers between devices  6.56 us (6%)
    all_to_all x4, blocking collectives, spread(): return lax.all_to_all(array, axis, split_axis=0, concat_axis=0, tiled=True)  70 us
    pallas_call x6, Pallas kernels, call(): pl.pallas_call(kernel, out_shape=shapes, in_specs=[VMEM] * len(operands),...  15.1 us
    ppermute x1, starting transfers between devices, local(): other = lax.ppermute(part, axes, exchange)  4.3 us
    ppermute x1, waiting for transfers between devices, local(): previous = lax.ppermute(image_in, axes, forward)  3.74 us
    ppermute x1, starting transfers between devices, local(): lax.ppermute(rim, 'space', [((i + 1) % SPACE, i) for i in range(SPACE)])  3.28 us
    ppermute x1, waiting for transfers between devices, local(): other = lax.ppermute(part, axes, exchange)  2.81 us
  transfers between devices with their start and end apart: 3, of which 2 were waited for; matrix products, arithmetic and copies ran while one was open for 0% of the time, Pallas kernels for 7%

profile of v9, /device:TPU:1, one launch (start us, length us, event | category | flops | bytes accessed | tf_op | source)
XLA Modules:
  0.0 103.8 jit_solution(11079822623246800692)
XLA Ops:
  0.6 0.0 copy-start
  0.6 1.4 %shard_map.122 = (bf16[16,12,512]{2,1,0:T(8,128)(2,1)S(1)}, bf16[2,2,8,16,512]{4,3,2,1,0:T(8,128)(2,1)S(1)}, bf16[896,96]{1,0:T(8,128)(2,1)S(1)}, bf16[256,48]{1...) custom-call(bf16[2,2,8,16,512]{4,3,2,1,0:T(8,128)(2,1)} %measured.1,, ...), custom_call_target="tpu_custom_call" | custom-call | tf_op jit(solution)/shard_map/pallas_call | solution.py:498
  2.0 3.3 %collective-permute-start = (bf16[16,12,512]{2,1,0:T(8,128)(2,1)S(1)}, bf16[16,12,512]{2,1,0:T(8,128)(2,1)S(1)}, u32[]{:S(2)}, u32[]{:S(2)}) collective-permute-start(bf16[16,12,512]{2,1,0:T(8,128)(2,1)S(1)} %get-tuple-element.22), channel_id=1, source_target_pairs={{1,0},{2,1},{3,2},{4,3},{5,4},{6,5},{7,6},{8,7},{9,8},{10,9},{11,1... | collective-permute-start | bytes 589832 | tf_op jit(solution)/shard_map/ppermute | solution.py:529
  5.3 0.0 copy-done
  5.3 7.3 %shard_map.123 = (f32[16,8,512]{2,1,0:T(8,128)S(1)}, f32[16,32,512]{2,1,0:T(8,128)S(1)}) custom-call(bf16[2,2,8,16,512]{4,3,2,1,0:T(8,128)(2,1)S(1)} %get-tuple-element.16.measured, f32[8,16,1]{2,1,0:T(8,128)S(1)} %get-tuple-element.17.keep, bf16[896,96]{1,0:T(8,128)(2,1)S(1)} %get-tuple-element.18.w1, bf16[96,896]{1,0:T(8,128)(2,1)S(1)} %get-tuple-element.19.w2, ...), custom_call_target="tpu_custom_call" | custom-call | tf_op jit(solution)/shard_map/pallas_call | solution.py:472
  12.6 0.0 collective-permute-done.halo
  12.6 3.4 %shard_map.124 = bf16[32,2,16,256]{3,2,1,0:T(8,128)(2,1)S(1)} custom-call(f32[16,8,512]{2,1,0:T(8,128)S(1)} %get-tuple-element.20.tail, f32[16,32,512]{2,1,0:T(8,128)S(1)} %get-tuple-element.21.total, bf16[16,12,512]{2,1,0:T(8,128)(2,1)S(1)} %collective-permute-done.halo, f32[8,8,1]{2,1,0:T(8,128)S(1)} %get-tuple-element.23.follow, ...), custom_call_target="tpu_custom_call" | custom-call | tf_op jit(solution)/shard_map/pallas_call | solution.py:472
  15.9 0.0 copy-start.1
  15.9 25.1 %all_to_all.20.received = bf16[32,2,16,256]{3,2,1,0:T(8,128)(2,1)S(1)} all-to-all(bf16[32,2,16,256]{3,2,1,0:T(8,128)(2,1)S(1)} %shard_map.124), channel_id=1, replica_groups=mesh['half'=2,'ring'=4,'space'=32] {'space'}, dimensions={0} | all-to-all | bytes 1048576 | tf_op jit(solution)/shard_map/all_to_all | solution.py:483
  41.1 0.0 copy-done.1
  41.1 1.5 %shard_map.125 = bf16[4,64,512]{2,1,0:T(8,128)(2,1)S(1)} custom-call(bf16[32,2,16,256]{3,2,1,0:T(8,128)(2,1)S(1)} %all_to_all.20.received, bf16[2,2,8,16,512]{4,3,2,1,0:T(8,128)(2,1)S(1)} %copy-done.1, bf16[16,12,512]{2,1,0:T(8,128)(2,1)S(1)} %collective-permute-done.halo, bf16[2,512,512]{2,1,0:T(8,128)(2,1)S(1)} %copy-done), custom_call_target="tpu_custom_call" | custom-call | tf_op jit(solution)/shard_map/pallas_call | solution.py:472
  42.6 0.0 copy-start.4
  42.6 0.0 copy-start.5
  42.6 0.0 copy-start.6
  42.6 0.0 copy-start.7
  42.7 10.5 %all_to_all.21 = bf16[4,64,512]{2,1,0:T(8,128)(2,1)S(1)} all-to-all(bf16[4,64,512]{2,1,0:T(8,128)(2,1)S(1)} %shard_map.125), channel_id=1, replica_groups=mesh['half'=2,'ring'=4,'space'=32] {'ring'}, dimensions={0} | all-to-all | bytes 524288 | tf_op jit(solution)/shard_map/all_to_all | solution.py:483
  53.2 0.0 copy-start.2
  53.2 4.3 %collective-permute-start.1 = (bf16[64,512]{1,0:T(8,128)(2,1)S(1)}, bf16[64,512]{1,0:T(8,128)(2,1)S(1)}, u32[]{:S(2)}, u32[]{:S(2)}) collective-permute-start(bf16[64,512]{1,0:T(8,128)(2,1)S(1)} %reduce_sum.12), channel_id=1, source_target_pairs={{0,128},{32,160},{64,192},{96,224},{97,225},{1,129},{33,161},{65,1... | collective-permute-start | bytes 196616 | tf_op jit(solution)/shard_map/ppermute | solution.py:569
  57.5 2.8 %collective-permute-done.1 = bf16[64,512]{1,0:T(8,128)(2,1)S(1)} collective-permute-done((bf16[64,512]{1,0:T(8,128)(2,1)S(1)}, bf16[64,512]{1,0:T(8,128)(2,1)S(1)}, u32[]{:S(2)}, u32[]{:S(2)}) %collective-permute-start.1) | collective-permute-done | bytes 65568 | tf_op jit(solution)/shard_map/ppermute | solution.py:569
  60.4 0.4 collective-permute-start.2
  60.7 0.0 copy-done.4
  60.7 0.0 copy-done.5
  60.8 0.0 copy-done.6
  60.8 0.0 copy-done.7
  60.8 0.3 shard_map.126
  61.0 3.7 %collective-permute-done.2.previous = bf16[64,512]{1,0:T(8,128)(2,1)S(1)} collective-permute-done((bf16[64,512]{1,0:T(8,128)(2,1)S(1)}, bf16[64,512]{1,0:T(8,128)(2,1)S(1)}, u32[]{:S(2)}, u32[]{:S(2)}) %collective-permute-start.2) | collective-permute-done | bytes 65568 | tf_op jit(solution)/shard_map/ppermute | solution.py:571
  64.8 1.8 %shard_map.127 = bf16[4,64,512]{2,1,0:T(8,128)(2,1)S(1)} custom-call(bf16[64,512]{1,0:T(8,128)(2,1)S(1)} %collective-permute-done.2.previous, bf16[64,512]{1,0:T(8,128)(2,1)S(1)} %add_convert_fusion.own, bf16[384,144]{1,0:T(8,128)(2,1)S(1)} %get-tuple-element.26.w1, bf16[72,384]{1,0:T(8,128)(2,1)S(1)} %get-tuple-element.27.w2), custom_call_target="tpu_custom_call" | custom-call | tf_op jit(solution)/shard_map/pallas_call | solution.py:472
  66.6 7.9 %all_to_all.22.gathered = bf16[4,64,512]{2,1,0:T(8,128)(2,1)S(1)} all-to-all(bf16[4,64,512]{2,1,0:T(8,128)(2,1)S(1)} %shard_map.127), channel_id=1, replica_groups=mesh['half'=2,'ring'=4,'space'=32] {'ring'}, dimensions={0} | all-to-all | bytes 524288 | tf_op jit(solution)/shard_map/all_to_all | solution.py:483
  74.5 0.0 copy-done.2
  74.5 0.9 shard_map.128
  75.4 0.0 copy-start.3
  75.5 26.4 %all_to_all.23.received = bf16[32,2,16,256]{3,2,1,0:T(8,128)(2,1)S(1)} all-to-all(bf16[32,2,16,256]{3,2,1,0:T(8,128)(2,1)S(1)} %get-tuple-element.28), channel_id=1, replica_groups=mesh['half'=2,'ring'=4,'space'=32] {'space'}, dimensions={0} | all-to-all | bytes 1048576 | tf_op jit(solution)/shard_map/all_to_all | solution.py:483
  101.9 0.0 copy-done.3
  101.9 2.0 %shard_map.129 = (bf16[2,2,8,16,512]{4,3,2,1,0:T(8,128)(2,1)}, bf16[2,8,16,512]{3,2,1,0:T(8,128)(2,1)}) custom-call(bf16[32,2,16,256]{3,2,1,0:T(8,128)(2,1)S(1)} %all_to_all.23.received, bf16[2,2,8,16,512]{4,3,2,1,0:T(8,128)(2,1)S(1)} %copy-done.3, f32[8,16,1]{2,1,0:T(8,128)S(1)} %get-tuple-element.17.keep, bf16[2,512,512]{2,1,0:T(8,128)(2,1)S(1)} %copy-done.2, ...), custom_call_target="tpu_custom_call" | custom-call | tf_op jit(solution)/shard_map/pallas_call | solution.py:598
  (2 shorter events, 0.1 us)
Async XLA Ops:
  0.6 4.7 %copy-start = (bf16[2,512,512]{2,1,0:T(8,128)(2,1)S(1)}, bf16[2,512,512]{2,1,0:T(8,128)(2,1)}, u32[]{:S(2)}) copy-start(bf16[2,512,512]{2,1,0:T(8,128)(2,1)} %constant.12.clone.table) | copy-start | bytes 3145732
  2.0 10.5 %collective-permute-start = (bf16[16,12,512]{2,1,0:T(8,128)(2,1)S(1)}, bf16[16,12,512]{2,1,0:T(8,128)(2,1)S(1)}, u32[]{:S(2)}, u32[]{:S(2)}) collective-permute-start(bf16[16,12,512]{2,1,0:T(8,128)(2,1)S(1)} %get-tuple-element.22), channel_id=1, source_target_pairs={{1,0},{2,1},{3,2},{4,3},{5,4},{6,5},{7,6},{8,7},{9,8},{10,9},{11,1... | collective-permute-start | bytes 589832 | tf_op jit(solution)/shard_map/ppermute | solution.py:529
  15.9 25.1 %copy-start.1 = (bf16[2,2,8,16,512]{4,3,2,1,0:T(8,128)(2,1)S(1)}, bf16[2,2,8,16,512]{4,3,2,1,0:T(8,128)(2,1)}, u32[]{:S(2)}) copy-start(bf16[2,2,8,16,512]{4,3,2,1,0:T(8,128)(2,1)} %sens.3) | copy-start | bytes 1572868
  42.6 18.1 %copy-start.4 = (bf16[6,54,144]{2,1,0:T(8,128)(2,1)S(1)}, bf16[6,54,144]{2,1,0:T(8,128)(2,1)}, u32[]{:S(2)}) copy-start(bf16[6,54,144]{2,1,0:T(8,128)(2,1)} %constant.13.clone.band1) | copy-start | bytes 279940
  42.6 18.1 %copy-start.5 = (bf16[3,72,108]{2,1,0:T(8,128)(2,1)S(1)}, bf16[3,72,108]{2,1,0:T(8,128)(2,1)}, u32[]{:S(2)}) copy-start(bf16[3,72,108]{2,1,0:T(8,128)(2,1)} %constant.14.clone.band2) | copy-start | bytes 139972
  42.6 18.1 %copy-start.6 = (bf16[64,2,3,3,3]{0,1,4,3,2:T(2,128)(2,1)S(1)}, bf16[64,2,3,3,3]{0,1,4,3,2:T(2,128)(2,1)}, u32[]{:S(2)}) copy-start(bf16[64,2,3,3,3]{0,1,4,3,2:T(2,128)(2,1)} %param.16) | copy-start | bytes 20740
  42.6 18.1 %copy-start.7 = (bf16[2,64,3,3,3]{1,0,4,3,2:T(2,128)(2,1)S(1)}, bf16[2,64,3,3,3]{1,0,4,3,2:T(2,128)(2,1)}, u32[]{:S(2)}) copy-start(bf16[2,64,3,3,3]{1,0,4,3,2:T(2,128)(2,1)} %param.17) | copy-start | bytes 20740
  53.2 21.3 %copy-start.2 = (bf16[2,512,512]{2,1,0:T(8,128)(2,1)S(1)}, bf16[2,512,512]{2,1,0:T(8,128)(2,1)}, u32[]{:S(2)}) copy-start(bf16[2,512,512]{2,1,0:T(8,128)(2,1)} %constant.11.clone.table) | copy-start | bytes 3145732
  53.2 7.1 %collective-permute-start.1 = (bf16[64,512]{1,0:T(8,128)(2,1)S(1)}, bf16[64,512]{1,0:T(8,128)(2,1)S(1)}, u32[]{:S(2)}, u32[]{:S(2)}) collective-permute-start(bf16[64,512]{1,0:T(8,128)(2,1)S(1)} %reduce_sum.12), channel_id=1, source_target_pairs={{0,128},{32,160},{64,192},{96,224},{97,225},{1,129},{33,161},{65,1... | collective-permute-start | bytes 196616 | tf_op jit(solution)/shard_map/ppermute | solution.py:569
  60.4 4.4 %collective-permute-start.2 = (bf16[64,512]{1,0:T(8,128)(2,1)S(1)}, bf16[64,512]{1,0:T(8,128)(2,1)S(1)}, u32[]{:S(2)}, u32[]{:S(2)}) collective-permute-start(bf16[64,512]{1,0:T(8,128)(2,1)S(1)} %add_convert_fusion.own), channel_id=1, source_target_pairs={{0,32},{32,64},{64,96},{96,97},{97,1},{1,33},{33,65},{65,66},{66,9... | collective-permute-start | bytes 196616 | tf_op jit(solution)/shard_map/ppermute | solution.py:571
  75.4 26.4 %copy-start.3 = (bf16[2,2,8,16,512]{4,3,2,1,0:T(8,128)(2,1)S(1)}, bf16[2,2,8,16,512]{4,3,2,1,0:T(8,128)(2,1)}, u32[]{:S(2)}) copy-start(bf16[2,2,8,16,512]{4,3,2,1,0:T(8,128)(2,1)} %measured.1) | copy-start | bytes 1572868

commit v10 on v9

--- a/solution.py
+++ b/solution.py
@@ -382,12 +382,7 @@
         w2[:, pair * 128 : (pair + 1) * 128] = dot(band2[pair], matrix).astype(BF)
 
 
-def image_kernel(previous, own, w1, w2, out, rows8, x3, acc, fin):
-    edge = outer()
-    put(rows8, previous[0:32].astype(F32) * edge[0], slice(0, 32))
-    put(rows8, previous[32:64].astype(F32), slice(32, 64))
-    put(rows8, own[0:32].astype(F32), slice(64, 96))
-    put(rows8, own[32:64].astype(F32) * edge[1], slice(96, 128))
+def image_patches(rows8, x3):
     x3[0:48] = jnp.zeros((48, N), BF)
     x3[432:480] = jnp.zeros((48, N), BF)
     for s in range(SLICES):
@@ -396,12 +391,14 @@
         x3[base : base + 16] = before(v).astype(BF)
         x3[base + 16 : base + 32] = v.astype(BF)
         x3[base + 32 : base + 48] = after(v).astype(BF)
-    acc[...] = jnp.zeros_like(acc)
+
+
+def image_sums(x3, w1, w2, acc):
     for start in range(0, SLICES, IMAGE_GROUP):
         group = range(start, start + IMAGE_GROUP)
         patches = jnp.concatenate([x3[t * 48 : t * 48 + 144] for t in group], axis=1)
-        hidden = jnp.maximum(dot(w1[...], patches).astype(BF), 0)
-        spread = dot(w2[...], hidden)
+        hidden = jnp.maximum(dot(w1, patches).astype(BF), 0)
+        spread = dot(w2, hidden)
         for t in group:
             columns = slice((t - start) * N, (t - start + 1) * N)
             for a in range(3):
@@ -409,6 +406,26 @@
                 if 0 <= s < SLICES:
                     rows = slice(s * 24, (s + 1) * 24)
                     acc[rows] = acc[rows] + spread[a * 24 : (a + 1) * 24, columns]
+
+
+def image_early(own, w1, w2, acc, rows8, x3):
+    put(rows8, jnp.zeros((64, N), F32), slice(0, 64))
+    put(rows8, own[0:32].astype(F32), slice(64, 96))
+    put(rows8, own[32:64].astype(F32) * outer()[1], slice(96, 128))
+    image_patches(rows8, x3)
+    acc[...] = jnp.zeros_like(acc)
+    image_sums(x3, w1[4 * CH :], w2[:, 4 * CH :], acc)
+
+
+def image_late(previous, own, w1, w2, early, out, rows8, x3, acc, fin):
+    edge = outer()
+    put(rows8, previous[0:32].astype(F32) * edge[0], slice(0, 32))
+    put(rows8, previous[32:64].astype(F32), slice(32, 64))
+    put(rows8, own[0:32].astype(F32), slice(64, 96))
+    put(rows8, own[32:64].astype(F32) * edge[1], slice(96, 128))
+    image_patches(rows8, x3)
+    acc[...] = early[...]
+    image_sums(x3, w1[: 4 * CH], w2[:, : 4 * CH], acc)
     for s in range(SLICES):
         v = acc[s * 24 : (s + 1) * 24]
         put(fin, before(v[0:8]) + v[8:16] + after(v[16:24]), slice(s * 8, (s + 1) * 8))
@@ -575,16 +592,14 @@
         [],
         image_first.transpose(2, 3, 4, 1, 0), image_second.transpose(2, 3, 4, 0, 1), iband1, iband2,
     )
+    rooms = [pltpu.VMEM((4, 128, 128), F32), pltpu.VMEM((480, N), BF)]
+    early = call(image_early, arr(SLICES * 24, N, dtype=F32), rooms, image_in, iw1, iw2)
     copies = call(
-        image_kernel,
+        image_late,
         arr(RING, 64, N),
-        [
-            pltpu.VMEM((4, 128, 128), F32),
-            pltpu.VMEM((480, N), BF),
-            pltpu.VMEM((SLICES * 24, N), F32),
-            pltpu.VMEM((4, SLICES * 8, 128), F32),
-        ],
-        previous, image_in, iw1, iw2,
+        rooms
+        + [pltpu.VMEM((SLICES * 24, N), F32), pltpu.VMEM((4, SLICES * 8, 128), F32)],
+        previous, image_in, iw1, iw2, early,
     )
     gathered = spread(copies, "ring")
     midway, image_out = call(

time: 104 us -> 104 us (level)
  waiting for transfers between devices: 6.56 us -> 5.41 us
    ppermute x1, waiting for transfers between devices: 3.74 us -> 2.59 us  [local(): previous = lax.ppermute(image_in, axes, forward)]
    pallas_call x6 -> x7, Pallas kernels: 15.1 us -> 16 us  [call(): pl.pallas_call(kernel, out_shape=shapes, in_specs=[VMEM] * len(operands),...]
  transfers between devices with their start and end apart: 3 -> 3, of which waited for: 2 -> 2; matrix products, arithmetic and copies ran while one was open for 0% -> 0% of each run, Pallas kernels for 7% -> 8%
where the time goes in v10:
time: 104 us
  blocking collectives  69.9 us (67%)
  Pallas kernels  19.4 us (19%)
  starting transfers between devices  7.94 us (8%)
  waiting for transfers between devices  5.41 us (5%)
    all_to_all x4, blocking collectives, spread(): return lax.all_to_all(array, axis, split_axis=0, concat_axis=0, tiled=True)  69.9 us
    pallas_call x7, Pallas kernels, call(): pl.pallas_call(kernel, out_shape=shapes, in_specs=[VMEM] * len(operands),...  16 us
    ppermute x1, starting transfers between devices, local(): other = lax.ppermute(part, axes, exchange)  4.3 us
    ppermute x1, starting transfers between devices, local(): lax.ppermute(rim, 'space', [((i + 1) % SPACE, i) for i in range(SPACE)])  3.28 us
    ppermute x1, waiting for transfers between devices, local(): other = lax.ppermute(part, axes, exchange)  2.81 us
    ppermute x1, waiting for transfers between devices, local(): previous = lax.ppermute(image_in, axes, forward)  2.59 us
  transfers between devices with their start and end apart: 3, of which 2 were waited for; matrix products, arithmetic and copies ran while one was open for 0% of the time, Pallas kernels for 8%

profile of v10, /device:TPU:1, one launch (start us, length us, event | category | flops | bytes accessed | tf_op | source)
XLA Modules:
  0.0 103.6 jit_solution(17622080035690055582)
XLA Ops:
  0.6 0.0 copy-start
  0.6 1.4 %shard_map.122 = (bf16[16,12,512]{2,1,0:T(8,128)(2,1)S(1)}, bf16[2,2,8,16,512]{4,3,2,1,0:T(8,128)(2,1)S(1)}, bf16[896,96]{1,0:T(8,128)(2,1)S(1)}, bf16[256,48]{1...) custom-call(bf16[2,2,8,16,512]{4,3,2,1,0:T(8,128)(2,1)} %measured.1,, ...), custom_call_target="tpu_custom_call" | custom-call | tf_op jit(solution)/shard_map/pallas_call | solution.py:515
  2.0 3.3 %collective-permute-start = (bf16[16,12,512]{2,1,0:T(8,128)(2,1)S(1)}, bf16[16,12,512]{2,1,0:T(8,128)(2,1)S(1)}, u32[]{:S(2)}, u32[]{:S(2)}) collective-permute-start(bf16[16,12,512]{2,1,0:T(8,128)(2,1)S(1)} %get-tuple-element.22), channel_id=1, source_target_pairs={{1,0},{2,1},{3,2},{4,3},{5,4},{6,5},{7,6},{8,7},{9,8},{10,9},{11,1... | collective-permute-start | bytes 589832 | tf_op jit(solution)/shard_map/ppermute | solution.py:546
  5.3 0.0 copy-done
  5.3 7.3 %shard_map.123 = (f32[16,8,512]{2,1,0:T(8,128)S(1)}, f32[16,32,512]{2,1,0:T(8,128)S(1)}) custom-call(bf16[2,2,8,16,512]{4,3,2,1,0:T(8,128)(2,1)S(1)} %get-tuple-element.16.measured, f32[8,16,1]{2,1,0:T(8,128)S(1)} %get-tuple-element.17.keep, bf16[896,96]{1,0:T(8,128)(2,1)S(1)} %get-tuple-element.18.w1, bf16[96,896]{1,0:T(8,128)(2,1)S(1)} %get-tuple-element.19.w2, ...), custom_call_target="tpu_custom_call" | custom-call | tf_op jit(solution)/shard_map/pallas_call | solution.py:489
  12.6 0.0 collective-permute-done.halo
  12.6 3.4 %shard_map.124 = bf16[32,2,16,256]{3,2,1,0:T(8,128)(2,1)S(1)} custom-call(f32[16,8,512]{2,1,0:T(8,128)S(1)} %get-tuple-element.20.tail, f32[16,32,512]{2,1,0:T(8,128)S(1)} %get-tuple-element.21.total, bf16[16,12,512]{2,1,0:T(8,128)(2,1)S(1)} %collective-permute-done.halo, f32[8,8,1]{2,1,0:T(8,128)S(1)} %get-tuple-element.23.follow, ...), custom_call_target="tpu_custom_call" | custom-call | tf_op jit(solution)/shard_map/pallas_call | solution.py:489
  15.9 0.0 copy-start.1
  15.9 25.1 %all_to_all.20.received = bf16[32,2,16,256]{3,2,1,0:T(8,128)(2,1)S(1)} all-to-all(bf16[32,2,16,256]{3,2,1,0:T(8,128)(2,1)S(1)} %shard_map.124), channel_id=1, replica_groups=mesh['half'=2,'ring'=4,'space'=32] {'space'}, dimensions={0} | all-to-all | bytes 1048576 | tf_op jit(solution)/shard_map/all_to_all | solution.py:500
  41.1 0.0 copy-done.1
  41.1 1.5 %shard_map.125 = bf16[4,64,512]{2,1,0:T(8,128)(2,1)S(1)} custom-call(bf16[32,2,16,256]{3,2,1,0:T(8,128)(2,1)S(1)} %all_to_all.20.received, bf16[2,2,8,16,512]{4,3,2,1,0:T(8,128)(2,1)S(1)} %copy-done.1, bf16[16,12,512]{2,1,0:T(8,128)(2,1)S(1)} %collective-permute-done.halo, bf16[2,512,512]{2,1,0:T(8,128)(2,1)S(1)} %copy-done), custom_call_target="tpu_custom_call" | custom-call | tf_op jit(solution)/shard_map/pallas_call | solution.py:489
  42.6 10.4 %all_to_all.21 = bf16[4,64,512]{2,1,0:T(8,128)(2,1)S(1)} all-to-all(bf16[4,64,512]{2,1,0:T(8,128)(2,1)S(1)} %shard_map.125), channel_id=1, replica_groups=mesh['half'=2,'ring'=4,'space'=32] {'ring'}, dimensions={0} | all-to-all | bytes 524288 | tf_op jit(solution)/shard_map/all_to_all | solution.py:500
  53.0 0.0 copy-start.5
  53.1 0.0 copy-start.4
  53.1 0.0 copy-start.6
  53.1 0.0 copy-start.7
  53.1 4.3 %collective-permute-start.1 = (bf16[64,512]{1,0:T(8,128)(2,1)S(1)}, bf16[64,512]{1,0:T(8,128)(2,1)S(1)}, u32[]{:S(2)}, u32[]{:S(2)}) collective-permute-start(bf16[64,512]{1,0:T(8,128)(2,1)S(1)} %reduce_sum.12), channel_id=1, source_target_pairs={{0,128},{32,160},{64,192},{96,224},{97,225},{1,129},{33,161},{65,1... | collective-permute-start | bytes 196616 | tf_op jit(solution)/shard_map/ppermute | solution.py:586
  57.4 2.8 %collective-permute-done.1 = bf16[64,512]{1,0:T(8,128)(2,1)S(1)} collective-permute-done((bf16[64,512]{1,0:T(8,128)(2,1)S(1)}, bf16[64,512]{1,0:T(8,128)(2,1)S(1)}, u32[]{:S(2)}, u32[]{:S(2)}) %collective-permute-start.1) | collective-permute-done | bytes 65568 | tf_op jit(solution)/shard_map/ppermute | solution.py:586
  60.2 0.4 collective-permute-start.2
  60.6 0.0 copy-done.5
  60.6 0.0 copy-done.4
  60.6 0.0 copy-done.6
  60.6 0.0 copy-done.7
  60.6 0.3 shard_map.126
  60.9 0.0 copy-start.2
  60.9 1.1 %shard_map.127.early = f32[192,512]{1,0:T(8,128)S(1)} custom-call(bf16[64,512]{1,0:T(8,128)(2,1)S(1)} %add_convert_fusion.own, bf16[384,144]{1,0:T(8,128)(2,1)S(1)} %get-tuple-element.26.w1, bf16[72,384]{1,0:T(8,128)(2,1)S(1)} %get-tuple-element.27.w2), custom_call_target="tpu_custom_call" | custom-call | tf_op jit(solution)/shard_map/pallas_call | solution.py:489
  62.1 2.6 %collective-permute-done.2.previous = bf16[64,512]{1,0:T(8,128)(2,1)S(1)} collective-permute-done((bf16[64,512]{1,0:T(8,128)(2,1)S(1)}, bf16[64,512]{1,0:T(8,128)(2,1)S(1)}, u32[]{:S(2)}, u32[]{:S(2)}) %collective-permute-start.2) | collective-permute-done | bytes 65568 | tf_op jit(solution)/shard_map/ppermute | solution.py:588
  64.6 1.6 %shard_map.128 = bf16[4,64,512]{2,1,0:T(8,128)(2,1)S(1)} custom-call(bf16[64,512]{1,0:T(8,128)(2,1)S(1)} %collective-permute-done.2.previous, bf16[64,512]{1,0:T(8,128)(2,1)S(1)} %add_convert_fusion.own, bf16[384,144]{1,0:T(8,128)(2,1)S(1)} %get-tuple-element.26.w1, bf16[72,384]{1,0:T(8,128)(2,1)S(1)} %get-tuple-element.27.w2, f32[192,512]{1,0:T(8,128)S(1)} %shard_map.127.early), custom_call_target="tpu_custom_call" | custom-call | tf_op jit(solution)/shard_map/pallas_call | solution.py:489
  66.2 7.9 %all_to_all.22.gathered = bf16[4,64,512]{2,1,0:T(8,128)(2,1)S(1)} all-to-all(bf16[4,64,512]{2,1,0:T(8,128)(2,1)S(1)} %shard_map.128), channel_id=1, replica_groups=mesh['half'=2,'ring'=4,'space'=32] {'ring'}, dimensions={0} | all-to-all | bytes 524288 | tf_op jit(solution)/shard_map/all_to_all | solution.py:500
  74.1 0.0 copy-done.2
  74.1 0.9 shard_map.129
  75.1 0.0 copy-start.3
  75.1 26.5 %all_to_all.23.received = bf16[32,2,16,256]{3,2,1,0:T(8,128)(2,1)S(1)} all-to-all(bf16[32,2,16,256]{3,2,1,0:T(8,128)(2,1)S(1)} %get-tuple-element.28), channel_id=1, replica_groups=mesh['half'=2,'ring'=4,'space'=32] {'space'}, dimensions={0} | all-to-all | bytes 1048576 | tf_op jit(solution)/shard_map/all_to_all | solution.py:500
  101.6 0.0 copy-done.3
  101.6 2.0 %shard_map.130 = (bf16[2,2,8,16,512]{4,3,2,1,0:T(8,128)(2,1)}, bf16[2,8,16,512]{3,2,1,0:T(8,128)(2,1)}) custom-call(bf16[32,2,16,256]{3,2,1,0:T(8,128)(2,1)S(1)} %all_to_all.23.received, bf16[2,2,8,16,512]{4,3,2,1,0:T(8,128)(2,1)S(1)} %copy-done.3, f32[8,16,1]{2,1,0:T(8,128)S(1)} %get-tuple-element.17.keep, bf16[2,512,512]{2,1,0:T(8,128)(2,1)S(1)} %copy-done.2, ...), custom_call_target="tpu_custom_call" | custom-call | tf_op jit(solution)/shard_map/pallas_call | solution.py:613
  (2 shorter events, 0.1 us)
Async XLA Ops:
  0.6 4.7 %copy-start = (bf16[2,512,512]{2,1,0:T(8,128)(2,1)S(1)}, bf16[2,512,512]{2,1,0:T(8,128)(2,1)}, u32[]{:S(2)}) copy-start(bf16[2,512,512]{2,1,0:T(8,128)(2,1)} %constant.12.clone.table) | copy-start | bytes 3145732
  2.0 10.5 %collective-permute-start = (bf16[16,12,512]{2,1,0:T(8,128)(2,1)S(1)}, bf16[16,12,512]{2,1,0:T(8,128)(2,1)S(1)}, u32[]{:S(2)}, u32[]{:S(2)}) collective-permute-start(bf16[16,12,512]{2,1,0:T(8,128)(2,1)S(1)} %get-tuple-element.22), channel_id=1, source_target_pairs={{1,0},{2,1},{3,2},{4,3},{5,4},{6,5},{7,6},{8,7},{9,8},{10,9},{11,1... | collective-permute-start | bytes 589832 | tf_op jit(solution)/shard_map/ppermute | solution.py:546
  15.9 25.1 %copy-start.1 = (bf16[2,2,8,16,512]{4,3,2,1,0:T(8,128)(2,1)S(1)}, bf16[2,2,8,16,512]{4,3,2,1,0:T(8,128)(2,1)}, u32[]{:S(2)}) copy-start(bf16[2,2,8,16,512]{4,3,2,1,0:T(8,128)(2,1)} %sens.3) | copy-start | bytes 1572868
  53.0 7.6 %copy-start.5 = (bf16[3,72,108]{2,1,0:T(8,128)(2,1)S(1)}, bf16[3,72,108]{2,1,0:T(8,128)(2,1)}, u32[]{:S(2)}) copy-start(bf16[3,72,108]{2,1,0:T(8,128)(2,1)} %constant.14.clone.band2) | copy-start | bytes 139972
  53.1 7.5 %copy-start.4 = (bf16[6,54,144]{2,1,0:T(8,128)(2,1)S(1)}, bf16[6,54,144]{2,1,0:T(8,128)(2,1)}, u32[]{:S(2)}) copy-start(bf16[6,54,144]{2,1,0:T(8,128)(2,1)} %constant.13.clone.band1) | copy-start | bytes 279940
  53.1 7.5 %copy-start.6 = (bf16[64,2,3,3,3]{0,1,4,3,2:T(2,128)(2,1)S(1)}, bf16[64,2,3,3,3]{0,1,4,3,2:T(2,128)(2,1)}, u32[]{:S(2)}) copy-start(bf16[64,2,3,3,3]{0,1,4,3,2:T(2,128)(2,1)} %param.16) | copy-start | bytes 20740
  53.1 7.5 %copy-start.7 = (bf16[2,64,3,3,3]{1,0,4,3,2:T(2,128)(2,1)S(1)}, bf16[2,64,3,3,3]{1,0,4,3,2:T(2,128)(2,1)}, u32[]{:S(2)}) copy-start(bf16[2,64,3,3,3]{1,0,4,3,2:T(2,128)(2,1)} %param.17) | copy-start | bytes 20740
  53.1 7.1 %collective-permute-start.1 = (bf16[64,512]{1,0:T(8,128)(2,1)S(1)}, bf16[64,512]{1,0:T(8,128)(2,1)S(1)}, u32[]{:S(2)}, u32[]{:S(2)}) collective-permute-start(bf16[64,512]{1,0:T(8,128)(2,1)S(1)} %reduce_sum.12), channel_id=1, source_target_pairs={{0,128},{32,160},{64,192},{96,224},{97,225},{1,129},{33,161},{65,1... | collective-permute-start | bytes 196616 | tf_op jit(solution)/shard_map/ppermute | solution.py:586
  60.2 4.4 %collective-permute-start.2 = (bf16[64,512]{1,0:T(8,128)(2,1)S(1)}, bf16[64,512]{1,0:T(8,128)(2,1)S(1)}, u32[]{:S(2)}, u32[]{:S(2)}) collective-permute-start(bf16[64,512]{1,0:T(8,128)(2,1)S(1)} %add_convert_fusion.own), channel_id=1, source_target_pairs={{0,32},{32,64},{64,96},{96,97},{97,1},{1,33},{33,65},{65,66},{66,9... | collective-permute-start | bytes 196616 | tf_op jit(solution)/shard_map/ppermute | solution.py:588
  60.9 13.2 %copy-start.2 = (bf16[2,512,512]{2,1,0:T(8,128)(2,1)S(1)}, bf16[2,512,512]{2,1,0:T(8,128)(2,1)}, u32[]{:S(2)}) copy-start(bf16[2,512,512]{2,1,0:T(8,128)(2,1)} %constant.11.clone.table) | copy-start | bytes 3145732
  75.1 26.5 %copy-start.3 = (bf16[2,2,8,16,512]{4,3,2,1,0:T(8,128)(2,1)S(1)}, bf16[2,2,8,16,512]{4,3,2,1,0:T(8,128)(2,1)}, u32[]{:S(2)}) copy-start(bf16[2,2,8,16,512]{4,3,2,1,0:T(8,128)(2,1)} %measured.1) | copy-start | bytes 1572868
